TPU v7x, 32 devices: a whole 2x2x4 slice. The times are simulated.
32 devices in a mesh: traj: 2 (over x), dom: 16 (over z, y, core).
Axes of the slice: x: 2, y: 2, z: 4, core: 2. Of those that a mesh axis runs over, the one named last changes fastest.
Arguments:
- node_lat: bfloat16 [2, 4096, 512], P('traj', 'dom'), may hold values from -6 to 6
- edge_lat: bfloat16 [2, 8192, 512], P('traj', 'dom'), may hold values from -6 to 6
- grad_edge: bfloat16 [2, 8192, 512], P('traj', 'dom'), may hold values from -6 to 6
- grad_agg: bfloat16 [2, 4096, 512], P('traj', 'dom'), may hold values from -6 to 6
- weight_edge: bfloat16 [512, 512], replicated, may hold values from -0.15625 to 0.15625
- weight_send: bfloat16 [512, 512], replicated, may hold values from -0.15625 to 0.15625
- weight_recv: bfloat16 [512, 512], replicated, may hold values from -0.15625 to 0.15625
- weight_out: bfloat16 [512, 512], replicated, may hold values from -0.25 to 0.25
- edge_src: int32 [8192], P('dom'), may hold values from 0 to 767
- edge_recv_block: int32 [64], P('dom'), may hold values from 0 to 1
- edge_recv_node: int32 [8192], P('dom'), may hold values from 0 to 127
- send_blocks: int32 [64], P('dom'), may hold values from 0 to 1
Outputs:
- agg: bfloat16 [2, 4096, 512], P('traj', 'dom')
- grad_edge_lat: bfloat16 [2, 8192, 512], P('traj', 'dom')
- grad_node_lat: bfloat16 [2, 4096, 512], P('traj', 'dom')
- weight_grads: float32 [4, 512, 512], P(None, 'dom')
Inputs may be any that keep to these rules, and one draw needn't show every extreme that they name: edge_src // 128 is a slot below 6.
All inputs are finite; a program needn't handle non-finite values.
Results may differ from a plain program's by a relative error of at most 0.012.
Values may be sent and summed in bfloat16 or wider, within the bound.
No kernel may reach another device: no remote copies, remote signals or barrier semaphores. Data moves between devices by JAX's collectives and lax.ppermute only.
A program may use at most 64 MiB of HBM per device.

v0:
```python
import jax
import jax.numpy as jnp
from jax import lax
from jax.sharding import PartitionSpec as P

ROUNDS = 4


def partner(shard, axis, stride):
    return lax.ppermute(shard, axis, [(i, i ^ 1 << stride) for i in range(lax.axis_size(axis))])


def dot_rows(former, latter):
    return lax.dot_general(
        former, latter, (((0,), (0,)), ((), ())), preferred_element_type=jnp.float32
    )


def dot_cols(former, latter):
    return lax.dot_general(
        former, latter, (((1,), (1,)), ((), ())), preferred_element_type=jnp.float32
    )


def dot_cols_exact(former, latter):
    return lax.dot_general(
        former,
        latter.astype(jnp.float32),
        (((1,), (1,)), ((), ())),
        precision=lax.Precision.HIGHEST,
        preferred_element_type=jnp.float32,
    )


def silu_grad(preact):
    sigmoid_val = jax.nn.sigmoid(preact)
    return sigmoid_val * (1.0 + preact * (1.0 - sigmoid_val))


def per_device(
    node_lat,
    edge_lat,
    grad_edge,
    grad_agg,
    weight_edge,
    weight_send,
    weight_recv,
    weight_out,
    edge_src,
    edge_recv_block,
    edge_recv_node,
    send_blocks,
):
    features = node_lat.shape[2]
    node_rows = node_lat[0]
    node_count = node_rows.shape[0]
    block_count = node_count // 128
    edge_rows = edge_lat[0]
    edge_count = edge_rows.shape[0]
    node_blocks = node_rows.reshape(block_count, 128, features)
    block_pick = (send_blocks[:, None] == jnp.arange(block_count, dtype=jnp.int32)[None, :]).astype(
        jnp.bfloat16
    )
    outgoing = jnp.einsum(
        "rb,bnd->rnd", block_pick, node_blocks, preferred_element_type=jnp.float32
    ).astype(jnp.bfloat16)
    received = []
    for section in range(ROUNDS):
        received.append(partner(outgoing[section], "dom", section))
    node_table = jnp.concatenate([node_rows] + received, axis=0)
    slot_count = node_table.shape[0]
    receiver = (
        jnp.repeat(edge_recv_block, 128, total_repeat_length=edge_count) * 128 + edge_recv_node
    )
    onehot_src = (edge_src[:, None] == jnp.arange(slot_count, dtype=jnp.int32)[None, :]).astype(
        jnp.bfloat16
    )
    onehot_recv = (receiver[:, None] == jnp.arange(node_count, dtype=jnp.int32)[None, :]).astype(
        jnp.bfloat16
    )
    send_rows = jnp.dot(onehot_src, node_table, preferred_element_type=jnp.float32).astype(
        jnp.bfloat16
    )
    recv_rows = jnp.dot(onehot_recv, node_rows, preferred_element_type=jnp.float32).astype(
        jnp.bfloat16
    )
    preact = jnp.dot(edge_rows, weight_edge, preferred_element_type=jnp.float32)
    preact = preact + jnp.dot(send_rows, weight_send, preferred_element_type=jnp.float32)
    preact = preact + jnp.dot(recv_rows, weight_recv, preferred_element_type=jnp.float32)
    hidden = jax.nn.silu(preact).astype(jnp.bfloat16)
    projected = jnp.dot(hidden, weight_out, preferred_element_type=jnp.float32)
    centered = projected - jnp.mean(projected, axis=1, keepdims=True)
    inv_std = lax.rsqrt(jnp.mean(centered * centered, axis=1, keepdims=True) + 1e-05)
    normed = centered * inv_std
    message = normed.astype(jnp.bfloat16)
    agg = dot_rows(onehot_recv, message)
    grad_msg = grad_edge[0].astype(jnp.float32) + jnp.dot(
        onehot_recv, grad_agg[0], preferred_element_type=jnp.float32
    )
    grad_proj = inv_std * (
        grad_msg
        - jnp.mean(grad_msg, axis=1, keepdims=True)
        - normed * jnp.mean(grad_msg * normed, axis=1, keepdims=True)
    )
    grad_proj = grad_proj.astype(jnp.bfloat16)
    grad_preact = (dot_cols(grad_proj, weight_out) * silu_grad(preact)).astype(jnp.bfloat16)
    partial_grads = jnp.stack(
        [
            dot_rows(edge_rows, grad_preact),
            dot_rows(send_rows, grad_preact),
            dot_rows(recv_rows, grad_preact),
            dot_rows(hidden, grad_proj),
        ]
    )
    grad_edges = grad_edge[0].astype(jnp.float32) + dot_cols(grad_preact, weight_edge)
    slot_sums = dot_rows(onehot_src, grad_preact)
    recv_sums = dot_rows(onehot_recv, grad_preact)
    slot_grads = dot_cols_exact(slot_sums, weight_send)
    local_grads = slot_grads[:node_count] + dot_cols_exact(recv_sums, weight_recv)
    local_blocks = local_grads.reshape(block_count, 128, features)
    borrowed = slot_grads[node_count:].reshape(ROUNDS, 128, features)
    returned_list = []
    for section in range(ROUNDS):
        returned_list.append(
            partner(borrowed[section].astype(jnp.bfloat16), "dom", section).astype(jnp.float32)
        )
    returned = jnp.stack(returned_list)
    local_blocks = local_blocks + jnp.einsum(
        "rb,rnd->bnd",
        block_pick.astype(jnp.float32),
        returned,
        precision=lax.Precision.HIGHEST,
        preferred_element_type=jnp.float32,
    )
    grad_nodes = local_blocks.reshape(node_count, features)
    shares = lax.psum_scatter(partial_grads, "dom", scatter_dimension=1, tiled=True)
    weight_grads = lax.psum(shares.astype(jnp.bfloat16), "traj").astype(jnp.float32)
    return (
        agg.astype(jnp.bfloat16)[None],
        grad_edges.astype(jnp.bfloat16)[None],
        grad_nodes.astype(jnp.bfloat16)[None],
        weight_grads,
    )


def solution(mesh):
    in_specs = (
        P("traj", "dom", None),
        P("traj", "dom", None),
        P("traj", "dom", None),
        P("traj", "dom", None),
        P(),
        P(),
        P(),
        P(),
        P("dom"),
        P("dom"),
        P("dom"),
        P("dom"),
    )
    out_specs = (
        P("traj", "dom", None),
        P("traj", "dom", None),
        P("traj", "dom", None),
        P(None, "dom", None),
    )
    return jax.shard_map(
        per_device, mesh=mesh, in_specs=in_specs, out_specs=out_specs, check_vma=False
    )
```

profile of v0, /device:TPU:0, one launch (start us, length us, event | category | flops | bytes accessed | tf_op | source)
XLA Modules:
  0.0 190.6 jit_solution(1319252073367854496)
XLA Ops:
  7.2 1.5 convolution_convert_fusion
  10.8 2.6 %collective-permute-start.1 = (bf16[128,512]{1,0:T(8,128)(2,1)S(1)}, bf16[128,512]{1,0:T(8,128)(2,1)}, u32[]{:S(2)}, u32[]{:S(2)}) collective-permute-start(bf16[128,512]{1,0:T(8,128)(2,1)S(1)} %bitcast.100), channel_id=1, source_target_pairs={{0,2},{1,3},{2,0},{3,1},{4,6},{5,7},{6,4},{7,5},{8,10},{9,11},{10,... | collective-permute-start | bytes 393224 | tf_op jit(solution)/shard_map/ppermute | solution.py:10
  13.4 1.6 collective-permute-start.2
  15.0 2.7 %collective-permute-start.3 = (bf16[128,512]{1,0:T(8,128)(2,1)S(1)}, bf16[128,512]{1,0:T(8,128)(2,1)}, u32[]{:S(2)}, u32[]{:S(2)}) collective-permute-start(bf16[128,512]{1,0:T(8,128)(2,1)S(1)} %bitcast.99), channel_id=1, source_target_pairs={{0,8},{1,9},{2,10},{3,11},{4,12},{5,13},{6,14},{7,15},{8,0},{9,1},... | collective-permute-start | bytes 393224 | tf_op jit(solution)/shard_map/ppermute | solution.py:10
  18.3 2.5 %compare_select_fusion.1 = s32[512,1]{0,1:T(1,128)S(1)} fusion(s32[512,1]{0,1:T(1,128)S(1)} %bitcast.103, s32[512,1]{0,1:T(1,128)S(1)} %bitcast.104, s32[]{:T(128)} %bitcast.4, s32[]{:T(128)} %bitcast.5, s32[]{:T(128)} %bitcast.7, s32[]{:T(128)} %bitcast.6), kind=kLoop, calls=%fused_computation.62 | loop fusion | flops 4096 | bytes 6160 | tf_op jit(solution)/shard_map/jit(_take)/gather | solution.py:73
  24.9 1.6 constant_dynamic-update-slice_fusion.3
  26.5 1.6 constant_dynamic-update-slice_fusion.2
  28.0 1.6 constant_dynamic-update-slice_fusion.1
  29.6 1.6 constant_dynamic-update-slice_fusion
  31.2 1.7 fusion.3
  37.5 1.3 fusion.5
  39.2 1.9 fusion
  41.1 1.6 convolution_bitcast_fusion
  42.6 1.5 convolution_bitcast_fusion.1
  45.1 1.4 convolution_bitcast_fusion.3
  46.6 2.0 %copy.58 = bf16[1,512,512]{2,1,0:T(8,128)(2,1)} copy(bf16[1,512,512]{1,2,0:T(8,128)(2,1)} %fusion.5) | data formatting | bytes 1048576
  48.6 4.2 %fusion.41 = (bf16[768,512]{1,0:T(8,128)(2,1)S(1)}, f32[768,512]{1,0:T(8,128)}) fusion(f32[768,512]{1,0:T(8,128)} %fusion, bf16[512,512]{1,0:T(8,128)(2,1)S(1)} %copy-done), kind=kOutput, calls=%fused_computation.85 | convolution fusion | flops 2416312320 | bytes 4456448 | tf_op jit(solution)/shard_map/dot_general | solution.py:26
  54.6 2.4 %pad_maximum_fusion = f32[4,512,512]{1,2,0:T(8,128)} fusion(f32[1,512,512]{1,2,0:T(8,128)S(1)} %copy-done.9, f32[1,512,512]{1,2,0:T(8,128)S(1)} %copy-done.1, f32[1,512,512]{1,2,0:T(8,128)S(1)} %convolution_bitcast_fusion.2, f32[1,512,512]{1,2,0:T(8,128)S(1)} %copy-done.2), kind=kLoop, calls=%fused_computation | loop fusion | flops 3145728 | bytes 8388608 | tf_op jit(solution)/shard_map/stack | solution.py:107
  57.0 5.5 %copy.57 = f32[4,512,512]{2,0,1:T(4,128)} copy(f32[4,512,512]{1,2,0:T(8,128)} %pad_maximum_fusion) | data formatting | bytes 8388608 | tf_op jit(solution)/shard_map/stack | solution.py:107
  62.5 96.2 %all-reduce.5 = bf16[4,512,512]{2,0,1:T(4,128)(2,1)} all-reduce(f32[4,512,512]{2,0,1:T(4,128)} %copy.57), channel_id=2, replica_groups=mesh['traj'=2,'dom'=16] {'dom'}, use_global_device_ids=true, to_apply=%region_4.5.clone | all-reduce | flops 1048576 | bytes 6291456
  158.6 1.6 dynamic-slice_convert_fusion
  160.3 1.6 convolution_add_fusion.4
  165.6 16.6 %all-reduce.4.cloned.1.call-done = bf16[4,32,512]{2,0,1:T(4,128)(2,1)} async-done(((bf16[4,32,512]{2,0,1:T(4,128)(2,1)}), bf16[4,32,512]{2,0,1:T(4,128)(2,1)}) %all-reduce.4.cloned.1.call-update) | async-done | bytes 131088 | tf_op jit(solution)/shard_map/psum | solution.py:137
  182.1 1.6 copy.59
  (80 shorter events, 17.3 us)
Async XLA Ops:
  7.2 25.8 %copy-start = (bf16[512,512]{1,0:T(8,128)(2,1)S(1)}, bf16[512,512]{1,0:T(8,128)(2,1)}, u32[]{:S(2)}) copy-start(bf16[512,512]{1,0:T(8,128)(2,1)} %param.19) | copy-start | bytes 1572868
  7.2 175.0 %all-reduce.4.cloned.1.call-start = ((), (), s32[]{:S(2)}) async-start(), calls=%async_computation | async-start | bytes 262144 | tf_op jit(solution)/shard_map/psum | solution.py:137
  8.8 8.9 %copy-start.11 = (s32[4]{0:T(128)S(1)}, s32[4]{0:T(128)}, u32[]{:S(2)}) copy-start(s32[4]{0:T(128)} %param.23) | copy-start | bytes 52
  8.8 12.0 %copy-start.12 = (s32[512]{0:T(512)S(1)}, s32[512]{0:T(512)}, u32[]{:S(2)}) copy-start(s32[512]{0:T(512)} %param.24) | copy-start | bytes 6148
  8.8 12.0 %copy-start.8 = (bf16[1,256,512]{2,1,0:T(8,128)(2,1)S(1)}, bf16[1,256,512]{2,1,0:T(8,128)(2,1)}, u32[]{:S(2)}) copy-start(bf16[1,256,512]{2,1,0:T(8,128)(2,1)} %param.14) | copy-start | bytes 786436
  9.6 11.6 %copy-start.3 = (bf16[512,512]{1,0:T(8,128)(2,1)S(1)}, bf16[512,512]{1,0:T(8,128)(2,1)}, u32[]{:S(2)}) copy-start(bf16[512,512]{1,0:T(8,128)(2,1)} %param.18) | copy-start | bytes 1572868
  9.6 11.6 %copy-start.4 = (bf16[1,512,512]{2,1,0:T(8,128)(2,1)S(1)}, bf16[1,512,512]{2,1,0:T(8,128)(2,1)}, u32[]{:S(2)}) copy-start(bf16[1,512,512]{2,1,0:T(8,128)(2,1)} %param.15) | copy-start | bytes 1572868
  10.3 14.6 %collective-permute-start = (bf16[128,512]{1,0:T(8,128)(2,1)}, bf16[128,512]{1,0:T(8,128)(2,1)}, u32[]{:S(2)}, u32[]{:S(2)}) collective-permute-start(bf16[128,512]{1,0:T(8,128)(2,1)} %bitcast.94), channel_id=1, source_target_pairs={{0,1},{1,0},{2,3},{3,2},{4,5},{5,4},{6,7},{7,6},{8,9},{9,8},{10,11... | collective-permute-start | bytes 393224 | tf_op jit(solution)/shard_map/ppermute | solution.py:10
  10.8 15.7 %collective-permute-start.1 = (bf16[128,512]{1,0:T(8,128)(2,1)S(1)}, bf16[128,512]{1,0:T(8,128)(2,1)}, u32[]{:S(2)}, u32[]{:S(2)}) collective-permute-start(bf16[128,512]{1,0:T(8,128)(2,1)S(1)} %bitcast.100), channel_id=1, source_target_pairs={{0,2},{1,3},{2,0},{3,1},{4,6},{5,7},{6,4},{7,5},{8,10},{9,11},{10,... | collective-permute-start | bytes 393224 | tf_op jit(solution)/shard_map/ppermute | solution.py:10
  13.4 14.7 %collective-permute-start.2 = (bf16[128,512]{1,0:T(8,128)(2,1)S(1)}, bf16[128,512]{1,0:T(8,128)(2,1)}, u32[]{:S(2)}, u32[]{:S(2)}) collective-permute-start(bf16[128,512]{1,0:T(8,128)(2,1)S(1)} %bitcast.98), channel_id=1, source_target_pairs={{0,4},{1,5},{2,6},{3,7},{4,0},{5,1},{6,2},{7,3},{8,12},{9,13},{10,... | collective-permute-start | bytes 393224 | tf_op jit(solution)/shard_map/ppermute | solution.py:10
  15.0 14.6 %collective-permute-start.3 = (bf16[128,512]{1,0:T(8,128)(2,1)S(1)}, bf16[128,512]{1,0:T(8,128)(2,1)}, u32[]{:S(2)}, u32[]{:S(2)}) collective-permute-start(bf16[128,512]{1,0:T(8,128)(2,1)S(1)} %bitcast.99), channel_id=1, source_target_pairs={{0,8},{1,9},{2,10},{3,11},{4,12},{5,13},{6,14},{7,15},{8,0},{9,1},... | collective-permute-start | bytes 393224 | tf_op jit(solution)/shard_map/ppermute | solution.py:10
  21.2 2.4 %copy-start.16 = (u32[32]{0:T(128)S(1)}, u32[32]{0:T(128)}, u32[]{:S(2)}) copy-start(u32[32]{0:T(128)} %constant.107) | copy-start | bytes 388
  21.7 9.5 %copy-start.15 = (s32[512]{0:T(512)S(1)}, s32[512]{0:T(512)}, u32[]{:S(2)}) copy-start(s32[512]{0:T(512)} %param.22) | copy-start | bytes 6148
  32.9 1.0 copy-start.6
  34.0 1.0 copy-start.14
  48.6 5.9 %copy-start.2 = (f32[1,512,512]{1,2,0:T(8,128)S(1)}, f32[1,512,512]{1,2,0:T(8,128)}, u32[]{:S(2)}) copy-start(f32[1,512,512]{1,2,0:T(8,128)} %convolution_bitcast_fusion.3) | copy-start | bytes 3145732
  48.6 5.9 %copy-start.9 = (f32[1,512,512]{1,2,0:T(8,128)S(1)}, f32[1,512,512]{1,2,0:T(8,128)}, u32[]{:S(2)}) copy-start(f32[1,512,512]{1,2,0:T(8,128)} %convolution_bitcast_fusion) | copy-start | bytes 3145732
  52.8 1.7 copy-start.1
  53.5 109.6 %collective-permute-start.7 = (bf16[128,512]{1,0:T(8,128)(2,1)}, bf16[128,512]{1,0:T(8,128)(2,1)S(1)}, u32[]{:S(2)}, u32[]{:S(2)}) collective-permute-start(bf16[128,512]{1,0:T(8,128)(2,1)} %get-tuple-element.35), channel_id=1, source_target_pairs={{0,8},{1,9},{2,10},{3,11},{4,12},{5,13},{6,14},{7,15},{8,0},{9,1},... | collective-permute-start | bytes 393224 | tf_op jit(solution)/shard_map/ppermute | solution.py:10
  53.9 109.2 %collective-permute-start.6 = (bf16[128,512]{1,0:T(8,128)(2,1)}, bf16[128,512]{1,0:T(8,128)(2,1)}, u32[]{:S(2)}, u32[]{:S(2)}) collective-permute-start(bf16[128,512]{1,0:T(8,128)(2,1)} %get-tuple-element.36), channel_id=1, source_target_pairs={{0,4},{1,5},{2,6},{3,7},{4,0},{5,1},{6,2},{7,3},{8,12},{9,13},{10,... | collective-permute-start | bytes 393224 | tf_op jit(solution)/shard_map/ppermute | solution.py:10
  54.3 108.8 %collective-permute-start.5 = (bf16[128,512]{1,0:T(8,128)(2,1)S(1)}, bf16[128,512]{1,0:T(8,128)(2,1)}, u32[]{:S(2)}, u32[]{:S(2)}) collective-permute-start(bf16[128,512]{1,0:T(8,128)(2,1)S(1)} %get-tuple-element.37), channel_id=1, source_target_pairs={{0,2},{1,3},{2,0},{3,1},{4,6},{5,7},{6,4},{7,5},{8,10},{9,11},{10,... | collective-permute-start | bytes 393224 | tf_op jit(solution)/shard_map/ppermute | solution.py:10
  54.5 108.6 %collective-permute-start.4 = (bf16[128,512]{1,0:T(8,128)(2,1)S(1)}, bf16[128,512]{1,0:T(8,128)(2,1)}, u32[]{:S(2)}, u32[]{:S(2)}) collective-permute-start(bf16[128,512]{1,0:T(8,128)(2,1)S(1)} %get-tuple-element.34), channel_id=1, source_target_pairs={{0,1},{1,0},{2,3},{3,2},{4,5},{5,4},{6,7},{7,6},{8,9},{9,8},{10,11... | collective-permute-start | bytes 393224 | tf_op jit(solution)/shard_map/ppermute | solution.py:10
  62.4 97.8 %copy-start.7 = (bf16[512,512]{1,0:T(8,128)(2,1)S(1)}, bf16[512,512]{1,0:T(8,128)(2,1)}, u32[]{:S(2)}) copy-start(bf16[512,512]{1,0:T(8,128)(2,1)} %param.20) | copy-start | bytes 1572868
  161.9 2.3 %copy-start.13 = (s32[4]{0:T(128)S(1)}, s32[4]{0:T(128)}, u32[]{:S(2)}) copy-start(s32[4]{0:T(128)} %param.25) | copy-start | bytes 52
  (2 other events, 2.0 us)
Sparse Core Ops, SparseCore 0:
  160.4 21.7 all-reduce.3
where the time goes:
time: 191 us
  blocking collectives  96.2 us (50%)
  local copies, waits for them, and re-layouts  24.3 us (13%)
  matrix products  22.7 us (12%)
  waiting for transfers between devices  16.6 us (9%)
  between operations  15 us (8%)
  starting transfers between devices  8.39 us (4%)
  other arithmetic  7.33 us (4%)
    unnamed x1, blocking collectives  96.2 us
    psum x1, waiting for transfers between devices, per_device(): lax.psum(shares.astype(jnp.bfloat16), 'traj').astype(jnp.float32)  16.6 us
    unnamed x46, local copies, waits for them, and re-layouts  13.6 us
    dot_general x7, matrix products, dot_rows(): lax.dot_general(former, latter, (((0,), (0,)), ((), ())), preferred_eleme...  8.41 us
    ppermute x8, starting transfers between devices, partner(): lax.ppermute(shard, axis, [(i, i ^ 1 << stride) for i in range(lax.axis_s...  8.35 us
    dot_general x2, matrix products, dot_cols_exact(): lax.dot_general(former, latter.astype(jnp.float32), (((1,), (1,)), ((), (...  5.84 us
    another operation x1, local copies, waits for them, and re-layouts, per_device(): jnp.stack([dot_rows(edge_rows, grad_preact), dot_rows(send_rows, grad_pre...  5.47 us
  transfers between devices with their start and end apart: 9, of which 1 were waited for; matrix products, arithmetic and copies ran while one was open for 14% of the time, Pallas kernels for 0%

commit v1 on v0

v1 whole, which is shorter than its diff:
```python
import functools

import jax
import jax.numpy as jnp
from jax import lax
from jax.experimental import pallas as pl
from jax.experimental.pallas import tpu as pltpu
from jax.sharding import Mesh, PartitionSpec as P

LANES = 128
BF16 = jnp.bfloat16
F32 = jnp.float32
VMEM = pl.BlockSpec(memory_space=pltpu.VMEM)
SMEM = pl.BlockSpec(memory_space=pltpu.SMEM)


def dot(former, latter):
    return jnp.dot(former, latter, preferred_element_type=F32)


def dot_rows(former, latter):
    return lax.dot_general(former, latter, (((0,), (0,)), ((), ())), preferred_element_type=F32)


def dot_cols(former, latter):
    return lax.dot_general(former, latter, (((1,), (1,)), ((), ())), preferred_element_type=F32)


def call(body, outs, ins, name):
    return pl.pallas_call(
        body,
        out_shape=[jax.ShapeDtypeStruct(shape, kind) for shape, kind in outs],
        in_specs=ins,
        out_specs=[VMEM] * len(outs),
        name=name,
    )


def swap(array, axis):
    return lax.ppermute(array, axis, [(0, 1), (1, 0)])


def down_rows(row, count):
    return jnp.transpose(jnp.broadcast_to(row, (LANES, count)))


def onehot_cols(index_cols, first, blocks):
    lane = lax.broadcasted_iota(jnp.int32, index_cols.shape, 1)
    parts = [
        jnp.where(index_cols == lane + (first + LANES * block), 1.0, 0.0).astype(BF16)
        for block in range(blocks)
    ]
    return jnp.concatenate(parts, axis=1)


def onehot_rows(index_row, first, rows):
    node = lax.broadcasted_iota(jnp.int32, (rows, index_row.shape[1]), 0) + first
    return jnp.where(node == index_row, 1.0, 0.0).astype(BF16)


def receiver_row(recv_block, recv_node):
    edges = recv_node.shape[1]
    return jnp.concatenate(
        [
            recv_node[:, LANES * block : LANES * (block + 1)] + recv_block[block] * LANES
            for block in range(edges // LANES)
        ],
        axis=1,
    )


def pick_body(send_blocks, node_lat, *lent):
    for section, out in enumerate(lent):
        out[...] = node_lat[pl.ds(pl.multiple_of(send_blocks[section] * LANES, LANES), LANES), :]


def early_body(
    recv_block, edge_src, recv_node, node_lat, edge_lat, grad_edge, grad_agg, weight_edge,
    weight_recv, recv_out, send_out, preact_out, grad_msg_out,
):
    nodes = node_lat.shape[0]
    edges = edge_lat.shape[0]
    receiver = down_rows(receiver_row(recv_block, recv_node[...]), edges)
    sender = down_rows(edge_src[...], edges)
    hot_recv = onehot_cols(receiver, 0, nodes // LANES)
    recv_rows = dot(hot_recv, node_lat[...]).astype(BF16)
    recv_out[...] = recv_rows
    send_out[...] = dot(onehot_cols(sender, 0, nodes // LANES), node_lat[...]).astype(BF16)
    preact_out[...] = dot(edge_lat[...], weight_edge[...]) + dot(recv_rows, weight_recv[...])
    grad_msg_out[...] = grad_edge[...].astype(F32) + dot(hot_recv, grad_agg[...])


def main_body(
    rounds, parts, core, recv_block, edge_src, recv_node, recv_rows, send_own, preact_own,
    grad_msg, edge_lat, weight_send, weight_out, *refs,
):
    borrowed = refs[:rounds]
    (give_out, keep_out, grad_preact_out, message_out, own_out, recv_out) = refs[rounds : rounds + 6]
    back_out = refs[rounds + 6 : 2 * rounds + 6]
    table, sums, send_ref, hidden_ref, grad_proj_ref = refs[2 * rounds + 6 :]
    edges, features = edge_lat.shape
    nodes = own_out.shape[0]
    for section in range(rounds):
        table[LANES * section : LANES * (section + 1), :] = borrowed[section][...]
    sender = down_rows(edge_src[...], edges)
    step = edges // 2
    for start in range(0, edges, step):
        rows = slice(start, start + step)
        hot = onehot_cols(sender[rows], nodes, rounds)
        send = (send_own[rows, :].astype(F32) + dot(hot, table[...])).astype(BF16)
        send_ref[rows, :] = send
        preact = preact_own[rows, :] + dot(send, weight_send[...])
        sigmoid = jax.nn.sigmoid(preact)
        hidden = (preact * sigmoid).astype(BF16)
        hidden_ref[rows, :] = hidden
        slope = sigmoid * (1.0 + preact * (1.0 - sigmoid))
        projected = dot(hidden, weight_out[...])
        centered = projected - jnp.mean(projected, axis=1, keepdims=True)
        inv_std = lax.rsqrt(jnp.mean(centered * centered, axis=1, keepdims=True) + 1e-05)
        normed = centered * inv_std
        message_out[rows, :] = normed.astype(BF16)
        grad = grad_msg[rows, :]
        grad_proj = inv_std * (
            grad
            - jnp.mean(grad, axis=1, keepdims=True)
            - normed * jnp.mean(grad * normed, axis=1, keepdims=True)
        )
        grad_proj = grad_proj.astype(BF16)
        grad_proj_ref[rows, :] = grad_proj
        grad_preact_out[rows, :] = (dot_cols(grad_proj, weight_out[...]) * slope).astype(BF16)
    grad_preact = grad_preact_out[...]
    receiver = receiver_row(recv_block, recv_node[...])
    slot_sums = dot(onehot_rows(edge_src[...], 0, nodes + rounds * LANES), grad_preact)
    own_out[...] = slot_sums[:nodes]
    for section in range(rounds):
        first = nodes + LANES * section
        back_out[section][...] = slot_sums[first : first + LANES].astype(BF16)
    recv_out[...] = dot(onehot_rows(receiver, 0, nodes), grad_preact)
    sums[3] = dot_rows(hidden_ref[...], grad_proj_ref[...])
    sums[0] = dot_rows(edge_lat[...], grad_preact)
    sums[1] = dot_rows(send_ref[...], grad_preact)
    sums[2] = dot_rows(recv_rows[...], grad_preact)
    members, mids, tops, take = parts
    share = features // (2 * mids * tops)
    per_part = sums.shape[0] // members
    for target, flip in ((keep_out, 0), (give_out, 1)):
        side = core[0] ^ flip
        for part in range(members):
            for mid in range(mids):
                for top in range(tops):
                    first = pl.multiple_of(((top * mids + mid) * 2 + side) * share, share)
                    piece = [
                        sums[part * per_part + which, pl.ds(first, share), :]
                        for which in range(per_part)
                    ]
                    place = ((part * mids + mid) * tops + top) * take
                    target[place : place + take, :] = jnp.concatenate(piece, axis=0).astype(
                        target.dtype
                    )


def add_body(keep, got, out):
    out[...] = (keep[...] + got[...].astype(F32)).astype(BF16)


def fold_body(groups, take, top, got, keep_out, give_out):
    for target, flip in ((keep_out, 0), (give_out, 1)):
        side = top[0] ^ flip
        total = None
        for group in range(groups):
            first = pl.multiple_of((2 * group + side) * take, take)
            piece = got[pl.ds(first, take), :].astype(F32)
            total = piece if total is None else total + piece
        target[...] = total.astype(target.dtype)


def edge_body(recv_block, recv_node, grad_preact, message, grad_edge, weight_edge, agg_out, edge_out):
    receiver = receiver_row(recv_block, recv_node[...])
    agg_out[...] = dot(onehot_rows(receiver, 0, agg_out.shape[0]), message[...]).astype(BF16)
    edge_out[...] = (
        grad_edge[...].astype(F32) + dot_cols(grad_preact[...], weight_edge[...])
    ).astype(BF16)


def dot_cols_split(former, latter):
    high = former.astype(BF16)
    low = (former - high.astype(F32)).astype(BF16)
    return dot_cols(high, latter) + dot_cols(low, latter)


def node_body(send_blocks, own_sums, recv_sums, weight_send, weight_recv, *refs):
    returned, out, total = refs[:-2], refs[-2], refs[-1]
    total[...] = own_sums[...]
    for section, block in enumerate(returned):
        rows = pl.ds(pl.multiple_of(send_blocks[section] * LANES, LANES), LANES)
        total[rows, :] = total[rows, :] + block[...].astype(F32)
    out[...] = (
        dot_cols_split(total[...], weight_send[...])
        + dot_cols_split(recv_sums[...], weight_recv[...])
    ).astype(BF16)


def per_device(
    traj_axes, dom_axes, node_lat, edge_lat, grad_edge, grad_agg, weight_edge, weight_send,
    weight_recv, weight_out, edge_src, edge_recv_block, edge_recv_node, send_blocks,
):
    node_lat, edge_lat, grad_edge, grad_agg = node_lat[0], edge_lat[0], grad_edge[0], grad_agg[0]
    nodes, features = node_lat.shape
    edges = edge_lat.shape[0]
    rounds = send_blocks.shape[0]
    edge_src = edge_src.reshape(1, edges)
    recv_node = edge_recv_node.reshape(1, edges)
    bits = dom_axes[::-1]
    domains = 2 ** len(bits)
    share = 4 * features // domains
    split = traj_axes[:1] if share >= 32 else ()
    take = share >> len(split)
    mids = bits[1:-1][::-1]
    members = 2 ** len(split)
    groups = 2 ** (len(mids) + len(split))
    half = 2 * features

    lent = call(
        pick_body, [((LANES, features), BF16)] * rounds, [SMEM, VMEM], "pick"
    )(send_blocks, node_lat)
    borrowed = [None] * rounds
    for section in reversed(range(rounds)):
        borrowed[section] = swap(lent[section], bits[section])

    recv_rows, send_own, preact_own, grad_msg = call(
        early_body,
        [((edges, features), BF16)] * 2 + [((edges, features), F32)] * 2,
        [SMEM] + [VMEM] * 8,
        "early",
    )(edge_recv_block, edge_src, recv_node, node_lat, edge_lat, grad_edge, grad_agg, weight_edge, weight_recv)

    core = lax.axis_index(bits[0]).astype(jnp.int32).reshape(1)
    main = pl.pallas_call(
        functools.partial(main_body, rounds, (members, 2 ** len(mids), 2, take)),
        out_shape=[
            jax.ShapeDtypeStruct((half, features), BF16),
            jax.ShapeDtypeStruct((half, features), F32),
            jax.ShapeDtypeStruct((edges, features), BF16),
            jax.ShapeDtypeStruct((edges, features), BF16),
            jax.ShapeDtypeStruct((nodes, features), F32),
            jax.ShapeDtypeStruct((nodes, features), F32),
        ]
        + [jax.ShapeDtypeStruct((LANES, features), BF16)] * rounds,
        in_specs=[SMEM, SMEM] + [VMEM] * (9 + rounds),
        out_specs=[VMEM] * (6 + rounds),
        scratch_shapes=[
            pltpu.VMEM((rounds * LANES, features), BF16),
            pltpu.VMEM((4, features, features), F32),
            pltpu.VMEM((edges, features), BF16),
            pltpu.VMEM((edges, features), BF16),
            pltpu.VMEM((edges, features), BF16),
        ],
        name="main",
    )
    give, keep, grad_preact, message, own_sums, recv_sums, *back = main(
        core, edge_recv_block, edge_src, recv_node, recv_rows, send_own, preact_own, grad_msg,
        edge_lat, weight_send, weight_out, *borrowed,
    )

    got = swap(give, bits[0])
    returned = [None] * rounds
    for section in reversed(range(rounds)):
        returned[section] = swap(back[section], bits[section])

    chip = call(add_body, [((half, features), BF16)], [VMEM, VMEM], "chip")(keep, got)[0]
    spread = lax.all_to_all(chip, split + mids, split_axis=0, concat_axis=0, tiled=True)
    agg, grad_edges = call(
        edge_body,
        [((nodes, features), BF16), ((edges, features), BF16)],
        [SMEM] + [VMEM] * 5,
        "edge",
    )(edge_recv_block, recv_node, grad_preact, message, grad_edge, weight_edge)
    grad_nodes = pl.pallas_call(
        node_body,
        out_shape=jax.ShapeDtypeStruct((nodes, features), BF16),
        in_specs=[SMEM] + [VMEM] * (4 + rounds),
        out_specs=VMEM,
        scratch_shapes=[pltpu.VMEM((nodes, features), F32)],
        name="node",
    )(send_blocks, own_sums, recv_sums, weight_send, weight_recv, *returned)

    top = lax.axis_index(bits[-1]).astype(jnp.int32).reshape(1)
    keep_top, give_top = call(
        functools.partial(fold_body, groups, take),
        [((take, features), F32), ((take, features), BF16)],
        [SMEM, VMEM],
        "fold",
    )(top, spread)
    total = keep_top + swap(give_top, bits[-1]).astype(F32)
    for axis in traj_axes[len(split) :]:
        sent = total.astype(BF16)
        total = sent.astype(F32) + swap(sent, axis).astype(F32)
    total = total.astype(BF16)
    if split:
        other = swap(total, split[0])
        first = lax.axis_index(split[0]) == 0
        total = jnp.concatenate(
            [jnp.where(first, total, other), jnp.where(first, other, total)], axis=0
        )
    weight_grads = total.astype(F32).reshape(4, share // 4, features)
    return agg[None], grad_edges[None], grad_nodes[None], weight_grads


def solution(mesh):
    traj_axes = tuple(f"t{bit}" for bit in reversed(range(mesh.shape["traj"].bit_length() - 1)))
    dom_axes = tuple(f"d{bit}" for bit in reversed(range(mesh.shape["dom"].bit_length() - 1)))
    names = traj_axes + dom_axes
    bit_mesh = Mesh(mesh.devices.reshape((2,) * len(names)), names)
    rows = P(traj_axes, dom_axes, None)
    in_specs = (rows,) * 4 + (P(),) * 4 + (P(dom_axes),) * 4
    out_specs = (rows,) * 3 + (P(None, dom_axes, None),)
    return jax.shard_map(
        functools.partial(per_device, traj_axes, dom_axes),
        mesh=bit_mesh,
        in_specs=in_specs,
        out_specs=out_specs,
        check_vma=False,
    )
```

time: 191 us -> 72.8 us (0.38)
  blocking collectives: 96.2 us -> 0 us
  Pallas kernels: 0 us -> 26 us
  matrix products: 22.7 us -> 0 us
  local copies, waits for them, and re-layouts: 24.3 us -> 3.3 us
  between operations: 15 us -> 0.77 us
  waiting for transfers between devices: 16.6 us -> 25.8 us
  starting transfers between devices: 8.39 us -> 14.9 us
  other arithmetic: 7.33 us -> 1.68 us
    unnamed x1 -> x0, blocking collectives: 96.2 us -> none
    pallas_call x0 -> x7, Pallas kernels: none -> 26 us  [the longest x1 9.12 us: per_device(): main(core, edge_recv_block, edge_src, recv_node, recv_rows, send_own, pre...]
    dot_general x20 -> x0, matrix products: 22.7 us -> none  [the longest x7 8.41 us: dot_rows(): lax.dot_general(former, latter, (((0,), (0,)), ((), ())), preferred_eleme...]
    psum x1 -> x0, waiting for transfers between devices: 16.6 us -> none  [per_device(): lax.psum(shares.astype(jnp.bfloat16), 'traj').astype(jnp.float32)]
    all_to_all x0 -> x1, waiting for transfers between devices: none -> 16.4 us  [per_device(): lax.all_to_all(chip, split + mids, split_axis=0, concat_axis=0, tiled=True)]
    unnamed x46 -> x28, local copies, waits for them, and re-layouts: 13.6 us -> 3.3 us
    ppermute x8 -> x11, waiting for transfers between devices: 0.02 us -> 9.34 us  [swap(): return lax.ppermute(array, axis, [(0, 1), (1, 0)])]
    another operation x1 -> x0, local copies, waits for them, and re-layouts: 5.47 us -> none  [per_device(): jnp.stack([dot_rows(edge_rows, grad_preact), dot_rows(send_rows, grad_pre...]
  transfers between devices with their start and end apart: 9 -> 12, of which waited for: 1 -> 5; matrix products, arithmetic and copies ran while one was open for 14% -> 1% of each run, Pallas kernels for 0% -> 14%
where the time goes in v1:
time: 72.8 us; the launch traced here: 72.4 us
  Pallas kernels  26 us (36%)
  waiting for transfers between devices  25.8 us (35%)
  starting transfers between devices  14.9 us (20%)
  local copies, waits for them, and re-layouts  3.3 us (5%)
  other arithmetic  1.68 us (2%)
  between operations  0.77 us (1%)
    all_to_all x1, waiting for transfers between devices, per_device(): lax.all_to_all(chip, split + mids, split_axis=0, concat_axis=0, tiled=True)  16.4 us
    ppermute x11, starting transfers between devices, swap(): return lax.ppermute(array, axis, [(0, 1), (1, 0)])  11.2 us
    ppermute x11, waiting for transfers between devices, swap(): return lax.ppermute(array, axis, [(0, 1), (1, 0)])  9.34 us
    pallas_call x1, Pallas kernels, per_device(): main(core, edge_recv_block, edge_src, recv_node, recv_rows, send_own, pre...  9.12 us
    pallas_call x1, Pallas kernels, per_device(): call(early_body, [((edges, features), BF16)] * 2 + [((edges, features), F...  4.07 us
    all_to_all x1, starting transfers between devices, per_device(): lax.all_to_all(chip, split + mids, split_axis=0, concat_axis=0, tiled=True)  3.7 us
    unnamed x28, local copies, waits for them, and re-layouts  3.3 us
    pallas_call x1, Pallas kernels, per_device(): pl.pallas_call(node_body, out_shape=jax.ShapeDtypeStruct((nodes, features...  3.18 us
  transfers between devices with their start and end apart: 12, of which 5 were waited for; matrix products, arithmetic and copies ran while one was open for 1% of the time, Pallas kernels for 14%

profile of v1, /device:TPU:0, one launch (start us, length us, event | category | flops | bytes accessed | tf_op | source)
XLA Modules:
  0.0 72.4 jit_solution(2664139207409109570)
XLA Ops:
  0.6 1.8 %pick.1 = (bf16[128,512]{1,0:T(8,128)(2,1)}, bf16[128,512]{1,0:T(8,128)(2,1)}, bf16[128,512]{1,0:T(8,128)(2,1)}, bf16[128,512]{1,0:T(8,128)(2,1)}) custom-call(s32[4]{0:T(128)} %send_blocks.3, bf16[256,512]{1,0:T(8,128)(2,1)} %bitcast.21), custom_call_target="tpu_custom_call" | custom-call | tf_op jit(solution)/shard_map/pick/pallas_call | solution.py:223
  2.9 2.5 %collective-permute-start.1 = (bf16[128,512]{1,0:T(8,128)(2,1)}, bf16[128,512]{1,0:T(8,128)(2,1)S(1)}, u32[]{:S(2)}, u32[]{:S(2)}) collective-permute-start(bf16[128,512]{1,0:T(8,128)(2,1)} %get-tuple-element.31), channel_id=1, source_target_pairs={{0,2},{2,0},{1,3},{3,1},{4,6},{6,4},{5,7},{7,5},{8,10},{10,8},{9,1... | collective-permute-start | bytes 393224 | tf_op jit(solution)/shard_map/ppermute | solution.py:40
  5.4 1.6 %collective-permute-start.2 = (bf16[128,512]{1,0:T(8,128)(2,1)}, bf16[128,512]{1,0:T(8,128)(2,1)S(1)}, u32[]{:S(2)}, u32[]{:S(2)}) collective-permute-start(bf16[128,512]{1,0:T(8,128)(2,1)} %get-tuple-element.32), channel_id=1, source_target_pairs={{0,4},{4,0},{1,5},{5,1},{2,6},{6,2},{3,7},{7,3},{8,12},{12,8},{9,1... | collective-permute-start | bytes 393224 | tf_op jit(solution)/shard_map/ppermute | solution.py:40
  7.0 2.6 %collective-permute-start.3 = (bf16[128,512]{1,0:T(8,128)(2,1)}, bf16[128,512]{1,0:T(8,128)(2,1)S(1)}, u32[]{:S(2)}, u32[]{:S(2)}) collective-permute-start(bf16[128,512]{1,0:T(8,128)(2,1)} %get-tuple-element.33), channel_id=1, source_target_pairs={{0,8},{8,0},{1,9},{9,1},{2,10},{10,2},{3,11},{11,3},{4,12},{12,4},... | collective-permute-start | bytes 393224 | tf_op jit(solution)/shard_map/ppermute | solution.py:40
  9.6 4.1 %early.1 = (bf16[512,512]{1,0:T(8,128)(2,1)}, bf16[512,512]{1,0:T(8,128)(2,1)}, f32[512,512]{1,0:T(8,128)}, f32[512,512]{1,0:T(8,128)}) custom-call(s32[4]{0:T(128)} %recv_block.5, s32[1,512]{1,0:T(1,128)} %bitcast.29, s32[1,512]{1,0:T(1,128)} %bitcast.26, bf16[256,512]{1,0:T(8,128)(2,1)} %bitcast.22, bf16[512,512]{1,0:T(8,128)(2,1)} %bitcast.17, ...), custom_call_target="tpu_custom_call" | custom-call | tf_op jit(solution)/shard_map/early/pallas_call | solution.py:230
  13.7 2.6 %collective-permute-done.3.refs_3_ = bf16[128,512]{1,0:T(8,128)(2,1)S(1)} collective-permute-done((bf16[128,512]{1,0:T(8,128)(2,1)}, bf16[128,512]{1,0:T(8,128)(2,1)S(1)}, u32[]{:S(2)}, u32[]{:S(2)}) %collective-permute-start.3) | collective-permute-done | bytes 131104 | tf_op jit(solution)/shard_map/ppermute | solution.py:40
  16.3 0.6 copy-done.9
  17.0 9.1 %main.1 = (bf16[1024,512]{1,0:T(8,128)(2,1)}, f32[1024,512]{1,0:T(8,128)}, bf16[512,512]{1,0:T(8,128)(2,1)}, bf16[512,512]{1,0:T(8,128)(2,1)}, f32[256,512]{1,0:...) custom-call(s32[1]{0:T(128)} %bitcast.1.core, ...), custom_call_target="tpu_custom_call" | custom-call | tf_op jit(solution)/shard_map/main/pallas_call | solution.py:260
  26.1 2.9 %collective-permute-done.8.got = bf16[1024,512]{1,0:T(8,128)(2,1)S(1)} collective-permute-done((bf16[1024,512]{1,0:T(8,128)(2,1)}, bf16[1024,512]{1,0:T(8,128)(2,1)S(1)}, u32[]{:S(2)}, u32[]{:S(2)}) %collective-permute-start.8) | collective-permute-done | bytes 1048608 | tf_op jit(solution)/shard_map/ppermute | solution.py:40
  29.0 1.0 %copy-done.1 = bf16[1024,512]{1,0:T(8,128)(2,1)} copy-done((bf16[1024,512]{1,0:T(8,128)(2,1)}, bf16[1024,512]{1,0:T(8,128)(2,1)S(1)}, u32[]{:S(2)}) %copy-start.1) | copy-done | bytes 1048600
  30.0 3.0 %chip.1 = bf16[1024,512]{1,0:T(8,128)(2,1)} custom-call(f32[1024,512]{1,0:T(8,128)} %get-tuple-element.44.keep, bf16[1024,512]{1,0:T(8,128)(2,1)} %copy-done.1), custom_call_target="tpu_custom_call" | custom-call | tf_op jit(solution)/shard_map/chip/pallas_call | solution.py:270
  33.0 3.7 %all-to-all-start = ((bf16[8,128,512]{2,1,0:T(8,128)(2,1)}), bf16[8,128,512]{2,1,0:T(8,128)(2,1)S(1)}, u32[]{:S(2)}, u32[]{:S(2)}) async-start(bf16[8,128,512]{2,1,0:T(8,128)(2,1)} %bitcast.16), calls=%async_computation | async-start | bytes 2097152 | tf_op jit(solution)/shard_map/all_to_all | solution.py:271
  36.7 16.4 %all-to-all-done = bf16[8,128,512]{2,1,0:T(8,128)(2,1)S(1)} async-done(((bf16[8,128,512]{2,1,0:T(8,128)(2,1)}), bf16[8,128,512]{2,1,0:T(8,128)(2,1)S(1)}, u32[]{:S(2)}, u32[]{:S(2)}) %all-to-all-start) | async-done | bytes 1048608 | tf_op jit(solution)/shard_map/all_to_all | solution.py:271
  53.1 1.0 %copy-done = bf16[8,128,512]{2,1,0:T(8,128)(2,1)} copy-done((bf16[8,128,512]{2,1,0:T(8,128)(2,1)}, bf16[8,128,512]{2,1,0:T(8,128)(2,1)S(1)}, u32[]{:S(2)}) %copy-start) | copy-done | bytes 1048600
  54.1 2.0 %fold.1 = (f32[64,512]{1,0:T(8,128)}, bf16[64,512]{1,0:T(8,128)(2,1)}) custom-call(s32[1]{0:T(128)} %bitcast.10.top, bf16[1024,512]{1,0:T(8,128)(2,1)} %bitcast.15), custom_call_target="tpu_custom_call" | custom-call | tf_op jit(solution)/shard_map/fold/pallas_call | solution.py:288
  56.1 1.5 %collective-permute-start.9 = (bf16[64,512]{1,0:T(8,128)(2,1)}, bf16[64,512]{1,0:T(8,128)(2,1)S(1)}, u32[]{:S(2)}, u32[]{:S(2)}) collective-permute-start(bf16[64,512]{1,0:T(8,128)(2,1)} %get-tuple-element.47), channel_id=1, source_target_pairs={{0,8},{8,0},{1,9},{9,1},{2,10},{10,2},{3,11},{11,3},{4,12},{12,4},... | collective-permute-start | bytes 196616 | tf_op jit(solution)/shard_map/ppermute | solution.py:40
  58.2 1.7 %collective-permute-start.7 = (bf16[128,512]{1,0:T(8,128)(2,1)S(1)}, bf16[128,512]{1,0:T(8,128)(2,1)S(1)}, u32[]{:S(2)}, u32[]{:S(2)}) collective-permute-start(bf16[128,512]{1,0:T(8,128)(2,1)S(1)} %copy-done.10), channel_id=1, source_target_pairs={{0,8},{8,0},{1,9},{9,1},{2,10},{10,2},{3,11},{11,3},{4,12},{12,4},... | collective-permute-start | bytes 393224 | tf_op jit(solution)/shard_map/ppermute | solution.py:40
  59.9 2.7 %collective-permute-done.9 = bf16[64,512]{1,0:T(8,128)(2,1)S(1)} collective-permute-done((bf16[64,512]{1,0:T(8,128)(2,1)}, bf16[64,512]{1,0:T(8,128)(2,1)S(1)}, u32[]{:S(2)}, u32[]{:S(2)}) %collective-permute-start.9) | collective-permute-done | bytes 65568 | tf_op jit(solution)/shard_map/ppermute | solution.py:40
  62.6 0.9 %add_convert_fusion = bf16[64,512]{1,0:T(8,128)(2,1)S(1)} fusion(f32[64,512]{1,0:T(8,128)} %get-tuple-element.46, bf16[64,512]{1,0:T(8,128)(2,1)S(1)} %collective-permute-done.9), kind=kLoop, calls=%fused_computation.1 | loop fusion | flops 98304 | bytes 262144 | tf_op jit(solution)/shard_map/convert_element_type | solution.py:298
  63.7 2.9 %edge.1 = (bf16[256,512]{1,0:T(8,128)(2,1)}, bf16[512,512]{1,0:T(8,128)(2,1)}) custom-call(s32[4]{0:T(128)} %recv_block.5, s32[1,512]{1,0:T(1,128)} %bitcast.28, bf16[512,512]{1,0:T(8,128)(2,1)} %get-tuple-element.34.grad_preact, bf16[512,512]{1,0:T(8,128)(2,1)} %get-tuple-element.35.message, bf16[512,512]{1,0:T(8,128)(2,1)} %bitcast.20, ...), custom_call_target="tpu_custom_call" | custom-call | tf_op jit(solution)/shard_map/edge/pallas_call | solution.py:272
  66.6 1.2 %collective-permute-done.7.refs_3_ = bf16[128,512]{1,0:T(8,128)(2,1)S(1)} collective-permute-done((bf16[128,512]{1,0:T(8,128)(2,1)S(1)}, bf16[128,512]{1,0:T(8,128)(2,1)S(1)}, u32[]{:S(2)}, u32[]{:S(2)}) %collective-permute-start.7) | collective-permute-done | bytes 131104 | tf_op jit(solution)/shard_map/ppermute | solution.py:40
  67.8 0.7 copy-done.5
  68.5 3.2 %node.1 = bf16[256,512]{1,0:T(8,128)(2,1)} custom-call(s32[4]{0:T(128)} %send_blocks.3, f32[256,512]{1,0:T(8,128)} %get-tuple-element.38.own_sums, f32[256,512]{1,0:T(8,128)} %get-tuple-element.39.recv_sums, bf16[512,512]{1,0:T(8,128)(2,1)} %weight_send.3, bf16[512,512]{1,0:T(8,128)(2,1)} %weight_recv.3, bf16[128,512]{1,0:T(8,128)(2,1)} %copy-done.2, ...), custom_call_target="tpu_custom_call" | custom-call | tf_op jit(solution)/shard_map/node/pallas_call | solution.py:278
  71.7 0.7 %convert.1 = f32[4,32,512]{2,1,0:T(8,128)} convert(bf16[4,32,512]{2,1,0:T(8,128)(2,1)S(1)} %bitcast.23) | non-fusion elementwise | flops 65536 | bytes 393216 | tf_op jit(solution)/shard_map/convert_element_type | solution.py:305
  (39 shorter events, 1.4 us)
Async XLA Ops:
  2.4 11.2 %collective-permute-start = (bf16[128,512]{1,0:T(8,128)(2,1)}, bf16[128,512]{1,0:T(8,128)(2,1)S(1)}, u32[]{:S(2)}, u32[]{:S(2)}) collective-permute-start(bf16[128,512]{1,0:T(8,128)(2,1)} %get-tuple-element.30), channel_id=1, source_target_pairs={{0,1},{1,0},{2,3},{3,2},{4,5},{5,4},{6,7},{7,6},{8,9},{9,8},{10,11... | collective-permute-start | bytes 393224 | tf_op jit(solution)/shard_map/ppermute | solution.py:40
  2.9 10.8 %collective-permute-start.1 = (bf16[128,512]{1,0:T(8,128)(2,1)}, bf16[128,512]{1,0:T(8,128)(2,1)S(1)}, u32[]{:S(2)}, u32[]{:S(2)}) collective-permute-start(bf16[128,512]{1,0:T(8,128)(2,1)} %get-tuple-element.31), channel_id=1, source_target_pairs={{0,2},{2,0},{1,3},{3,1},{4,6},{6,4},{5,7},{7,5},{8,10},{10,8},{9,1... | collective-permute-start | bytes 393224 | tf_op jit(solution)/shard_map/ppermute | solution.py:40
  5.4 8.3 %collective-permute-start.2 = (bf16[128,512]{1,0:T(8,128)(2,1)}, bf16[128,512]{1,0:T(8,128)(2,1)S(1)}, u32[]{:S(2)}, u32[]{:S(2)}) collective-permute-start(bf16[128,512]{1,0:T(8,128)(2,1)} %get-tuple-element.32), channel_id=1, source_target_pairs={{0,4},{4,0},{1,5},{5,1},{2,6},{6,2},{3,7},{7,3},{8,12},{12,8},{9,1... | collective-permute-start | bytes 393224 | tf_op jit(solution)/shard_map/ppermute | solution.py:40
  7.0 9.3 %collective-permute-start.3 = (bf16[128,512]{1,0:T(8,128)(2,1)}, bf16[128,512]{1,0:T(8,128)(2,1)S(1)}, u32[]{:S(2)}, u32[]{:S(2)}) collective-permute-start(bf16[128,512]{1,0:T(8,128)(2,1)} %get-tuple-element.33), channel_id=1, source_target_pairs={{0,8},{8,0},{1,9},{9,1},{2,10},{10,2},{3,11},{11,3},{4,12},{12,4},... | collective-permute-start | bytes 393224 | tf_op jit(solution)/shard_map/ppermute | solution.py:40
  13.6 2.7 %copy-start.6 = (bf16[128,512]{1,0:T(8,128)(2,1)}, bf16[128,512]{1,0:T(8,128)(2,1)S(1)}, u32[]{:S(2)}) copy-start(bf16[128,512]{1,0:T(8,128)(2,1)S(1)} %collective-permute-done.refs_0_) | copy-start | bytes 393220
  13.7 2.6 %copy-start.7 = (bf16[128,512]{1,0:T(8,128)(2,1)}, bf16[128,512]{1,0:T(8,128)(2,1)S(1)}, u32[]{:S(2)}) copy-start(bf16[128,512]{1,0:T(8,128)(2,1)S(1)} %collective-permute-done.1.refs_1_) | copy-start | bytes 393220
  13.7 2.6 %copy-start.8 = (bf16[128,512]{1,0:T(8,128)(2,1)}, bf16[128,512]{1,0:T(8,128)(2,1)S(1)}, u32[]{:S(2)}) copy-start(bf16[128,512]{1,0:T(8,128)(2,1)S(1)} %collective-permute-done.2.refs_2_) | copy-start | bytes 393220
  26.1 2.9 %collective-permute-start.8 = (bf16[1024,512]{1,0:T(8,128)(2,1)}, bf16[1024,512]{1,0:T(8,128)(2,1)S(1)}, u32[]{:S(2)}, u32[]{:S(2)}) collective-permute-start(bf16[1024,512]{1,0:T(8,128)(2,1)} %get-tuple-element.45), channel_id=1, source_target_pairs={{0,1},{1,0},{2,3},{3,2},{4,5},{5,4},{6,7},{7,6},{8,9},{9,8},{10,11... | collective-permute-start | bytes 3145736 | tf_op jit(solution)/shard_map/ppermute | solution.py:40
  29.0 1.0 %copy-start.1 = (bf16[1024,512]{1,0:T(8,128)(2,1)}, bf16[1024,512]{1,0:T(8,128)(2,1)S(1)}, u32[]{:S(2)}) copy-start(bf16[1024,512]{1,0:T(8,128)(2,1)S(1)} %collective-permute-done.8.got) | copy-start | bytes 3145732
  33.0 24.6 %copy-start.13 = (bf16[128,512]{1,0:T(8,128)(2,1)S(1)}, bf16[128,512]{1,0:T(8,128)(2,1)}, u32[]{:S(2)}) copy-start(bf16[128,512]{1,0:T(8,128)(2,1)} %get-tuple-element.40) | copy-start | bytes 393220
  33.0 24.6 %copy-start.12 = (bf16[128,512]{1,0:T(8,128)(2,1)S(1)}, bf16[128,512]{1,0:T(8,128)(2,1)}, u32[]{:S(2)}) copy-start(bf16[128,512]{1,0:T(8,128)(2,1)} %get-tuple-element.41) | copy-start | bytes 393220
  33.0 24.7 %copy-start.11 = (bf16[128,512]{1,0:T(8,128)(2,1)S(1)}, bf16[128,512]{1,0:T(8,128)(2,1)}, u32[]{:S(2)}) copy-start(bf16[128,512]{1,0:T(8,128)(2,1)} %get-tuple-element.42) | copy-start | bytes 393220
  33.0 25.2 %copy-start.10 = (bf16[128,512]{1,0:T(8,128)(2,1)S(1)}, bf16[128,512]{1,0:T(8,128)(2,1)}, u32[]{:S(2)}) copy-start(bf16[128,512]{1,0:T(8,128)(2,1)} %get-tuple-element.43) | copy-start | bytes 393220
  33.0 20.1 %all-to-all-start = ((bf16[8,128,512]{2,1,0:T(8,128)(2,1)}), bf16[8,128,512]{2,1,0:T(8,128)(2,1)S(1)}, u32[]{:S(2)}, u32[]{:S(2)}) async-start(bf16[8,128,512]{2,1,0:T(8,128)(2,1)} %bitcast.16), calls=%async_computation | async-start | bytes 2097152 | tf_op jit(solution)/shard_map/all_to_all | solution.py:271
  53.1 1.0 %copy-start = (bf16[8,128,512]{2,1,0:T(8,128)(2,1)}, bf16[8,128,512]{2,1,0:T(8,128)(2,1)S(1)}, u32[]{:S(2)}) copy-start(bf16[8,128,512]{2,1,0:T(8,128)(2,1)S(1)} %all-to-all-done) | copy-start | bytes 3145732
  56.1 6.5 %collective-permute-start.9 = (bf16[64,512]{1,0:T(8,128)(2,1)}, bf16[64,512]{1,0:T(8,128)(2,1)S(1)}, u32[]{:S(2)}, u32[]{:S(2)}) collective-permute-start(bf16[64,512]{1,0:T(8,128)(2,1)} %get-tuple-element.47), channel_id=1, source_target_pairs={{0,8},{8,0},{1,9},{9,1},{2,10},{10,2},{3,11},{11,3},{4,12},{12,4},... | collective-permute-start | bytes 196616 | tf_op jit(solution)/shard_map/ppermute | solution.py:40
  57.6 9.0 %collective-permute-start.4 = (bf16[128,512]{1,0:T(8,128)(2,1)S(1)}, bf16[128,512]{1,0:T(8,128)(2,1)S(1)}, u32[]{:S(2)}, u32[]{:S(2)}) collective-permute-start(bf16[128,512]{1,0:T(8,128)(2,1)S(1)} %copy-done.13), channel_id=1, source_target_pairs={{0,1},{1,0},{2,3},{3,2},{4,5},{5,4},{6,7},{7,6},{8,9},{9,8},{10,11... | collective-permute-start | bytes 393224 | tf_op jit(solution)/shard_map/ppermute | solution.py:40
  57.6 9.0 %collective-permute-start.5 = (bf16[128,512]{1,0:T(8,128)(2,1)S(1)}, bf16[128,512]{1,0:T(8,128)(2,1)S(1)}, u32[]{:S(2)}, u32[]{:S(2)}) collective-permute-start(bf16[128,512]{1,0:T(8,128)(2,1)S(1)} %copy-done.12), channel_id=1, source_target_pairs={{0,2},{2,0},{1,3},{3,1},{4,6},{6,4},{5,7},{7,5},{8,10},{10,8},{9,1... | collective-permute-start | bytes 393224 | tf_op jit(solution)/shard_map/ppermute | solution.py:40
  57.7 8.9 %collective-permute-start.6 = (bf16[128,512]{1,0:T(8,128)(2,1)S(1)}, bf16[128,512]{1,0:T(8,128)(2,1)S(1)}, u32[]{:S(2)}, u32[]{:S(2)}) collective-permute-start(bf16[128,512]{1,0:T(8,128)(2,1)S(1)} %copy-done.11), channel_id=1, source_target_pairs={{0,4},{4,0},{1,5},{5,1},{2,6},{6,2},{3,7},{7,3},{8,12},{12,8},{9,1... | collective-permute-start | bytes 393224 | tf_op jit(solution)/shard_map/ppermute | solution.py:40
  58.2 9.6 %collective-permute-start.7 = (bf16[128,512]{1,0:T(8,128)(2,1)S(1)}, bf16[128,512]{1,0:T(8,128)(2,1)S(1)}, u32[]{:S(2)}, u32[]{:S(2)}) collective-permute-start(bf16[128,512]{1,0:T(8,128)(2,1)S(1)} %copy-done.10), channel_id=1, source_target_pairs={{0,8},{8,0},{1,9},{9,1},{2,10},{10,2},{3,11},{11,3},{4,12},{12,4},... | collective-permute-start | bytes 393224 | tf_op jit(solution)/shard_map/ppermute | solution.py:40
  63.5 8.1 %collective-permute-start.10 = (bf16[64,512]{1,0:T(8,128)(2,1)S(1)}, bf16[64,512]{1,0:T(8,128)(2,1)S(1)}, u32[]{:S(2)}, u32[]{:S(2)}) collective-permute-start(bf16[64,512]{1,0:T(8,128)(2,1)S(1)} %add_convert_fusion), channel_id=1, source_target_pairs={{0,16},{16,0},{1,17},{17,1},{2,18},{18,2},{3,19},{19,3},{4,20},{20... | collective-permute-start | bytes 196616 | tf_op jit(solution)/shard_map/ppermute | solution.py:40
  66.6 1.2 %copy-start.2 = (bf16[128,512]{1,0:T(8,128)(2,1)}, bf16[128,512]{1,0:T(8,128)(2,1)S(1)}, u32[]{:S(2)}) copy-start(bf16[128,512]{1,0:T(8,128)(2,1)S(1)} %collective-permute-done.4.refs_0_) | copy-start | bytes 393220
  66.6 1.2 %copy-start.3 = (bf16[128,512]{1,0:T(8,128)(2,1)}, bf16[128,512]{1,0:T(8,128)(2,1)S(1)}, u32[]{:S(2)}) copy-start(bf16[128,512]{1,0:T(8,128)(2,1)S(1)} %collective-permute-done.5.refs_1_) | copy-start | bytes 393220
  66.6 1.2 %copy-start.4 = (bf16[128,512]{1,0:T(8,128)(2,1)}, bf16[128,512]{1,0:T(8,128)(2,1)S(1)}, u32[]{:S(2)}) copy-start(bf16[128,512]{1,0:T(8,128)(2,1)S(1)} %collective-permute-done.6.refs_2_) | copy-start | bytes 393220
  (2 other events, 1.3 us)

commit v2 on v1

v2 whole, which is shorter than its diff:
```python
import functools

import jax
import jax.numpy as jnp
from jax import lax
from jax.experimental import pallas as pl
from jax.experimental.pallas import tpu as pltpu
from jax.sharding import Mesh, PartitionSpec as P


LANES = 128
ROOM = 24 << 20
BF16 = jnp.bfloat16
F32 = jnp.float32
VMEM = pl.BlockSpec(memory_space=pltpu.VMEM)
SMEM = pl.BlockSpec(memory_space=pltpu.SMEM)


def dot(former, latter):
    return jnp.dot(former, latter, preferred_element_type=F32)


def dot_rows(former, latter):
    return lax.dot_general(former, latter, (((0,), (0,)), ((), ())), preferred_element_type=F32)


def dot_cols(former, latter):
    return lax.dot_general(former, latter, (((1,), (1,)), ((), ())), preferred_element_type=F32)


def near(array):
    return pltpu.with_memory_space_constraint(array, pltpu.VMEM)


def far(array):
    return pltpu.with_memory_space_constraint(array, pltpu.HBM)


def call(body, outs, ins, kept=True, scratch=()):
    fresh = pltpu.VMEM if kept else jax.ShapeDtypeStruct
    return pl.pallas_call(
        body,
        out_shape=[fresh(shape, kind) for shape, kind in outs],
        in_specs=ins,
        out_specs=[VMEM] * len(outs),
        scratch_shapes=scratch,
        compiler_params=pltpu.CompilerParams(vmem_limit_bytes=ROOM),
    )


def swap(array, axis):
    return lax.ppermute(array, axis, [(0, 1), (1, 0)])


def down_rows(row, count):
    return jnp.transpose(jnp.broadcast_to(row, (LANES, count)))


def onehot_cols(index_cols, first, blocks):
    lane = lax.broadcasted_iota(jnp.int32, index_cols.shape, 1)
    parts = [
        jnp.where(index_cols == lane + (first + LANES * block), 1.0, 0.0).astype(BF16)
        for block in range(blocks)
    ]
    return jnp.concatenate(parts, axis=1)


def onehot_rows(index_row, first, rows):
    node = lax.broadcasted_iota(jnp.int32, (rows, index_row.shape[1]), 0) + first
    return jnp.where(node == index_row, 1.0, 0.0).astype(BF16)


def receiver_row(recv_block, recv_node):
    edges = recv_node.shape[1]
    return jnp.concatenate(
        [
            recv_node[:, LANES * block : LANES * (block + 1)] + recv_block[block] * LANES
            for block in range(edges // LANES)
        ],
        axis=1,
    )


def pick_body(send_blocks, node_lat, *lent):
    for section, out in enumerate(lent):
        out[...] = node_lat[pl.ds(pl.multiple_of(send_blocks[section] * LANES, LANES), LANES), :]


def early_body(
    rounds, recv_block, edge_src, recv_node, node_lat, edge_lat, grad_edge, grad_agg, weight_edge,
    weight_recv, recv_out, send_out, hot_out, preact_out, grad_msg_out,
):
    nodes = node_lat.shape[0]
    edges = edge_lat.shape[0]
    receiver = down_rows(receiver_row(recv_block, recv_node[...]), edges)
    sender = down_rows(edge_src[...], edges)
    hot_recv = onehot_cols(receiver, 0, nodes // LANES)
    recv_rows = dot(hot_recv, node_lat[...]).astype(BF16)
    recv_out[...] = recv_rows
    send_out[...] = dot(onehot_cols(sender, 0, nodes // LANES), node_lat[...]).astype(BF16)
    hot_out[...] = onehot_cols(sender, nodes, rounds)
    preact_out[...] = dot(edge_lat[...], weight_edge[...]) + dot(recv_rows, weight_recv[...])
    grad_msg_out[...] = grad_edge[...].astype(F32) + dot(hot_recv, grad_agg[...])


def main_body(
    rounds, plan, place, recv_rows, send_own, hot, preact_own, grad_msg, edge_lat, weight_send,
    weight_out, *refs,
):
    borrowed = refs[:rounds]
    give_out, keep_out, grad_preact_out, message_out = refs[rounds : rounds + 4]
    table, sums, send_ref, hidden_ref, grad_proj_ref = refs[rounds + 4 :]
    edges = edge_lat.shape[0]
    for section in range(rounds):
        table[LANES * section : LANES * (section + 1), :] = borrowed[section][...]
    step = edges // 2
    for start in range(0, edges, step):
        rows = slice(start, start + step)
        send = (send_own[rows, :].astype(F32) + dot(hot[rows, :], table[...])).astype(BF16)
        send_ref[rows, :] = send
        preact = preact_own[rows, :] + dot(send, weight_send[...])
        sigmoid = jax.nn.sigmoid(preact)
        hidden = (preact * sigmoid).astype(BF16)
        hidden_ref[rows, :] = hidden
        slope = sigmoid * (1.0 + preact * (1.0 - sigmoid))
        projected = dot(hidden, weight_out[...])
        centered = projected - jnp.mean(projected, axis=1, keepdims=True)
        inv_std = lax.rsqrt(jnp.mean(centered * centered, axis=1, keepdims=True) + 1e-05)
        normed = centered * inv_std
        message_out[rows, :] = normed.astype(BF16)
        grad = grad_msg[rows, :]
        grad_proj = inv_std * (
            grad
            - jnp.mean(grad, axis=1, keepdims=True)
            - normed * jnp.mean(grad * normed, axis=1, keepdims=True)
        )
        grad_proj = grad_proj.astype(BF16)
        grad_proj_ref[rows, :] = grad_proj
        grad_preact_out[rows, :] = (dot_cols(grad_proj, weight_out[...]) * slope).astype(BF16)
    grad_preact = grad_preact_out[...]
    sums[3] = dot_rows(hidden_ref[...], grad_proj_ref[...])
    sums[0] = dot_rows(edge_lat[...], grad_preact)
    sums[1] = dot_rows(send_ref[...], grad_preact)
    sums[2] = dot_rows(recv_rows[...], grad_preact)
    pieces, share = plan
    at = 0
    for whiches, flip, domain in pieces:
        for target, side in ((keep_out, 0), (give_out, 1)):
            first = pl.multiple_of((place[1] ^ (domain | side)) * share, share)
            parts = [
                sums[which ^ (flip * place[0]), pl.ds(first, share), :] for which in whiches
            ]
            count = share * len(parts)
            block = parts[0] if len(parts) == 1 else jnp.concatenate(parts, axis=0)
            target[at : at + count, :] = block.astype(target.dtype)
        at += count


def sums_body(recv_block, edge_src, recv_node, grad_preact, own_out, recv_out, *back_out):
    nodes = own_out.shape[0]
    rounds = len(back_out)
    receiver = receiver_row(recv_block, recv_node[...])
    rows = grad_preact[...]
    slot_sums = dot(onehot_rows(edge_src[...], 0, nodes + rounds * LANES), rows)
    own_out[...] = slot_sums[:nodes]
    for section in range(rounds):
        first = nodes + LANES * section
        back_out[section][...] = slot_sums[first : first + LANES].astype(BF16)
    recv_out[...] = dot(onehot_rows(receiver, 0, nodes), rows)


def split_body(colours, keep, got, *outs):
    span = keep.shape[0] // colours
    for colour in range(colours):
        keep_out, give_out = outs[2 * colour : 2 * colour + 2]
        for target, first in ((keep_out, span * colour), (give_out, span * colour + span // 2)):
            rows = slice(first, first + span // 2)
            target[...] = (keep[rows, :] + got[rows, :].astype(F32)).astype(target.dtype)


def merge_body(colours, size, *refs):
    keep_out, give_out = refs[2 * colours :]
    runs = refs[0].shape[0] // size
    for colour in range(colours):
        keep, got = refs[2 * colour : 2 * colour + 2]
        for run in range(runs):
            target = keep_out if run < runs // 2 else give_out
            rows = slice(run * size, (run + 1) * size)
            at = ((run % (runs // 2)) * colours + colour) * size
            target[at : at + size, :] = (keep[rows, :] + got[rows, :].astype(F32)).astype(
                target.dtype
            )


def round_body(keep, got, out):
    out[...] = (keep[...] + got[...].astype(F32)).astype(BF16)


def finish_body(place, *refs):
    *parts, out = refs
    take = parts[0].shape[0]
    for flip, part in enumerate(parts):
        first = pl.multiple_of((place[0] ^ flip) * take, take)
        out[pl.ds(first, take), :] = part[...].astype(F32)


def edge_body(recv_block, recv_node, grad_preact, message, grad_edge, weight_edge, agg_out, edge_out):
    receiver = receiver_row(recv_block, recv_node[...])
    agg_out[...] = dot(onehot_rows(receiver, 0, agg_out.shape[0]), message[...]).astype(BF16)
    edge_out[...] = (
        grad_edge[...].astype(F32) + dot_cols(grad_preact[...], weight_edge[...])
    ).astype(BF16)


def dot_cols_split(former, latter):
    high = former.astype(BF16)
    low = (former - high.astype(F32)).astype(BF16)
    return dot_cols(high, latter) + dot_cols(low, latter)


def node_body(send_blocks, own_sums, recv_sums, weight_send, weight_recv, *refs):
    returned, out, total = refs[:-2], refs[-2], refs[-1]
    total[...] = own_sums[...]
    for section, block in enumerate(returned):
        rows = pl.ds(pl.multiple_of(send_blocks[section] * LANES, LANES), LANES)
        total[rows, :] = total[rows, :] + block[...].astype(F32)
    out[...] = (
        dot_cols_split(total[...], weight_send[...])
        + dot_cols_split(recv_sums[...], weight_recv[...])
    ).astype(BF16)


def layout(share, parts, tops):
    colours = 2 if parts == 2 and tops and share >= 16 else 1
    per_part = 4 // parts
    orders = [(["part"] if parts == 2 else []) + list(range(1, tops + 1))]
    if colours == 2:
        orders.append([1, "part"] + list(range(2, tops + 1)))
    pieces = []
    for colour, order in enumerate(orders):
        whiches = tuple(range(per_part))[colour * per_part // colours :][: per_part // colours]
        for index in range(2 ** len(order)):
            domain, flip = 0, 0
            for level, bit in enumerate(order):
                on = index >> (len(order) - 1 - level) & 1
                if bit == "part":
                    flip = on
                else:
                    domain |= on << bit
            pieces.append((tuple(which ^ (flip * per_part) for which in whiches), per_part, domain))
    return tuple(pieces), orders, share * per_part // colours


def per_device(
    traj_axes, dom_axes, node_lat, edge_lat, grad_edge, grad_agg, weight_edge, weight_send,
    weight_recv, weight_out, edge_src, edge_recv_block, edge_recv_node, send_blocks,
):
    node_lat, edge_lat, grad_edge, grad_agg = node_lat[0], edge_lat[0], grad_edge[0], grad_agg[0]
    nodes, features = node_lat.shape
    edges = edge_lat.shape[0]
    rounds = send_blocks.shape[0]
    edge_src = edge_src.reshape(1, edges)
    recv_node = edge_recv_node.reshape(1, edges)
    bits = dom_axes[::-1]
    share = features // 2 ** len(bits)
    split = traj_axes[:1] if 2 * share >= 16 else ()
    pieces, orders, size = layout(share, 1 + len(split), len(bits) - 1)
    colours = len(orders)
    half = 2 * features
    wide = ((edges, features), BF16)
    wide_sum = ((edges, features), F32)
    node_sum = ((nodes, features), F32)
    block = ((LANES, features), BF16)
    part = lax.axis_index(split[0]) if split else 0
    place = jnp.stack([jnp.int32(part), lax.axis_index(dom_axes).astype(jnp.int32)])

    lent = call(pick_body, [block] * rounds, [SMEM, VMEM])(
        far(send_blocks), far(node_lat)
    )
    borrowed = [swap(lent[section], bits[section]) for section in range(rounds)]
    recv_rows, send_own, hot, preact_own, grad_msg = call(
        functools.partial(early_body, rounds),
        [wide, wide, ((edges, rounds * LANES), BF16), wide_sum, wide_sum],
        [SMEM] + [VMEM] * 8,
    )(
        *map(far, (edge_recv_block, edge_src, recv_node, node_lat, edge_lat)),
        *map(far, (grad_edge, grad_agg, weight_edge, weight_recv)),
    )
    give, keep, grad_preact, message = call(
        functools.partial(main_body, rounds, (pieces, share)),
        [((half, features), BF16), ((half, features), F32), wide, wide],
        [SMEM] + [VMEM] * (8 + rounds),
        scratch=[
            pltpu.VMEM((rounds * LANES, features), BF16),
            pltpu.VMEM((4, features, features), F32),
            pltpu.VMEM((edges, features), BF16),
            pltpu.VMEM((edges, features), BF16),
            pltpu.VMEM((edges, features), BF16),
        ],
    )(
        place, recv_rows, send_own, hot, preact_own, grad_msg, near(edge_lat),
        near(weight_send), near(weight_out), *map(near, borrowed),
    )

    own_sums, recv_sums, *back = call(
        sums_body, [node_sum, node_sum] + [block] * rounds, [SMEM] + [VMEM] * 3
    )(edge_recv_block, edge_src, recv_node, grad_preact)
    returned = [swap(back[section], bits[section]) for section in range(rounds)]

    def axis_of(bit):
        return split[0] if bit == "part" else bits[bit]

    def halves(rows):
        return [((rows // 2, features), F32), ((rows // 2, features), BF16)]

    got = swap(give, bits[0])
    flows = call(
        functools.partial(split_body, colours), halves(half // colours) * colours, [VMEM] * 2
    )(keep, near(got))
    depth = len(orders[0])
    level = 0
    rows = half // colours // 2
    flows = [(flows[2 * colour], flows[2 * colour + 1], order) for colour, order in enumerate(orders)]
    while True:
        pairs = []
        for keep, give, order in flows:
            pairs += [keep, near(swap(give, axis_of(order[level])))]
        level += 1
        if level == depth:
            break
        merged = len(flows) if level == colours else 1
        if len(flows) == 2 and merged == 1:
            flows = [
                (*call(functools.partial(split_body, 1), halves(rows), [VMEM] * 2)(*pairs[2 * colour : 2 * colour + 2]), order)
                for colour, (_, _, order) in enumerate(flows)
            ]
            rows //= 2
        else:
            keep, give = call(
                functools.partial(merge_body, merged, size), halves(rows * merged), [VMEM] * (2 * merged)
            )(*pairs)
            flows = [(keep, give, orders[0])]
            rows = rows * merged // 2
    (total,) = call(round_body, [((rows, features), BF16)], [VMEM] * 2)(*pairs)
    for axis in traj_axes[len(split) :]:
        (total,) = call(round_body, [((rows, features), BF16)], [VMEM] * 2)(
            total, near(swap(total, axis))
        )
    parts = [total] + [near(swap(total, axis)) for axis in split]
    (weight_grads,) = call(
        finish_body, [((4 * share, features), F32)], [SMEM] + [VMEM] * len(parts), kept=False
    )(place, *parts)
    agg, grad_edges = call(
        edge_body, [((nodes, features), BF16), wide], [SMEM] + [VMEM] * 5, kept=False
    )(edge_recv_block, recv_node, grad_preact, message, grad_edge, weight_edge)
    (grad_nodes,) = call(
        node_body,
        [((nodes, features), BF16)],
        [SMEM] + [VMEM] * (4 + rounds),
        kept=False,
        scratch=[pltpu.VMEM((nodes, features), F32)],
    )(send_blocks, own_sums, recv_sums, weight_send, weight_recv, *map(near, returned))
    return agg[None], grad_edges[None], grad_nodes[None], weight_grads.reshape(4, share, features)


def solution(mesh):
    traj_axes = tuple(f"t{bit}" for bit in reversed(range(mesh.shape["traj"].bit_length() - 1)))
    dom_axes = tuple(f"d{bit}" for bit in reversed(range(mesh.shape["dom"].bit_length() - 1)))
    names = traj_axes + dom_axes
    bit_mesh = Mesh(mesh.devices.reshape((2,) * len(names)), names)
    rows = P(traj_axes, dom_axes, None)
    in_specs = (rows,) * 4 + (P(),) * 4 + (P(dom_axes),) * 4
    out_specs = (rows,) * 3 + (P(None, dom_axes, None),)

    def body(*arrays):
        return per_device(traj_axes, dom_axes, *arrays)

    return jax.shard_map(
        body, mesh=bit_mesh, in_specs=in_specs, out_specs=out_specs, check_vma=False
    )
```

time: 72.8 us -> 61 us (0.84)
  Pallas kernels: 26 us -> 15.4 us
  starting transfers between devices: 14.9 us -> 18.7 us
  local copies, waits for them, and re-layouts: 3.3 us -> 0.05 us
  other arithmetic: 1.68 us -> 0.08 us
    ppermute x11 -> x16, waiting for transfers between devices: 9.34 us -> 25.8 us  [swap(): return lax.ppermute(array, axis, [(0, 1), (1, 0)])]
    all_to_all x1 -> x0, waiting for transfers between devices: 16.4 us -> none  [per_device(): lax.all_to_all(chip, split + mids, split_axis=0, concat_axis=0, tiled=True)]
    pallas_call x7 -> x13, Pallas kernels: 26 us -> 15.4 us  [the longest x1 4.38 us: per_device(): call(functools.partial(main_body, rounds, (pieces, share)), [((half, feat...]
    ppermute x11 -> x16, starting transfers between devices: 11.2 us -> 18.7 us  [swap(): return lax.ppermute(array, axis, [(0, 1), (1, 0)])]
    all_to_all x1 -> x0, starting transfers between devices: 3.7 us -> none  [per_device(): lax.all_to_all(chip, split + mids, split_axis=0, concat_axis=0, tiled=True)]
    unnamed x28 -> x20, local copies, waits for them, and re-layouts: 3.3 us -> 0.05 us
    convert_element_type x2 -> x0, other arithmetic: 1.65 us -> none  [the longest x1 0.92 us: per_device(): total = total.astype(BF16)]
  transfers between devices with their start and end apart: 12 -> 16, of which waited for: 5 -> 8; matrix products, arithmetic and copies ran while one was open for 1% -> 0% of each run, Pallas kernels for 14% -> 14%
where the time goes in v2:
time: 61 us; the launch traced here: 60.8 us
  waiting for transfers between devices  25.8 us (42%)
  starting transfers between devices  18.7 us (31%)
  Pallas kernels  15.4 us (25%)
  between operations  0.81 us (1%)
    ppermute x16, waiting for transfers between devices, swap(): return lax.ppermute(array, axis, [(0, 1), (1, 0)])  25.8 us
    ppermute x16, starting transfers between devices, swap(): return lax.ppermute(array, axis, [(0, 1), (1, 0)])  18.7 us
    pallas_call x1, Pallas kernels, per_device(): call(functools.partial(main_body, rounds, (pieces, share)), [((half, feat...  4.38 us
    pallas_call x1, Pallas kernels, per_device(): call(functools.partial(early_body, rounds), [wide, wide, ((edges, rounds...  2.95 us
    pallas_call x1, Pallas kernels, per_device(): call(node_body, [((nodes, features), BF16)], [SMEM] + [VMEM] * (4 + round...  2.08 us
    pallas_call x1, Pallas kernels, per_device(): call(edge_body, [((nodes, features), BF16), wide], [SMEM] + [VMEM] * 5, k...  1.91 us
    pallas_call x1, Pallas kernels, per_device(): call(finish_body, [((4 * share, features), F32)], [SMEM] + [VMEM] * len(p...  1.26 us
    pallas_call x1, Pallas kernels, per_device(): call(sums_body, [node_sum, node_sum] + [block] * rounds, [SMEM] + [VMEM]...  1.24 us
  transfers between devices with their start and end apart: 16, of which 8 were waited for; matrix products, arithmetic and copies ran while one was open for 0% of the time, Pallas kernels for 14%

profile of v2, /device:TPU:0, one launch (start us, length us, event | category | flops | bytes accessed | tf_op | source)
XLA Modules:
  0.0 60.8 jit_solution(16218107528069391887)
XLA Ops:
  0.7 1.1 %shard_map.148 = (bf16[128,512]{1,0:T(8,128)(2,1)S(1)}, bf16[128,512]{1,0:T(8,128)(2,1)S(1)}, bf16[128,512]{1,0:T(8,128)(2,1)S(1)}, bf16[128,512]{1,0:T(8,128)(2,1)S(1)}) custom-call(s32[4]{0:T(128)} %send_blocks.3, bf16[256,512]{1,0:T(8,128)(2,1)} %bitcast.21), custom_call_target="tpu_custom_call" | custom-call | tf_op jit(solution)/shard_map/pallas_call | solution.py:277
  2.3 2.6 %collective-permute-start.1 = (bf16[128,512]{1,0:T(8,128)(2,1)S(1)}, bf16[128,512]{1,0:T(8,128)(2,1)S(1)}, u32[]{:S(2)}, u32[]{:S(2)}) collective-permute-start(bf16[128,512]{1,0:T(8,128)(2,1)S(1)} %get-tuple-element.43), channel_id=1, source_target_pairs={{0,2},{2,0},{1,3},{3,1},{4,6},{6,4},{5,7},{7,5},{8,10},{10,8},{9,1... | collective-permute-start | bytes 393224 | tf_op jit(solution)/shard_map/ppermute | solution.py:52
  4.9 1.6 %collective-permute-start.2 = (bf16[128,512]{1,0:T(8,128)(2,1)S(1)}, bf16[128,512]{1,0:T(8,128)(2,1)S(1)}, u32[]{:S(2)}, u32[]{:S(2)}) collective-permute-start(bf16[128,512]{1,0:T(8,128)(2,1)S(1)} %get-tuple-element.44), channel_id=1, source_target_pairs={{0,4},{4,0},{1,5},{5,1},{2,6},{6,2},{3,7},{7,3},{8,12},{12,8},{9,1... | collective-permute-start | bytes 393224 | tf_op jit(solution)/shard_map/ppermute | solution.py:52
  6.5 2.6 %collective-permute-start.3 = (bf16[128,512]{1,0:T(8,128)(2,1)S(1)}, bf16[128,512]{1,0:T(8,128)(2,1)S(1)}, u32[]{:S(2)}, u32[]{:S(2)}) collective-permute-start(bf16[128,512]{1,0:T(8,128)(2,1)S(1)} %get-tuple-element.45), channel_id=1, source_target_pairs={{0,8},{8,0},{1,9},{9,1},{2,10},{10,2},{3,11},{11,3},{4,12},{12,4},... | collective-permute-start | bytes 393224 | tf_op jit(solution)/shard_map/ppermute | solution.py:52
  9.1 3.0 %shard_map.147 = (bf16[512,512]{1,0:T(8,128)(2,1)S(1)}, bf16[512,512]{1,0:T(8,128)(2,1)S(1)}, bf16[512,512]{1,0:T(8,128)(2,1)S(1)}, f32[512,512]{1,0:T(8,128)S(1)}, f32[512,512]{1,0:T(8,128)S(1)}) custom-call(s32[4]{0:T(128)} %recv_block.5, s32[1,512]{1,0:T(1,128)} %bitcast.19, s32[1,512]{1,0:T(1,128)} %bitcast.16, bf16[256,512]{1,0:T(8,128)(2,1)} %bitcast.22, ...), custom_call_target="tpu_custom_call" | custom-call | tf_op jit(solution)/shard_map/pallas_call | solution.py:281
  12.1 0.7 %collective-permute-done.2.refs_2_ = bf16[128,512]{1,0:T(8,128)(2,1)S(1)} collective-permute-done((bf16[128,512]{1,0:T(8,128)(2,1)S(1)}, bf16[128,512]{1,0:T(8,128)(2,1)S(1)}, u32[]{:S(2)}, u32[]{:S(2)}) %collective-permute-start.2) | collective-permute-done | bytes 131104 | tf_op jit(solution)/shard_map/ppermute | solution.py:52
  12.8 2.7 %collective-permute-done.3.refs_3_ = bf16[128,512]{1,0:T(8,128)(2,1)S(1)} collective-permute-done((bf16[128,512]{1,0:T(8,128)(2,1)S(1)}, bf16[128,512]{1,0:T(8,128)(2,1)S(1)}, u32[]{:S(2)}, u32[]{:S(2)}) %collective-permute-start.3) | collective-permute-done | bytes 131104 | tf_op jit(solution)/shard_map/ppermute | solution.py:52
  15.5 4.4 %shard_map.149 = (bf16[1024,512]{1,0:T(8,128)(2,1)S(1)}, f32[1024,512]{1,0:T(8,128)S(1)}, bf16[512,512]{1,0:T(8,128)(2,1)S(1)}, bf16[512,512]{1,0:T(8,128)(2,1)S(1)}) custom-call(s32[2]{0:T(128)S(1)} %pad_add_fusion.place, bf16[512,512]{1,0:T(8,128)(2,1)S(1)} %get-tuple-element.37.recv_rows, bf16[512,512]{1,0:T(8,128)(2,1)S(1)} %get-tuple-element.38.send_own, ...), custom_call_target="tpu_custom_call" | custom-call | tf_op jit(solution)/shard_map/pallas_call | solution.py:289
  20.0 2.6 %collective-permute-done.8.got = bf16[1024,512]{1,0:T(8,128)(2,1)S(1)} collective-permute-done((bf16[1024,512]{1,0:T(8,128)(2,1)S(1)}, bf16[1024,512]{1,0:T(8,128)(2,1)S(1)}, u32[]{:S(2)}, u32[]{:S(2)}) %collective-permute-start.8) | collective-permute-done | bytes 1048608 | tf_op jit(solution)/shard_map/ppermute | solution.py:52
  22.9 1.5 %collective-permute-start.9 = (bf16[256,512]{1,0:T(8,128)(2,1)S(1)}, bf16[256,512]{1,0:T(8,128)(2,1)S(1)}, u32[]{:S(2)}, u32[]{:S(2)}) collective-permute-start(bf16[256,512]{1,0:T(8,128)(2,1)S(1)} %get-tuple-element.59), channel_id=1, source_target_pairs={{0,16},{16,0},{1,17},{17,1},{2,18},{18,2},{3,19},{19,3},{4,20},{20... | collective-permute-start | bytes 786440 | tf_op jit(solution)/shard_map/ppermute | solution.py:52
  25.0 6.3 %collective-permute-done.9.got = bf16[256,512]{1,0:T(8,128)(2,1)S(1)} collective-permute-done((bf16[256,512]{1,0:T(8,128)(2,1)S(1)}, bf16[256,512]{1,0:T(8,128)(2,1)S(1)}, u32[]{:S(2)}, u32[]{:S(2)}) %collective-permute-start.9) | collective-permute-done | bytes 262176 | tf_op jit(solution)/shard_map/ppermute | solution.py:52
  32.6 1.0 %collective-permute-start.12 = (bf16[128,512]{1,0:T(8,128)(2,1)S(1)}, bf16[128,512]{1,0:T(8,128)(2,1)S(1)}, u32[]{:S(2)}, u32[]{:S(2)}) collective-permute-start(bf16[128,512]{1,0:T(8,128)(2,1)S(1)} %get-tuple-element.65), channel_id=1, source_target_pairs={{0,16},{16,0},{1,17},{17,1},{2,18},{18,2},{3,19},{19,3},{4,20},{20... | collective-permute-start | bytes 393224 | tf_op jit(solution)/shard_map/ppermute | solution.py:52
  33.6 2.8 %collective-permute-done.10.refs_1_ = bf16[128,512]{1,0:T(8,128)(2,1)S(1)} collective-permute-done((bf16[128,512]{1,0:T(8,128)(2,1)S(1)}, bf16[128,512]{1,0:T(8,128)(2,1)S(1)}, u32[]{:S(2)}, u32[]{:S(2)}) %collective-permute-start.10) | collective-permute-done | bytes 131104 | tf_op jit(solution)/shard_map/ppermute | solution.py:52
  36.4 1.2 %collective-permute-done.12.refs_3_ = bf16[128,512]{1,0:T(8,128)(2,1)S(1)} collective-permute-done((bf16[128,512]{1,0:T(8,128)(2,1)S(1)}, bf16[128,512]{1,0:T(8,128)(2,1)S(1)}, u32[]{:S(2)}, u32[]{:S(2)}) %collective-permute-start.12) | collective-permute-done | bytes 131104 | tf_op jit(solution)/shard_map/ppermute | solution.py:52
  38.2 1.2 %shard_map.151 = (f32[256,512]{1,0:T(8,128)S(1)}, f32[256,512]{1,0:T(8,128)S(1)}, bf16[128,512]{1,0:T(8,128)(2,1)S(1)}, bf16[128,512]{1,0:T(8,128)(2,1)S(1)}, bf...) custom-call(s32[4]{0:T(128)S(1)} %copy-done.8, s32[1,512]{1,0:T(1,128)S(1)} %bitcast.20, s32[1,512]{1,0:T(1,128)S(1)} %bitcast.17, ...), custom_call_target="tpu_custom_call" | custom-call | tf_op jit(solution)/shard_map/pallas_call | solution.py:305
  39.5 1.0 %collective-permute-start.5 = (bf16[128,512]{1,0:T(8,128)(2,1)S(1)}, bf16[128,512]{1,0:T(8,128)(2,1)S(1)}, u32[]{:S(2)}, u32[]{:S(2)}) collective-permute-start(bf16[128,512]{1,0:T(8,128)(2,1)S(1)} %get-tuple-element.53), channel_id=1, source_target_pairs={{0,2},{2,0},{1,3},{3,1},{4,6},{6,4},{5,7},{7,5},{8,10},{10,8},{9,1... | collective-permute-start | bytes 393224 | tf_op jit(solution)/shard_map/ppermute | solution.py:52
  40.5 1.6 %collective-permute-start.6 = (bf16[128,512]{1,0:T(8,128)(2,1)S(1)}, bf16[128,512]{1,0:T(8,128)(2,1)S(1)}, u32[]{:S(2)}, u32[]{:S(2)}) collective-permute-start(bf16[128,512]{1,0:T(8,128)(2,1)S(1)} %get-tuple-element.54), channel_id=1, source_target_pairs={{0,4},{4,0},{1,5},{5,1},{2,6},{6,2},{3,7},{7,3},{8,12},{12,8},{9,1... | collective-permute-start | bytes 393224 | tf_op jit(solution)/shard_map/ppermute | solution.py:52
  42.1 1.1 %collective-permute-start.7 = (bf16[128,512]{1,0:T(8,128)(2,1)S(1)}, bf16[128,512]{1,0:T(8,128)(2,1)S(1)}, u32[]{:S(2)}, u32[]{:S(2)}) collective-permute-start(bf16[128,512]{1,0:T(8,128)(2,1)S(1)} %get-tuple-element.55), channel_id=1, source_target_pairs={{0,8},{8,0},{1,9},{9,1},{2,10},{10,2},{3,11},{11,3},{4,12},{12,4},... | collective-permute-start | bytes 393224 | tf_op jit(solution)/shard_map/ppermute | solution.py:52
  43.2 1.9 %collective-permute-start.14 = (bf16[64,512]{1,0:T(8,128)(2,1)S(1)}, bf16[64,512]{1,0:T(8,128)(2,1)S(1)}, u32[]{:S(2)}, u32[]{:S(2)}) collective-permute-start(bf16[64,512]{1,0:T(8,128)(2,1)S(1)} %get-tuple-element.69), channel_id=1, source_target_pairs={{0,8},{8,0},{1,9},{9,1},{2,10},{10,2},{3,11},{11,3},{4,12},{12,4},... | collective-permute-start | bytes 196616 | tf_op jit(solution)/shard_map/ppermute | solution.py:52
  45.1 8.8 %collective-permute-done.14.got = bf16[64,512]{1,0:T(8,128)(2,1)S(1)} collective-permute-done((bf16[64,512]{1,0:T(8,128)(2,1)S(1)}, bf16[64,512]{1,0:T(8,128)(2,1)S(1)}, u32[]{:S(2)}, u32[]{:S(2)}) %collective-permute-start.14) | collective-permute-done | bytes 65568 | tf_op jit(solution)/shard_map/ppermute | solution.py:52
  54.0 1.5 %collective-permute-start.15 = (bf16[64,512]{1,0:T(8,128)(2,1)S(1)}, bf16[64,512]{1,0:T(8,128)(2,1)S(1)}, u32[]{:S(2)}, u32[]{:S(2)}) collective-permute-start(bf16[64,512]{1,0:T(8,128)(2,1)S(1)} %shard_map.158.refs_0_), channel_id=1, source_target_pairs={{0,16},{16,0},{1,17},{17,1},{2,18},{18,2},{3,19},{19,3},{4,20},{20... | collective-permute-start | bytes 196616 | tf_op jit(solution)/shard_map/ppermute | solution.py:52
  55.5 1.9 %shard_map.150 = (bf16[256,512]{1,0:T(8,128)(2,1)}, bf16[512,512]{1,0:T(8,128)(2,1)}) custom-call(s32[4]{0:T(128)S(1)} %copy-done.8, s32[1,512]{1,0:T(1,128)S(1)} %bitcast.18, bf16[512,512]{1,0:T(8,128)(2,1)S(1)} %get-tuple-element.46.grad_preact, bf16[512,512]{1,0:T(8,128)(2,1)S(1)} %get-tuple-element.47.message, bf16[512,512]{1,0:T(8,128)(2,1)S(1)} %bitcast.15, ...), custom_call_target="tpu_custom_call" | custom-call | tf_op jit(solution)/shard_map/pallas_call | solution.py:353
  57.5 2.1 %shard_map.152 = bf16[256,512]{1,0:T(8,128)(2,1)} custom-call(s32[4]{0:T(128)S(1)} %copy-done.9, f32[256,512]{1,0:T(8,128)S(1)} %get-tuple-element.50.own_sums, f32[256,512]{1,0:T(8,128)S(1)} %get-tuple-element.51.recv_sums, bf16[512,512]{1,0:T(8,128)(2,1)S(1)} %copy-done.1, bf16[512,512]{1,0:T(8,128)(2,1)S(1)} %copy-done.4, ...), custom_call_target="tpu_custom_call" | custom-call | tf_op jit(solution)/shard_map/pallas_call | solution.py:356
  59.6 1.3 %shard_map.159 = f32[128,512]{1,0:T(8,128)} custom-call(s32[2]{0:T(128)S(1)} %pad_add_fusion.place, bf16[64,512]{1,0:T(8,128)(2,1)S(1)} %shard_map.158.refs_0_, bf16[64,512]{1,0:T(8,128)(2,1)S(1)} %collective-permute-done.15.refs_1_), custom_call_target="tpu_custom_call" | custom-call | tf_op jit(solution)/shard_map/pallas_call | solution.py:350
  (42 shorter events, 3.4 us)
Async XLA Ops:
  0.6 14.9 %copy-start = (bf16[1,512,512]{2,1,0:T(8,128)(2,1)S(1)}, bf16[1,512,512]{2,1,0:T(8,128)(2,1)}, u32[]{:S(2)}) copy-start(bf16[1,512,512]{2,1,0:T(8,128)(2,1)} %param.13) | copy-start | bytes 1572868
  1.8 10.3 %collective-permute-start = (bf16[128,512]{1,0:T(8,128)(2,1)S(1)}, bf16[128,512]{1,0:T(8,128)(2,1)S(1)}, u32[]{:S(2)}, u32[]{:S(2)}) collective-permute-start(bf16[128,512]{1,0:T(8,128)(2,1)S(1)} %get-tuple-element.42), channel_id=1, source_target_pairs={{0,1},{1,0},{2,3},{3,2},{4,5},{5,4},{6,7},{7,6},{8,9},{9,8},{10,11... | collective-permute-start | bytes 393224 | tf_op jit(solution)/shard_map/ppermute | solution.py:52
  2.3 9.8 %collective-permute-start.1 = (bf16[128,512]{1,0:T(8,128)(2,1)S(1)}, bf16[128,512]{1,0:T(8,128)(2,1)S(1)}, u32[]{:S(2)}, u32[]{:S(2)}) collective-permute-start(bf16[128,512]{1,0:T(8,128)(2,1)S(1)} %get-tuple-element.43), channel_id=1, source_target_pairs={{0,2},{2,0},{1,3},{3,1},{4,6},{6,4},{5,7},{7,5},{8,10},{10,8},{9,1... | collective-permute-start | bytes 393224 | tf_op jit(solution)/shard_map/ppermute | solution.py:52
  4.9 7.9 %collective-permute-start.2 = (bf16[128,512]{1,0:T(8,128)(2,1)S(1)}, bf16[128,512]{1,0:T(8,128)(2,1)S(1)}, u32[]{:S(2)}, u32[]{:S(2)}) collective-permute-start(bf16[128,512]{1,0:T(8,128)(2,1)S(1)} %get-tuple-element.44), channel_id=1, source_target_pairs={{0,4},{4,0},{1,5},{5,1},{2,6},{6,2},{3,7},{7,3},{8,12},{12,8},{9,1... | collective-permute-start | bytes 393224 | tf_op jit(solution)/shard_map/ppermute | solution.py:52
  6.5 9.0 %collective-permute-start.3 = (bf16[128,512]{1,0:T(8,128)(2,1)S(1)}, bf16[128,512]{1,0:T(8,128)(2,1)S(1)}, u32[]{:S(2)}, u32[]{:S(2)}) collective-permute-start(bf16[128,512]{1,0:T(8,128)(2,1)S(1)} %get-tuple-element.45), channel_id=1, source_target_pairs={{0,8},{8,0},{1,9},{9,1},{2,10},{10,2},{3,11},{11,3},{4,12},{12,4},... | collective-permute-start | bytes 393224 | tf_op jit(solution)/shard_map/ppermute | solution.py:52
  19.9 2.7 %collective-permute-start.8 = (bf16[1024,512]{1,0:T(8,128)(2,1)S(1)}, bf16[1024,512]{1,0:T(8,128)(2,1)S(1)}, u32[]{:S(2)}, u32[]{:S(2)}) collective-permute-start(bf16[1024,512]{1,0:T(8,128)(2,1)S(1)} %get-tuple-element.57), channel_id=1, source_target_pairs={{0,1},{1,0},{2,3},{3,2},{4,5},{5,4},{6,7},{7,6},{8,9},{9,8},{10,11... | collective-permute-start | bytes 3145736 | tf_op jit(solution)/shard_map/ppermute | solution.py:52
  22.7 15.5 %copy-start.6 = (s32[512]{0:T(512)S(1)}, s32[512]{0:T(512)}, u32[]{:S(2)}) copy-start(s32[512]{0:T(512)} %param.22) | copy-start | bytes 6148
  22.7 15.5 %copy-start.7 = (s32[512]{0:T(512)S(1)}, s32[512]{0:T(512)}, u32[]{:S(2)}) copy-start(s32[512]{0:T(512)} %param.20) | copy-start | bytes 6148
  22.7 15.5 %copy-start.8 = (s32[4]{0:T(128)S(1)}, s32[4]{0:T(128)}, u32[]{:S(2)}) copy-start(s32[4]{0:T(128)} %recv_block.5) | copy-start | bytes 52
  22.9 32.6 %copy-start.2 = (bf16[1,512,512]{2,1,0:T(8,128)(2,1)S(1)}, bf16[1,512,512]{2,1,0:T(8,128)(2,1)}, u32[]{:S(2)}) copy-start(bf16[1,512,512]{2,1,0:T(8,128)(2,1)} %param.14) | copy-start | bytes 1572868
  22.9 32.6 %copy-start.3 = (bf16[512,512]{1,0:T(8,128)(2,1)S(1)}, bf16[512,512]{1,0:T(8,128)(2,1)}, u32[]{:S(2)}) copy-start(bf16[512,512]{1,0:T(8,128)(2,1)} %weight_edge.3) | copy-start | bytes 1572868
  22.9 8.4 %collective-permute-start.9 = (bf16[256,512]{1,0:T(8,128)(2,1)S(1)}, bf16[256,512]{1,0:T(8,128)(2,1)S(1)}, u32[]{:S(2)}, u32[]{:S(2)}) collective-permute-start(bf16[256,512]{1,0:T(8,128)(2,1)S(1)} %get-tuple-element.59), channel_id=1, source_target_pairs={{0,16},{16,0},{1,17},{17,1},{2,18},{18,2},{3,19},{19,3},{4,20},{20... | collective-permute-start | bytes 786440 | tf_op jit(solution)/shard_map/ppermute | solution.py:52
  24.4 8.1 %collective-permute-start.11 = (bf16[256,512]{1,0:T(8,128)(2,1)S(1)}, bf16[256,512]{1,0:T(8,128)(2,1)S(1)}, u32[]{:S(2)}, u32[]{:S(2)}) collective-permute-start(bf16[256,512]{1,0:T(8,128)(2,1)S(1)} %get-tuple-element.63), channel_id=1, source_target_pairs={{0,2},{2,0},{1,3},{3,1},{4,6},{6,4},{5,7},{7,5},{8,10},{10,8},{9,1... | collective-permute-start | bytes 786440 | tf_op jit(solution)/shard_map/ppermute | solution.py:52
  31.4 5.0 %collective-permute-start.10 = (bf16[128,512]{1,0:T(8,128)(2,1)S(1)}, bf16[128,512]{1,0:T(8,128)(2,1)S(1)}, u32[]{:S(2)}, u32[]{:S(2)}) collective-permute-start(bf16[128,512]{1,0:T(8,128)(2,1)S(1)} %get-tuple-element.61), channel_id=1, source_target_pairs={{0,2},{2,0},{1,3},{3,1},{4,6},{6,4},{5,7},{7,5},{8,10},{10,8},{9,1... | collective-permute-start | bytes 393224 | tf_op jit(solution)/shard_map/ppermute | solution.py:52
  32.6 24.9 %copy-start.4 = (bf16[512,512]{1,0:T(8,128)(2,1)S(1)}, bf16[512,512]{1,0:T(8,128)(2,1)}, u32[]{:S(2)}) copy-start(bf16[512,512]{1,0:T(8,128)(2,1)} %weight_recv.3) | copy-start | bytes 1572868
  32.6 24.9 %copy-start.9 = (s32[4]{0:T(128)S(1)}, s32[4]{0:T(128)}, u32[]{:S(2)}) copy-start(s32[4]{0:T(128)} %send_blocks.3) | copy-start | bytes 52
  32.6 5.0 %collective-permute-start.12 = (bf16[128,512]{1,0:T(8,128)(2,1)S(1)}, bf16[128,512]{1,0:T(8,128)(2,1)S(1)}, u32[]{:S(2)}, u32[]{:S(2)}) collective-permute-start(bf16[128,512]{1,0:T(8,128)(2,1)S(1)} %get-tuple-element.65), channel_id=1, source_target_pairs={{0,16},{16,0},{1,17},{17,1},{2,18},{18,2},{3,19},{19,3},{4,20},{20... | collective-permute-start | bytes 393224 | tf_op jit(solution)/shard_map/ppermute | solution.py:52
  37.7 5.5 %collective-permute-start.13 = (bf16[128,512]{1,0:T(8,128)(2,1)S(1)}, bf16[128,512]{1,0:T(8,128)(2,1)S(1)}, u32[]{:S(2)}, u32[]{:S(2)}) collective-permute-start(bf16[128,512]{1,0:T(8,128)(2,1)S(1)} %get-tuple-element.67), channel_id=1, source_target_pairs={{0,4},{4,0},{1,5},{5,1},{2,6},{6,2},{3,7},{7,3},{8,12},{12,8},{9,1... | collective-permute-start | bytes 393224 | tf_op jit(solution)/shard_map/ppermute | solution.py:52
  39.4 18.0 %collective-permute-start.4 = (bf16[128,512]{1,0:T(8,128)(2,1)S(1)}, bf16[128,512]{1,0:T(8,128)(2,1)S(1)}, u32[]{:S(2)}, u32[]{:S(2)}) collective-permute-start(bf16[128,512]{1,0:T(8,128)(2,1)S(1)} %get-tuple-element.52), channel_id=1, source_target_pairs={{0,1},{1,0},{2,3},{3,2},{4,5},{5,4},{6,7},{7,6},{8,9},{9,8},{10,11... | collective-permute-start | bytes 393224 | tf_op jit(solution)/shard_map/ppermute | solution.py:52
  39.5 17.9 %collective-permute-start.5 = (bf16[128,512]{1,0:T(8,128)(2,1)S(1)}, bf16[128,512]{1,0:T(8,128)(2,1)S(1)}, u32[]{:S(2)}, u32[]{:S(2)}) collective-permute-start(bf16[128,512]{1,0:T(8,128)(2,1)S(1)} %get-tuple-element.53), channel_id=1, source_target_pairs={{0,2},{2,0},{1,3},{3,1},{4,6},{6,4},{5,7},{7,5},{8,10},{10,8},{9,1... | collective-permute-start | bytes 393224 | tf_op jit(solution)/shard_map/ppermute | solution.py:52
  40.5 16.9 %collective-permute-start.6 = (bf16[128,512]{1,0:T(8,128)(2,1)S(1)}, bf16[128,512]{1,0:T(8,128)(2,1)S(1)}, u32[]{:S(2)}, u32[]{:S(2)}) collective-permute-start(bf16[128,512]{1,0:T(8,128)(2,1)S(1)} %get-tuple-element.54), channel_id=1, source_target_pairs={{0,4},{4,0},{1,5},{5,1},{2,6},{6,2},{3,7},{7,3},{8,12},{12,8},{9,1... | collective-permute-start | bytes 393224 | tf_op jit(solution)/shard_map/ppermute | solution.py:52
  42.1 15.3 %collective-permute-start.7 = (bf16[128,512]{1,0:T(8,128)(2,1)S(1)}, bf16[128,512]{1,0:T(8,128)(2,1)S(1)}, u32[]{:S(2)}, u32[]{:S(2)}) collective-permute-start(bf16[128,512]{1,0:T(8,128)(2,1)S(1)} %get-tuple-element.55), channel_id=1, source_target_pairs={{0,8},{8,0},{1,9},{9,1},{2,10},{10,2},{3,11},{11,3},{4,12},{12,4},... | collective-permute-start | bytes 393224 | tf_op jit(solution)/shard_map/ppermute | solution.py:52
  43.2 10.8 %collective-permute-start.14 = (bf16[64,512]{1,0:T(8,128)(2,1)S(1)}, bf16[64,512]{1,0:T(8,128)(2,1)S(1)}, u32[]{:S(2)}, u32[]{:S(2)}) collective-permute-start(bf16[64,512]{1,0:T(8,128)(2,1)S(1)} %get-tuple-element.69), channel_id=1, source_target_pairs={{0,8},{8,0},{1,9},{9,1},{2,10},{10,2},{3,11},{11,3},{4,12},{12,4},... | collective-permute-start | bytes 196616 | tf_op jit(solution)/shard_map/ppermute | solution.py:52
  54.0 5.6 %collective-permute-start.15 = (bf16[64,512]{1,0:T(8,128)(2,1)S(1)}, bf16[64,512]{1,0:T(8,128)(2,1)S(1)}, u32[]{:S(2)}, u32[]{:S(2)}) collective-permute-start(bf16[64,512]{1,0:T(8,128)(2,1)S(1)} %shard_map.158.refs_0_), channel_id=1, source_target_pairs={{0,16},{16,0},{1,17},{17,1},{2,18},{18,2},{3,19},{19,3},{4,20},{20... | collective-permute-start | bytes 196616 | tf_op jit(solution)/shard_map/ppermute | solution.py:52
  (2 other events, 29.8 us)

commit v3 on v2

v3 whole, which is shorter than its diff:
```python
import functools

import jax
import jax.numpy as jnp
from jax import lax
from jax.experimental import pallas as pl
from jax.experimental.pallas import tpu as pltpu
from jax.sharding import Mesh, PartitionSpec as P


LANES = 128
ROOM = 24 << 20
BF16 = jnp.bfloat16
F32 = jnp.float32
VMEM = pl.BlockSpec(memory_space=pltpu.VMEM)
SMEM = pl.BlockSpec(memory_space=pltpu.SMEM)


def dot(former, latter):
    return jnp.dot(former, latter, preferred_element_type=F32)


def dot_rows(former, latter):
    return lax.dot_general(former, latter, (((0,), (0,)), ((), ())), preferred_element_type=F32)


def dot_cols(former, latter):
    return lax.dot_general(former, latter, (((1,), (1,)), ((), ())), preferred_element_type=F32)


def near(array):
    return pltpu.with_memory_space_constraint(array, pltpu.VMEM)


def far(array):
    return pltpu.with_memory_space_constraint(array, pltpu.HBM)


def call(body, outs, ins, kept=True, scratch=()):
    fresh = pltpu.VMEM if kept else jax.ShapeDtypeStruct
    return pl.pallas_call(
        body,
        out_shape=[fresh(shape, kind) for shape, kind in outs],
        in_specs=ins,
        out_specs=[VMEM] * len(outs),
        scratch_shapes=scratch,
        compiler_params=pltpu.CompilerParams(vmem_limit_bytes=ROOM),
    )


def swap(array, axis):
    return lax.ppermute(array, axis, [(0, 1), (1, 0)])


def down_rows(row, count):
    return jnp.transpose(jnp.broadcast_to(row, (LANES, count)))


def onehot_cols(index_cols, first, blocks):
    lane = lax.broadcasted_iota(jnp.int32, index_cols.shape, 1)
    parts = [
        jnp.where(index_cols == lane + (first + LANES * block), 1.0, 0.0).astype(BF16)
        for block in range(blocks)
    ]
    return jnp.concatenate(parts, axis=1)


def onehot_rows(index_row, first, rows):
    node = lax.broadcasted_iota(jnp.int32, (rows, index_row.shape[1]), 0) + first
    return jnp.where(node == index_row, 1.0, 0.0).astype(BF16)


def receiver_row(recv_block, recv_node):
    edges = recv_node.shape[1]
    return jnp.concatenate(
        [
            recv_node[:, LANES * block : LANES * (block + 1)] + recv_block[block] * LANES
            for block in range(edges // LANES)
        ],
        axis=1,
    )


def pick_body(send_blocks, node_lat, *lent):
    for section, out in enumerate(lent):
        out[...] = node_lat[pl.ds(pl.multiple_of(send_blocks[section] * LANES, LANES), LANES), :]


def early_body(
    rounds, recv_block, edge_src, recv_node, node_lat, edge_lat, grad_edge, grad_agg, weight_edge,
    weight_recv, receiver_out, recv_out, send_out, hot_out, preact_out, grad_msg_out,
):
    nodes = node_lat.shape[0]
    edges = edge_lat.shape[0]
    row = receiver_row(recv_block, recv_node[...])
    receiver_out[...] = row
    receiver = down_rows(row, edges)
    sender = down_rows(edge_src[...], edges)
    hot_recv = onehot_cols(receiver, 0, nodes // LANES)
    recv_rows = dot(hot_recv, node_lat[...]).astype(BF16)
    recv_out[...] = recv_rows
    send_out[...] = dot(onehot_cols(sender, 0, nodes // LANES), node_lat[...]).astype(BF16)
    hot_out[...] = onehot_cols(sender, nodes, rounds)
    preact_out[...] = dot(edge_lat[...], weight_edge[...]) + dot(recv_rows, weight_recv[...])
    grad_msg_out[...] = grad_edge[...].astype(F32) + dot(hot_recv, grad_agg[...])


def main_body(
    rounds, send_own, hot, preact_own, grad_msg, weight_send, weight_out, *refs
):
    borrowed = refs[:rounds]
    send_out, hidden_out, grad_proj_out, grad_preact_out, message_out, table = refs[rounds:]
    edges = send_own.shape[0]
    for section in range(rounds):
        table[LANES * section : LANES * (section + 1), :] = borrowed[section][...]
    step = edges // 2
    for start in range(0, edges, step):
        rows = slice(start, start + step)
        send = (send_own[rows, :].astype(F32) + dot(hot[rows, :], table[...])).astype(BF16)
        send_out[rows, :] = send
        preact = preact_own[rows, :] + dot(send, weight_send[...])
        sigmoid = jax.nn.sigmoid(preact)
        hidden = (preact * sigmoid).astype(BF16)
        hidden_out[rows, :] = hidden
        slope = sigmoid * (1.0 + preact * (1.0 - sigmoid))
        projected = dot(hidden, weight_out[...])
        centered = projected - jnp.mean(projected, axis=1, keepdims=True)
        inv_std = lax.rsqrt(jnp.mean(centered * centered, axis=1, keepdims=True) + 1e-05)
        normed = centered * inv_std
        message_out[rows, :] = normed.astype(BF16)
        grad = grad_msg[rows, :]
        grad_proj = inv_std * (
            grad
            - jnp.mean(grad, axis=1, keepdims=True)
            - normed * jnp.mean(grad * normed, axis=1, keepdims=True)
        )
        grad_proj = grad_proj.astype(BF16)
        grad_proj_out[rows, :] = grad_proj
        grad_preact_out[rows, :] = (dot_cols(grad_proj, weight_out[...]) * slope).astype(BF16)


def place_of(split, dom_axes):
    domain = 0
    for axis in dom_axes:
        domain = domain * 2 + lax.axis_index(axis)
    return lax.axis_index(split[0]) if split else 0, domain


def pieces_of(plan, where, sums, side):
    part, own = where()
    for whiches, flip, domain in plan:
        owner = own ^ (domain | side)
        parts = [sums[which ^ (flip * part), owner] for which in whiches]
        yield parts[0] if len(parts) == 1 else jnp.concatenate(parts, axis=0)


def grads_body(plan, where, *refs):
    sums, give_out = refs[-2:]
    for which in range(sums.shape[0]):
        total = dot_rows(refs[2 * which][...], refs[2 * which + 1][...])
        sums[which] = total.reshape(sums.shape[1:])
    at = 0
    for piece in pieces_of(plan, where, sums, 1):
        give_out[at : at + piece.shape[0], :] = piece.astype(BF16)
        at += piece.shape[0]


def chip_body(plan, where, sums, got, keep_out, give_out):
    at = 0
    half = keep_out.shape[0]
    for piece in pieces_of(plan, where, sums, 0):
        rows = slice(at, at + piece.shape[0])
        target, first = (keep_out, at) if at < half else (give_out, at - half)
        total = piece + got[rows, :].astype(F32)
        target[first : first + piece.shape[0], :] = total.astype(target.dtype)
        at += piece.shape[0]


def sums_body(edge_src, receiver, grad_preact, own_out, recv_out, *back_out):
    nodes = own_out.shape[0]
    rounds = len(back_out)
    rows = grad_preact[...]
    slot_sums = dot(onehot_rows(edge_src[...], 0, nodes + rounds * LANES), rows)
    own_out[...] = slot_sums[:nodes]
    for section in range(rounds):
        first = nodes + LANES * section
        back_out[section][...] = slot_sums[first : first + LANES].astype(BF16)
    recv_out[...] = dot(onehot_rows(receiver[...], 0, nodes), rows)


def split_body(keep, got, keep_out, give_out):
    half = keep.shape[0] // 2
    for target, first in ((give_out, half), (keep_out, 0)):
        rows = slice(first, first + half)
        target[...] = (keep[rows, :] + got[rows, :].astype(F32)).astype(target.dtype)


def round_body(keep, got, out):
    out[...] = (keep[...] + got[...].astype(F32)).astype(BF16)


def finish_body(colours, where, *refs):
    *parts, out = refs
    own, _ = where()
    take = parts[0].shape[0]
    for index, part in enumerate(parts):
        flip, colour = divmod(index, colours)
        first = pl.multiple_of(((own ^ flip) * colours + colour) * take, take)
        out[pl.ds(first, take), :] = part[...].astype(F32)


def edge_body(receiver, grad_preact, message, grad_edge, weight_edge, agg_out, edge_out):
    agg_out[...] = dot(onehot_rows(receiver[...], 0, agg_out.shape[0]), message[...]).astype(BF16)
    edge_out[...] = (
        grad_edge[...].astype(F32) + dot_cols(grad_preact[...], weight_edge[...])
    ).astype(BF16)


def dot_cols_split(former, latter):
    high = former.astype(BF16)
    low = (former - high.astype(F32)).astype(BF16)
    return dot_cols(high, latter) + dot_cols(low, latter)


def node_body(send_blocks, own_sums, recv_sums, weight_send, weight_recv, *refs):
    returned, out, total = refs[:-2], refs[-2], refs[-1]
    for first in range(0, out.shape[0], LANES):
        rows = slice(first, first + LANES)
        summed = own_sums[rows, :]
        for section, block in enumerate(returned):
            mine = send_blocks[:, section : section + 1] == first // LANES
            summed = summed + jnp.where(mine, block[...].astype(F32), 0.0)
        total[rows, :] = summed
    out[...] = (
        dot_cols_split(total[...], weight_send[...])
        + dot_cols_split(recv_sums[...], weight_recv[...])
    ).astype(BF16)


def layout(share, parts, tops):
    colours = 2 if parts == 2 and tops and share >= 16 else 1
    per_part = 4 // parts
    orders = [(["part"] if parts == 2 else []) + list(range(1, tops + 1))]
    if colours == 2:
        orders.append([1, "part"] + list(range(2, tops + 1)))
    plans = []
    for order in orders:
        pieces = []
        for index in range(2 ** len(order)):
            domain, flip = 0, 0
            for level, bit in enumerate(order):
                on = index >> (len(order) - 1 - level) & 1
                if bit == "part":
                    flip = on
                else:
                    domain |= on << bit
            count = per_part // colours
            pieces.append((tuple(which ^ (flip * count) for which in range(count)), count, domain))
        plans.append(tuple(pieces))
    return plans, orders


def per_device(
    traj_axes, dom_axes, node_lat, edge_lat, grad_edge, grad_agg, weight_edge, weight_send,
    weight_recv, weight_out, edge_src, edge_recv_block, edge_recv_node, send_blocks,
):
    node_lat, edge_lat, grad_edge, grad_agg = node_lat[0], edge_lat[0], grad_edge[0], grad_agg[0]
    nodes, features = node_lat.shape
    edges = edge_lat.shape[0]
    rounds = send_blocks.shape[0]
    edge_src = edge_src.reshape(1, edges)
    recv_node = edge_recv_node.reshape(1, edges)
    bits = dom_axes[::-1]
    share = features // 2 ** len(bits)
    split = traj_axes[:1] if 2 * share >= 16 else ()
    plans, orders = layout(share, 1 + len(split), len(bits) - 1)
    colours = len(orders)
    half = 2 * features
    wide = ((edges, features), BF16)
    wide_sum = ((edges, features), F32)
    node_sum = ((nodes, features), F32)
    block = ((LANES, features), BF16)
    where = functools.partial(place_of, split, dom_axes)

    lent = call(pick_body, [block] * rounds, [SMEM, VMEM])(
        far(send_blocks), far(node_lat)
    )
    borrowed = [swap(lent[section], bits[section]) for section in range(rounds)]
    receiver, recv_rows, send_own, hot, preact_own, grad_msg = call(
        functools.partial(early_body, rounds),
        [((1, edges), jnp.int32), wide, wide, ((edges, rounds * LANES), BF16), wide_sum, wide_sum],
        [SMEM] + [VMEM] * 8,
    )(
        *map(far, (edge_recv_block, edge_src, recv_node, node_lat, edge_lat)),
        *map(far, (grad_edge, grad_agg, weight_edge, weight_recv)),
    )
    send_rows, hidden, grad_proj, grad_preact, message = call(
        functools.partial(main_body, rounds),
        [wide] * 5,
        [VMEM] * (6 + rounds),
        scratch=[pltpu.VMEM((rounds * LANES, features), BF16)],
    )(
        send_own, hot, preact_own, grad_msg, near(weight_send), near(weight_out),
        *map(near, borrowed),
    )

    factors = [
        (near(edge_lat), grad_preact), (send_rows, grad_preact), (recv_rows, grad_preact),
        (hidden, grad_proj),
    ]
    rows = half // colours
    flows = [None] * colours
    for colour in reversed(range(colours)):
        used = factors[colour::colours]
        sums, give = call(
            functools.partial(grads_body, plans[colour], where),
            [((len(used), 2 ** len(bits), share, features), F32), ((rows, features), BF16)],
            [VMEM] * (2 * len(used)),
        )(*sum(used, ()))
        flows[colour] = (sums, near(swap(give, bits[0])))

    own_sums, recv_sums, *back = call(
        sums_body, [node_sum, node_sum] + [block] * rounds, [VMEM] * 3
    )(near(edge_src), receiver, grad_preact)
    returned = [swap(back[section], bits[section]) for section in range(rounds)]

    def halves(rows):
        return [((rows, features), F32), ((rows, features), BF16)]

    for level in range(len(orders[0])):
        rows //= 2
        for colour, order in enumerate(orders):
            if level:
                fold = call(split_body, halves(rows), [VMEM] * 2)
            else:
                body = functools.partial(chip_body, plans[colour], where)
                fold = call(body, halves(rows), [VMEM] * 2)
            keep, give = fold(*flows[colour])
            axis = split[0] if order[level] == "part" else bits[order[level]]
            flows[colour] = (keep, near(swap(give, axis)))
    totals = []
    for flow in flows:
        (total,) = call(round_body, [((rows, features), BF16)], [VMEM] * 2)(*flow)
        for axis in traj_axes[len(split) :]:
            (total,) = call(round_body, [((rows, features), BF16)], [VMEM] * 2)(
                total, near(swap(total, axis))
            )
        totals.append(total)
    totals += [near(swap(total, axis)) for axis in split for total in totals]
    (weight_grads,) = call(
        functools.partial(finish_body, colours, where),
        [((4 * share, features), F32)],
        [VMEM] * len(totals),
        kept=False,
    )(*totals)
    agg, grad_edges = call(
        edge_body, [((nodes, features), BF16), wide], [VMEM] * 5, kept=False
    )(receiver, grad_preact, message, near(grad_edge), near(weight_edge))
    (grad_nodes,) = call(
        node_body,
        [((nodes, features), BF16)],
        [VMEM] * (5 + rounds),
        kept=False,
        scratch=[pltpu.VMEM((nodes, features), F32)],
    )(
        near(send_blocks.reshape(1, rounds)), own_sums, recv_sums, near(weight_send), near(weight_recv),
        *map(near, returned),
    )
    return agg[None], grad_edges[None], grad_nodes[None], weight_grads.reshape(4, share, features)


def solution(mesh):
    traj_axes = tuple(f"t{bit}" for bit in reversed(range(mesh.shape["traj"].bit_length() - 1)))
    dom_axes = tuple(f"d{bit}" for bit in reversed(range(mesh.shape["dom"].bit_length() - 1)))
    names = traj_axes + dom_axes
    bit_mesh = Mesh(mesh.devices.reshape((2,) * len(names)), names)
    rows = P(traj_axes, dom_axes, None)
    in_specs = (rows,) * 4 + (P(),) * 4 + (P(dom_axes),) * 4
    out_specs = (rows,) * 3 + (P(None, dom_axes, None),)

    def body(*arrays):
        return per_device(traj_axes, dom_axes, *arrays)

    return jax.shard_map(
        body, mesh=bit_mesh, in_specs=in_specs, out_specs=out_specs, check_vma=False
    )
```

time: 61 us -> 61.3 us (level)
  Pallas kernels: 15.4 us -> 12.9 us
  starting transfers between devices: 18.7 us -> 20.4 us
  waiting for transfers between devices: 25.8 us -> 26.7 us
    pallas_call x12 -> x18, Pallas kernels: 14.2 us -> 11.8 us  [the longest x1 2.95 us: per_device(): call(functools.partial(early_body, rounds), [((1, edges), jnp.int32), wid...]
    ppermute x16 -> x20, starting transfers between devices: 18.7 us -> 20.4 us  [swap(): return lax.ppermute(array, axis, [(0, 1), (1, 0)])]
    ppermute x16 -> x20, waiting for transfers between devices: 25.8 us -> 26.7 us  [swap(): return lax.ppermute(array, axis, [(0, 1), (1, 0)])]
  transfers between devices with their start and end apart: 16 -> 20, of which waited for: 8 -> 10; matrix products, arithmetic and copies ran while one was open for 0% -> 0% of each run, Pallas kernels for 14% -> 13%
where the time goes in v3:
time: 61.3 us; the launch traced here: 61.1 us
  waiting for transfers between devices  26.7 us (44%)
  starting transfers between devices  20.4 us (33%)
  Pallas kernels  12.9 us (21%)
  between operations  0.85 us (1%)
    ppermute x20, waiting for transfers between devices, swap(): return lax.ppermute(array, axis, [(0, 1), (1, 0)])  26.7 us
    ppermute x20, starting transfers between devices, swap(): return lax.ppermute(array, axis, [(0, 1), (1, 0)])  20.4 us
    pallas_call x1, Pallas kernels, per_device(): call(functools.partial(early_body, rounds), [((1, edges), jnp.int32), wid...  2.95 us
    pallas_call x1, Pallas kernels, per_device(): call(functools.partial(main_body, rounds), [wide] * 5, [VMEM] * (6 + roun...  2.51 us
    pallas_call x1, Pallas kernels, per_device(): call(node_body, [((nodes, features), BF16)], [VMEM] * (5 + rounds), kept=...  1.58 us
    pallas_call x2, Pallas kernels, per_device(): call(functools.partial(grads_body, plans[colour], where), [((len(used), 2...  1.57 us
    pallas_call x1, Pallas kernels, per_device(): call(edge_body, [((nodes, features), BF16), wide], [VMEM] * 5, kept=False)  1.37 us
  transfers between devices with their start and end apart: 20, of which 10 were waited for; matrix products, arithmetic and copies ran while one was open for 0% of the time, Pallas kernels for 13%

profile of v3, /device:TPU:0, one launch (start us, length us, event | category | flops | bytes accessed | tf_op | source)
XLA Modules:
  0.0 61.1 jit_solution(7958379769158166403)
XLA Ops:
  0.7 1.1 %shard_map.148 = (bf16[128,512]{1,0:T(8,128)(2,1)S(1)}, bf16[128,512]{1,0:T(8,128)(2,1)S(1)}, bf16[128,512]{1,0:T(8,128)(2,1)S(1)}, bf16[128,512]{1,0:T(8,128)(2,1)S(1)}) custom-call(s32[4]{0:T(128)} %send_blocks.1, bf16[256,512]{1,0:T(8,128)(2,1)} %bitcast.18), custom_call_target="tpu_custom_call" | custom-call | tf_op jit(solution)/shard_map/pallas_call | solution.py:285
  2.3 2.6 %collective-permute-start.1 = (bf16[128,512]{1,0:T(8,128)(2,1)S(1)}, bf16[128,512]{1,0:T(8,128)(2,1)S(1)}, u32[]{:S(2)}, u32[]{:S(2)}) collective-permute-start(bf16[128,512]{1,0:T(8,128)(2,1)S(1)} %get-tuple-element.53), channel_id=1, source_target_pairs={{0,2},{2,0},{1,3},{3,1},{4,6},{6,4},{5,7},{7,5},{8,10},{10,8},{9,1... | collective-permute-start | bytes 393224 | tf_op jit(solution)/shard_map/ppermute | solution.py:52
  4.9 1.6 %collective-permute-start.2 = (bf16[128,512]{1,0:T(8,128)(2,1)S(1)}, bf16[128,512]{1,0:T(8,128)(2,1)S(1)}, u32[]{:S(2)}, u32[]{:S(2)}) collective-permute-start(bf16[128,512]{1,0:T(8,128)(2,1)S(1)} %get-tuple-element.54), channel_id=1, source_target_pairs={{0,4},{4,0},{1,5},{5,1},{2,6},{6,2},{3,7},{7,3},{8,12},{12,8},{9,1... | collective-permute-start | bytes 393224 | tf_op jit(solution)/shard_map/ppermute | solution.py:52
  6.5 2.6 %collective-permute-start.3 = (bf16[128,512]{1,0:T(8,128)(2,1)S(1)}, bf16[128,512]{1,0:T(8,128)(2,1)S(1)}, u32[]{:S(2)}, u32[]{:S(2)}) collective-permute-start(bf16[128,512]{1,0:T(8,128)(2,1)S(1)} %get-tuple-element.55), channel_id=1, source_target_pairs={{0,8},{8,0},{1,9},{9,1},{2,10},{10,2},{3,11},{11,3},{4,12},{12,4},... | collective-permute-start | bytes 393224 | tf_op jit(solution)/shard_map/ppermute | solution.py:52
  9.1 3.0 %shard_map.147 = (s32[1,512]{1,0:T(1,128)S(1)}, bf16[512,512]{1,0:T(8,128)(2,1)S(1)}, bf16[512,512]{1,0:T(8,128)(2,1)S(1)}, bf16[512,512]{1,0:T(8,128)(2,1)S(1)}...) custom-call(s32[4]{0:T(128)} %recv_block.1, s32[1,512]{1,0:T(1,128)} %bitcast.15, s32[1,512]{1,0:T(1,128)} %bitcast.23, ...), custom_call_target="tpu_custom_call" | custom-call | tf_op jit(solution)/shard_map/pallas_call | solution.py:289
  12.0 0.7 %collective-permute-done.2.refs_2_ = bf16[128,512]{1,0:T(8,128)(2,1)S(1)} collective-permute-done((bf16[128,512]{1,0:T(8,128)(2,1)S(1)}, bf16[128,512]{1,0:T(8,128)(2,1)S(1)}, u32[]{:S(2)}, u32[]{:S(2)}) %collective-permute-start.2) | collective-permute-done | bytes 131104 | tf_op jit(solution)/shard_map/ppermute | solution.py:52
  12.8 2.7 %collective-permute-done.3.refs_3_ = bf16[128,512]{1,0:T(8,128)(2,1)S(1)} collective-permute-done((bf16[128,512]{1,0:T(8,128)(2,1)S(1)}, bf16[128,512]{1,0:T(8,128)(2,1)S(1)}, u32[]{:S(2)}, u32[]{:S(2)}) %collective-permute-start.3) | collective-permute-done | bytes 131104 | tf_op jit(solution)/shard_map/ppermute | solution.py:52
  15.5 2.5 %shard_map.149 = (bf16[512,512]{1,0:T(8,128)(2,1)S(1)}, bf16[512,512]{1,0:T(8,128)(2,1)S(1)}, bf16[512,512]{1,0:T(8,128)(2,1)S(1)}, bf16[512,512]{1,0:T(8,128)(2,1)S(1)}, bf16[512,512]{1,0:T(8,128)(2,1)S(1)}) custom-call(bf16[512,512]{1,0:T(8,128)(2,1)S(1)} %get-tuple-element.48.send_own, bf16[512,512]{1,0:T(8,128)(2,1)S(1)} %get-tuple-element.49.hot, ...), custom_call_target="tpu_custom_call" | custom-call | tf_op jit(solution)/shard_map/pallas_call | solution.py:297
  18.0 0.8 %shard_map.159 = (f32[2,16,32,512]{3,2,1,0:T(8,128)S(1)}, bf16[512,512]{1,0:T(8,128)(2,1)S(1)}) custom-call(bf16[512,512]{1,0:T(8,128)(2,1)S(1)} %get-tuple-element.77.refs_0_, bf16[512,512]{1,0:T(8,128)(2,1)S(1)} %get-tuple-element.56.grad_preact.refs_1_.refs_3_, bf16[512,512]{1,0:T(8,128)(2,1)S(1)} %get-tuple-element.78.refs_2_, ...), custom_call_target="tpu_custom_call" | custom-call | tf_op jit(solution)/shard_map/pallas_call | solution.py:315
  19.1 0.8 %shard_map.153 = (f32[2,16,32,512]{3,2,1,0:T(8,128)S(1)}, bf16[512,512]{1,0:T(8,128)(2,1)S(1)}) custom-call(bf16[512,512]{1,0:T(8,128)(2,1)S(1)} %bitcast.14, bf16[512,512]{1,0:T(8,128)(2,1)S(1)} %get-tuple-element.56.grad_preact.refs_1_.refs_3_, bf16[512,512]{1,0:T(8,128)(2,1)S(1)} %get-tuple-element.66.refs_2_, ...), custom_call_target="tpu_custom_call" | custom-call | tf_op jit(solution)/shard_map/pallas_call | solution.py:315
  22.0 1.6 %collective-permute-start.9 = (bf16[256,512]{1,0:T(8,128)(2,1)S(1)}, bf16[256,512]{1,0:T(8,128)(2,1)S(1)}, u32[]{:S(2)}, u32[]{:S(2)}) collective-permute-start(bf16[256,512]{1,0:T(8,128)(2,1)S(1)} %get-tuple-element.70), channel_id=1, source_target_pairs={{0,16},{16,0},{1,17},{17,1},{2,18},{18,2},{3,19},{19,3},{4,20},{20... | collective-permute-start | bytes 786440 | tf_op jit(solution)/shard_map/ppermute | solution.py:52
  23.5 5.8 %collective-permute-done.14.got = bf16[256,512]{1,0:T(8,128)(2,1)S(1)} collective-permute-done((bf16[256,512]{1,0:T(8,128)(2,1)S(1)}, bf16[256,512]{1,0:T(8,128)(2,1)S(1)}, u32[]{:S(2)}, u32[]{:S(2)}) %collective-permute-start.14) | collective-permute-done | bytes 262176 | tf_op jit(solution)/shard_map/ppermute | solution.py:52
  29.4 1.6 %collective-permute-start.15 = (bf16[128,512]{1,0:T(8,128)(2,1)S(1)}, bf16[128,512]{1,0:T(8,128)(2,1)S(1)}, u32[]{:S(2)}, u32[]{:S(2)}) collective-permute-start(bf16[128,512]{1,0:T(8,128)(2,1)S(1)} %get-tuple-element.85), channel_id=1, source_target_pairs={{0,16},{16,0},{1,17},{17,1},{2,18},{18,2},{3,19},{19,3},{4,20},{20... | collective-permute-start | bytes 393224 | tf_op jit(solution)/shard_map/ppermute | solution.py:52
  31.6 2.8 %collective-permute-done.15.got = bf16[128,512]{1,0:T(8,128)(2,1)S(1)} collective-permute-done((bf16[128,512]{1,0:T(8,128)(2,1)S(1)}, bf16[128,512]{1,0:T(8,128)(2,1)S(1)}, u32[]{:S(2)}, u32[]{:S(2)}) %collective-permute-start.15) | collective-permute-done | bytes 131104 | tf_op jit(solution)/shard_map/ppermute | solution.py:52
  35.0 1.1 %collective-permute-done.10.got = bf16[128,512]{1,0:T(8,128)(2,1)S(1)} collective-permute-done((bf16[128,512]{1,0:T(8,128)(2,1)S(1)}, bf16[128,512]{1,0:T(8,128)(2,1)S(1)}, u32[]{:S(2)}, u32[]{:S(2)}) %collective-permute-start.10) | collective-permute-done | bytes 131104 | tf_op jit(solution)/shard_map/ppermute | solution.py:52
  38.0 1.5 %collective-permute-start.6 = (bf16[128,512]{1,0:T(8,128)(2,1)S(1)}, bf16[128,512]{1,0:T(8,128)(2,1)S(1)}, u32[]{:S(2)}, u32[]{:S(2)}) collective-permute-start(bf16[128,512]{1,0:T(8,128)(2,1)S(1)} %get-tuple-element.64), channel_id=1, source_target_pairs={{0,4},{4,0},{1,5},{5,1},{2,6},{6,2},{3,7},{7,3},{8,12},{12,8},{9,1... | collective-permute-start | bytes 393224 | tf_op jit(solution)/shard_map/ppermute | solution.py:52
  39.5 1.5 %collective-permute-start.7 = (bf16[128,512]{1,0:T(8,128)(2,1)S(1)}, bf16[128,512]{1,0:T(8,128)(2,1)S(1)}, u32[]{:S(2)}, u32[]{:S(2)}) collective-permute-start(bf16[128,512]{1,0:T(8,128)(2,1)S(1)} %get-tuple-element.65), channel_id=1, source_target_pairs={{0,8},{8,0},{1,9},{9,1},{2,10},{10,2},{3,11},{11,3},{4,12},{12,4},... | collective-permute-start | bytes 393224 | tf_op jit(solution)/shard_map/ppermute | solution.py:52
  41.1 1.5 %collective-permute-start.17 = (bf16[32,512]{1,0:T(8,128)(2,1)S(1)}, bf16[32,512]{1,0:T(8,128)(2,1)S(1)}, u32[]{:S(2)}, u32[]{:S(2)}) collective-permute-start(bf16[32,512]{1,0:T(8,128)(2,1)S(1)} %get-tuple-element.89), channel_id=1, source_target_pairs={{0,8},{8,0},{1,9},{9,1},{2,10},{10,2},{3,11},{11,3},{4,12},{12,4},... | collective-permute-start | bytes 98312 | tf_op jit(solution)/shard_map/ppermute | solution.py:52
  42.6 7.7 %collective-permute-done.17.got = bf16[32,512]{1,0:T(8,128)(2,1)S(1)} collective-permute-done((bf16[32,512]{1,0:T(8,128)(2,1)S(1)}, bf16[32,512]{1,0:T(8,128)(2,1)S(1)}, u32[]{:S(2)}, u32[]{:S(2)}) %collective-permute-start.17) | collective-permute-done | bytes 32800 | tf_op jit(solution)/shard_map/ppermute | solution.py:52
  50.3 4.8 %collective-permute-done.12.got = bf16[32,512]{1,0:T(8,128)(2,1)S(1)} collective-permute-done((bf16[32,512]{1,0:T(8,128)(2,1)S(1)}, bf16[32,512]{1,0:T(8,128)(2,1)S(1)}, u32[]{:S(2)}, u32[]{:S(2)}) %collective-permute-start.12) | collective-permute-done | bytes 32800 | tf_op jit(solution)/shard_map/ppermute | solution.py:52
  55.1 1.3 %collective-permute-start.19 = (bf16[32,512]{1,0:T(8,128)(2,1)S(1)}, bf16[32,512]{1,0:T(8,128)(2,1)S(1)}, u32[]{:S(2)}, u32[]{:S(2)}) collective-permute-start(bf16[32,512]{1,0:T(8,128)(2,1)S(1)} %shard_map.164.refs_1_), channel_id=1, source_target_pairs={{0,16},{16,0},{1,17},{17,1},{2,18},{18,2},{3,19},{19,3},{4,20},{20... | collective-permute-start | bytes 98312 | tf_op jit(solution)/shard_map/ppermute | solution.py:52
  56.4 0.8 %collective-permute-start.18 = (bf16[32,512]{1,0:T(8,128)(2,1)S(1)}, bf16[32,512]{1,0:T(8,128)(2,1)S(1)}, u32[]{:S(2)}, u32[]{:S(2)}) collective-permute-start(bf16[32,512]{1,0:T(8,128)(2,1)S(1)} %shard_map.158.refs_0_), channel_id=1, source_target_pairs={{0,16},{16,0},{1,17},{17,1},{2,18},{18,2},{3,19},{19,3},{4,20},{20... | collective-permute-start | bytes 98312 | tf_op jit(solution)/shard_map/ppermute | solution.py:52
  57.2 1.4 %shard_map.150 = (bf16[256,512]{1,0:T(8,128)(2,1)}, bf16[512,512]{1,0:T(8,128)(2,1)}) custom-call(s32[1,512]{1,0:T(1,128)S(1)} %get-tuple-element.47.receiver, bf16[512,512]{1,0:T(8,128)(2,1)S(1)} %get-tuple-element.56.grad_preact.refs_1_.refs_3_, bf16[512,512]{1,0:T(8,128)(2,1)S(1)} %get-tuple-element.57.message, bf16[512,512]{1,0:T(8,128)(2,1)S(1)} %bitcast.12, ...), custom_call_target="tpu_custom_call" | custom-call | tf_op jit(solution)/shard_map/pallas_call | solution.py:356
  58.6 1.6 %shard_map.152 = bf16[256,512]{1,0:T(8,128)(2,1)} custom-call(s32[1,4]{1,0:T(1,128)S(1)} %bitcast.17, f32[256,512]{1,0:T(8,128)S(1)} %get-tuple-element.60.own_sums, f32[256,512]{1,0:T(8,128)S(1)} %get-tuple-element.61.recv_sums, bf16[512,512]{1,0:T(8,128)(2,1)S(1)} %copy-done.2, bf16[512,512]{1,0:T(8,128)(2,1)S(1)} %copy-done.4, ...), custom_call_target="tpu_custom_call" | custom-call | tf_op jit(solution)/shard_map/pallas_call | solution.py:359
  (51 shorter events, 7.1 us)
Async XLA Ops:
  1.7 10.3 %collective-permute-start = (bf16[128,512]{1,0:T(8,128)(2,1)S(1)}, bf16[128,512]{1,0:T(8,128)(2,1)S(1)}, u32[]{:S(2)}, u32[]{:S(2)}) collective-permute-start(bf16[128,512]{1,0:T(8,128)(2,1)S(1)} %get-tuple-element.52), channel_id=1, source_target_pairs={{0,1},{1,0},{2,3},{3,2},{4,5},{5,4},{6,7},{7,6},{8,9},{9,8},{10,11... | collective-permute-start | bytes 393224 | tf_op jit(solution)/shard_map/ppermute | solution.py:52
  2.3 9.7 %collective-permute-start.1 = (bf16[128,512]{1,0:T(8,128)(2,1)S(1)}, bf16[128,512]{1,0:T(8,128)(2,1)S(1)}, u32[]{:S(2)}, u32[]{:S(2)}) collective-permute-start(bf16[128,512]{1,0:T(8,128)(2,1)S(1)} %get-tuple-element.53), channel_id=1, source_target_pairs={{0,2},{2,0},{1,3},{3,1},{4,6},{6,4},{5,7},{7,5},{8,10},{10,8},{9,1... | collective-permute-start | bytes 393224 | tf_op jit(solution)/shard_map/ppermute | solution.py:52
  4.9 7.9 %collective-permute-start.2 = (bf16[128,512]{1,0:T(8,128)(2,1)S(1)}, bf16[128,512]{1,0:T(8,128)(2,1)S(1)}, u32[]{:S(2)}, u32[]{:S(2)}) collective-permute-start(bf16[128,512]{1,0:T(8,128)(2,1)S(1)} %get-tuple-element.54), channel_id=1, source_target_pairs={{0,4},{4,0},{1,5},{5,1},{2,6},{6,2},{3,7},{7,3},{8,12},{12,8},{9,1... | collective-permute-start | bytes 393224 | tf_op jit(solution)/shard_map/ppermute | solution.py:52
  6.5 9.0 %collective-permute-start.3 = (bf16[128,512]{1,0:T(8,128)(2,1)S(1)}, bf16[128,512]{1,0:T(8,128)(2,1)S(1)}, u32[]{:S(2)}, u32[]{:S(2)}) collective-permute-start(bf16[128,512]{1,0:T(8,128)(2,1)S(1)} %get-tuple-element.55), channel_id=1, source_target_pairs={{0,8},{8,0},{1,9},{9,1},{2,10},{10,2},{3,11},{11,3},{4,12},{12,4},... | collective-permute-start | bytes 393224 | tf_op jit(solution)/shard_map/ppermute | solution.py:52
  18.8 2.0 %collective-permute-start.13 = (bf16[512,512]{1,0:T(8,128)(2,1)S(1)}, bf16[512,512]{1,0:T(8,128)(2,1)S(1)}, u32[]{:S(2)}, u32[]{:S(2)}) collective-permute-start(bf16[512,512]{1,0:T(8,128)(2,1)S(1)} %get-tuple-element.81), channel_id=1, source_target_pairs={{0,1},{1,0},{2,3},{3,2},{4,5},{5,4},{6,7},{7,6},{8,9},{9,8},{10,11... | collective-permute-start | bytes 1572872 | tf_op jit(solution)/shard_map/ppermute | solution.py:52
  19.8 2.0 %collective-permute-start.8 = (bf16[512,512]{1,0:T(8,128)(2,1)S(1)}, bf16[512,512]{1,0:T(8,128)(2,1)S(1)}, u32[]{:S(2)}, u32[]{:S(2)}) collective-permute-start(bf16[512,512]{1,0:T(8,128)(2,1)S(1)} %get-tuple-element.68), channel_id=1, source_target_pairs={{0,1},{1,0},{2,3},{3,2},{4,5},{5,4},{6,7},{7,6},{8,9},{9,8},{10,11... | collective-permute-start | bytes 1572872 | tf_op jit(solution)/shard_map/ppermute | solution.py:52
  20.9 8.4 %collective-permute-start.14 = (bf16[256,512]{1,0:T(8,128)(2,1)S(1)}, bf16[256,512]{1,0:T(8,128)(2,1)S(1)}, u32[]{:S(2)}, u32[]{:S(2)}) collective-permute-start(bf16[256,512]{1,0:T(8,128)(2,1)S(1)} %get-tuple-element.83), channel_id=1, source_target_pairs={{0,2},{2,0},{1,3},{3,1},{4,6},{6,4},{5,7},{7,5},{8,10},{10,8},{9,1... | collective-permute-start | bytes 786440 | tf_op jit(solution)/shard_map/ppermute | solution.py:52
  21.9 35.2 %copy-start = (bf16[1,512,512]{2,1,0:T(8,128)(2,1)S(1)}, bf16[1,512,512]{2,1,0:T(8,128)(2,1)}, u32[]{:S(2)}) copy-start(bf16[1,512,512]{2,1,0:T(8,128)(2,1)} %param.14) | copy-start | bytes 1572868
  22.0 35.2 %copy-start.1 = (bf16[512,512]{1,0:T(8,128)(2,1)S(1)}, bf16[512,512]{1,0:T(8,128)(2,1)}, u32[]{:S(2)}) copy-start(bf16[512,512]{1,0:T(8,128)(2,1)} %weight_edge.3) | copy-start | bytes 1572868
  22.0 9.0 %collective-permute-start.9 = (bf16[256,512]{1,0:T(8,128)(2,1)S(1)}, bf16[256,512]{1,0:T(8,128)(2,1)S(1)}, u32[]{:S(2)}, u32[]{:S(2)}) collective-permute-start(bf16[256,512]{1,0:T(8,128)(2,1)S(1)} %get-tuple-element.70), channel_id=1, source_target_pairs={{0,16},{16,0},{1,17},{17,1},{2,18},{18,2},{3,19},{19,3},{4,20},{20... | collective-permute-start | bytes 786440 | tf_op jit(solution)/shard_map/ppermute | solution.py:52
  29.4 5.0 %collective-permute-start.15 = (bf16[128,512]{1,0:T(8,128)(2,1)S(1)}, bf16[128,512]{1,0:T(8,128)(2,1)S(1)}, u32[]{:S(2)}, u32[]{:S(2)}) collective-permute-start(bf16[128,512]{1,0:T(8,128)(2,1)S(1)} %get-tuple-element.85), channel_id=1, source_target_pairs={{0,16},{16,0},{1,17},{17,1},{2,18},{18,2},{3,19},{19,3},{4,20},{20... | collective-permute-start | bytes 393224 | tf_op jit(solution)/shard_map/ppermute | solution.py:52
  31.0 27.6 %copy-start.4 = (bf16[512,512]{1,0:T(8,128)(2,1)S(1)}, bf16[512,512]{1,0:T(8,128)(2,1)}, u32[]{:S(2)}) copy-start(bf16[512,512]{1,0:T(8,128)(2,1)} %weight_recv.3) | copy-start | bytes 1572868
  31.0 27.6 %copy-start.7 = (s32[4]{0:T(128)S(1)}, s32[4]{0:T(128)}, u32[]{:S(2)}) copy-start(s32[4]{0:T(128)} %send_blocks.1) | copy-start | bytes 52
  31.0 5.0 %collective-permute-start.10 = (bf16[128,512]{1,0:T(8,128)(2,1)S(1)}, bf16[128,512]{1,0:T(8,128)(2,1)S(1)}, u32[]{:S(2)}, u32[]{:S(2)}) collective-permute-start(bf16[128,512]{1,0:T(8,128)(2,1)S(1)} %get-tuple-element.72), channel_id=1, source_target_pairs={{0,2},{2,0},{1,3},{3,1},{4,6},{6,4},{5,7},{7,5},{8,10},{10,8},{9,1... | collective-permute-start | bytes 393224 | tf_op jit(solution)/shard_map/ppermute | solution.py:52
  34.4 5.1 %collective-permute-start.16 = (bf16[64,512]{1,0:T(8,128)(2,1)S(1)}, bf16[64,512]{1,0:T(8,128)(2,1)S(1)}, u32[]{:S(2)}, u32[]{:S(2)}) collective-permute-start(bf16[64,512]{1,0:T(8,128)(2,1)S(1)} %get-tuple-element.87), channel_id=1, source_target_pairs={{0,4},{4,0},{1,5},{5,1},{2,6},{6,2},{3,7},{7,3},{8,12},{12,8},{9,1... | collective-permute-start | bytes 196616 | tf_op jit(solution)/shard_map/ppermute | solution.py:52
  36.1 5.0 %collective-permute-start.11 = (bf16[64,512]{1,0:T(8,128)(2,1)S(1)}, bf16[64,512]{1,0:T(8,128)(2,1)S(1)}, u32[]{:S(2)}, u32[]{:S(2)}) collective-permute-start(bf16[64,512]{1,0:T(8,128)(2,1)S(1)} %get-tuple-element.74), channel_id=1, source_target_pairs={{0,4},{4,0},{1,5},{5,1},{2,6},{6,2},{3,7},{7,3},{8,12},{12,8},{9,1... | collective-permute-start | bytes 196616 | tf_op jit(solution)/shard_map/ppermute | solution.py:52
  37.3 19.1 %collective-permute-start.4 = (bf16[128,512]{1,0:T(8,128)(2,1)S(1)}, bf16[128,512]{1,0:T(8,128)(2,1)S(1)}, u32[]{:S(2)}, u32[]{:S(2)}) collective-permute-start(bf16[128,512]{1,0:T(8,128)(2,1)S(1)} %get-tuple-element.62), channel_id=1, source_target_pairs={{0,1},{1,0},{2,3},{3,2},{4,5},{5,4},{6,7},{7,6},{8,9},{9,8},{10,11... | collective-permute-start | bytes 393224 | tf_op jit(solution)/shard_map/ppermute | solution.py:52
  37.4 21.1 %collective-permute-start.5 = (bf16[128,512]{1,0:T(8,128)(2,1)S(1)}, bf16[128,512]{1,0:T(8,128)(2,1)S(1)}, u32[]{:S(2)}, u32[]{:S(2)}) collective-permute-start(bf16[128,512]{1,0:T(8,128)(2,1)S(1)} %get-tuple-element.63), channel_id=1, source_target_pairs={{0,2},{2,0},{1,3},{3,1},{4,6},{6,4},{5,7},{7,5},{8,10},{10,8},{9,1... | collective-permute-start | bytes 393224 | tf_op jit(solution)/shard_map/ppermute | solution.py:52
  38.0 20.5 %collective-permute-start.6 = (bf16[128,512]{1,0:T(8,128)(2,1)S(1)}, bf16[128,512]{1,0:T(8,128)(2,1)S(1)}, u32[]{:S(2)}, u32[]{:S(2)}) collective-permute-start(bf16[128,512]{1,0:T(8,128)(2,1)S(1)} %get-tuple-element.64), channel_id=1, source_target_pairs={{0,4},{4,0},{1,5},{5,1},{2,6},{6,2},{3,7},{7,3},{8,12},{12,8},{9,1... | collective-permute-start | bytes 393224 | tf_op jit(solution)/shard_map/ppermute | solution.py:52
  39.5 19.0 %collective-permute-start.7 = (bf16[128,512]{1,0:T(8,128)(2,1)S(1)}, bf16[128,512]{1,0:T(8,128)(2,1)S(1)}, u32[]{:S(2)}, u32[]{:S(2)}) collective-permute-start(bf16[128,512]{1,0:T(8,128)(2,1)S(1)} %get-tuple-element.65), channel_id=1, source_target_pairs={{0,8},{8,0},{1,9},{9,1},{2,10},{10,2},{3,11},{11,3},{4,12},{12,4},... | collective-permute-start | bytes 393224 | tf_op jit(solution)/shard_map/ppermute | solution.py:52
  41.1 9.2 %collective-permute-start.17 = (bf16[32,512]{1,0:T(8,128)(2,1)S(1)}, bf16[32,512]{1,0:T(8,128)(2,1)S(1)}, u32[]{:S(2)}, u32[]{:S(2)}) collective-permute-start(bf16[32,512]{1,0:T(8,128)(2,1)S(1)} %get-tuple-element.89), channel_id=1, source_target_pairs={{0,8},{8,0},{1,9},{9,1},{2,10},{10,2},{3,11},{11,3},{4,12},{12,4},... | collective-permute-start | bytes 98312 | tf_op jit(solution)/shard_map/ppermute | solution.py:52
  50.2 4.8 %collective-permute-start.12 = (bf16[32,512]{1,0:T(8,128)(2,1)S(1)}, bf16[32,512]{1,0:T(8,128)(2,1)S(1)}, u32[]{:S(2)}, u32[]{:S(2)}) collective-permute-start(bf16[32,512]{1,0:T(8,128)(2,1)S(1)} %get-tuple-element.76), channel_id=1, source_target_pairs={{0,8},{8,0},{1,9},{9,1},{2,10},{10,2},{3,11},{11,3},{4,12},{12,4},... | collective-permute-start | bytes 98312 | tf_op jit(solution)/shard_map/ppermute | solution.py:52
  55.1 5.1 %collective-permute-start.19 = (bf16[32,512]{1,0:T(8,128)(2,1)S(1)}, bf16[32,512]{1,0:T(8,128)(2,1)S(1)}, u32[]{:S(2)}, u32[]{:S(2)}) collective-permute-start(bf16[32,512]{1,0:T(8,128)(2,1)S(1)} %shard_map.164.refs_1_), channel_id=1, source_target_pairs={{0,16},{16,0},{1,17},{17,1},{2,18},{18,2},{3,19},{19,3},{4,20},{20... | collective-permute-start | bytes 98312 | tf_op jit(solution)/shard_map/ppermute | solution.py:52
  56.4 4.0 %collective-permute-start.18 = (bf16[32,512]{1,0:T(8,128)(2,1)S(1)}, bf16[32,512]{1,0:T(8,128)(2,1)S(1)}, u32[]{:S(2)}, u32[]{:S(2)}) collective-permute-start(bf16[32,512]{1,0:T(8,128)(2,1)S(1)} %shard_map.158.refs_0_), channel_id=1, source_target_pairs={{0,16},{16,0},{1,17},{17,1},{2,18},{18,2},{3,19},{19,3},{4,20},{20... | collective-permute-start | bytes 98312 | tf_op jit(solution)/shard_map/ppermute | solution.py:52
  (4 other events, 45.6 us)

commit v4 on v3

--- a/solution.py
+++ b/solution.py
@@ -87,13 +87,17 @@
 
 
 def early_body(
-    rounds, recv_block, edge_src, recv_node, node_lat, edge_lat, grad_edge, grad_agg, weight_edge,
-    weight_recv, receiver_out, recv_out, send_out, hot_out, preact_out, grad_msg_out,
+    rounds, recv_block, send_blocks, edge_src, recv_node, node_lat, edge_lat, grad_edge, grad_agg, weight_edge,
+    weight_recv, blocks_out, sender_out, receiver_out, edge_out, recv_out, send_out, hot_out,
+    preact_out, grad_msg_out,
 ):
     nodes = node_lat.shape[0]
     edges = edge_lat.shape[0]
     row = receiver_row(recv_block, recv_node[...])
     receiver_out[...] = row
+    blocks_out[...] = send_blocks[...]
+    sender_out[...] = edge_src[...]
+    edge_out[...] = edge_lat[...]
     receiver = down_rows(row, edges)
     sender = down_rows(edge_src[...], edges)
     hot_recv = onehot_cols(receiver, 0, nodes // LANES)
@@ -105,40 +109,6 @@
     grad_msg_out[...] = grad_edge[...].astype(F32) + dot(hot_recv, grad_agg[...])
 
 
-def main_body(
-    rounds, send_own, hot, preact_own, grad_msg, weight_send, weight_out, *refs
-):
-    borrowed = refs[:rounds]
-    send_out, hidden_out, grad_proj_out, grad_preact_out, message_out, table = refs[rounds:]
-    edges = send_own.shape[0]
-    for section in range(rounds):
-        table[LANES * section : LANES * (section + 1), :] = borrowed[section][...]
-    step = edges // 2
-    for start in range(0, edges, step):
-        rows = slice(start, start + step)
-        send = (send_own[rows, :].astype(F32) + dot(hot[rows, :], table[...])).astype(BF16)
-        send_out[rows, :] = send
-        preact = preact_own[rows, :] + dot(send, weight_send[...])
-        sigmoid = jax.nn.sigmoid(preact)
-        hidden = (preact * sigmoid).astype(BF16)
-        hidden_out[rows, :] = hidden
-        slope = sigmoid * (1.0 + preact * (1.0 - sigmoid))
-        projected = dot(hidden, weight_out[...])
-        centered = projected - jnp.mean(projected, axis=1, keepdims=True)
-        inv_std = lax.rsqrt(jnp.mean(centered * centered, axis=1, keepdims=True) + 1e-05)
-        normed = centered * inv_std
-        message_out[rows, :] = normed.astype(BF16)
-        grad = grad_msg[rows, :]
-        grad_proj = inv_std * (
-            grad
-            - jnp.mean(grad, axis=1, keepdims=True)
-            - normed * jnp.mean(grad * normed, axis=1, keepdims=True)
-        )
-        grad_proj = grad_proj.astype(BF16)
-        grad_proj_out[rows, :] = grad_proj
-        grad_preact_out[rows, :] = (dot_cols(grad_proj, weight_out[...]) * slope).astype(BF16)
-
-
 def place_of(split, dom_axes):
     domain = 0
     for axis in dom_axes:
@@ -146,34 +116,86 @@
     return lax.axis_index(split[0]) if split else 0, domain
 
 
-def pieces_of(plan, where, sums, side):
+def store_rows(target, at, blocks):
+    run = []
+    for block in blocks:
+        run.append(block)
+        rows = sum(part.shape[0] for part in run)
+        if rows % 16 == 0:
+            whole = run[0] if len(run) == 1 else jnp.concatenate(run, axis=0)
+            target[at : at + rows, :] = whole.astype(target.dtype)
+            at += rows
+            run = []
+
+
+def give_rows(domains, where, sums, give_out):
+    _, own = where()
+    store_rows(give_out, 0, [sums[own ^ (domain | 1)] for domain in domains])
+
+
+def main_body(
+    rounds, domains, where, send_own, hot, preact_own, grad_msg, weight_send, weight_out, *refs
+):
+    borrowed = refs[:rounds]
+    send_out, grad_preact_out, message_out, sums_out, give_out, table = refs[rounds:]
+    for section in range(rounds):
+        table[LANES * section : LANES * (section + 1), :] = borrowed[section][...]
+    send = (send_own[...].astype(F32) + dot(hot[...], table[...])).astype(BF16)
+    send_out[...] = send
+    preact = preact_own[...] + dot(send, weight_send[...])
+    sigmoid = jax.nn.sigmoid(preact)
+    hidden = (preact * sigmoid).astype(BF16)
+    slope = sigmoid * (1.0 + preact * (1.0 - sigmoid))
+    projected = dot(hidden, weight_out[...])
+    centered = projected - jnp.mean(projected, axis=1, keepdims=True)
+    inv_std = lax.rsqrt(jnp.mean(centered * centered, axis=1, keepdims=True) + 1e-05)
+    normed = centered * inv_std
+    message_out[...] = normed.astype(BF16)
+    grad = grad_msg[...]
+    grad_proj = inv_std * (
+        grad
+        - jnp.mean(grad, axis=1, keepdims=True)
+        - normed * jnp.mean(grad * normed, axis=1, keepdims=True)
+    )
+    grad_proj = grad_proj.astype(BF16)
+    grad_preact_out[...] = (dot_cols(grad_proj, weight_out[...]) * slope).astype(BF16)
+    sums_out[...] = dot_rows(hidden, grad_proj).reshape(sums_out.shape)
+    give_rows(domains, where, sums_out, give_out)
+
+
+def grads_body(domains, where, former, latter, sums_out, give_out):
+    sums_out[...] = dot_rows(former[...], latter[...]).reshape(sums_out.shape)
+    give_rows(domains, where, sums_out, give_out)
+
+
+def chip_body(plan, parts, where, *refs):
+    keep_out, give_out = refs[-2:]
+    sums, gots = refs[0:-2:2], refs[1:-2:2]
+    count = len(sums) // parts
     part, own = where()
-    for whiches, flip, domain in plan:
-        owner = own ^ (domain | side)
-        parts = [sums[which ^ (flip * part), owner] for which in whiches]
-        yield parts[0] if len(parts) == 1 else jnp.concatenate(parts, axis=0)
-
-
-def grads_body(plan, where, *refs):
-    sums, give_out = refs[-2:]
-    for which in range(sums.shape[0]):
-        total = dot_rows(refs[2 * which][...], refs[2 * which + 1][...])
-        sums[which] = total.reshape(sums.shape[1:])
-    at = 0
-    for piece in pieces_of(plan, where, sums, 1):
-        give_out[at : at + piece.shape[0], :] = piece.astype(BF16)
-        at += piece.shape[0]
-
-
-def chip_body(plan, where, sums, got, keep_out, give_out):
-    at = 0
-    half = keep_out.shape[0]
-    for piece in pieces_of(plan, where, sums, 0):
-        rows = slice(at, at + piece.shape[0])
-        target, first = (keep_out, at) if at < half else (give_out, at - half)
-        total = piece + got[rows, :].astype(F32)
-        target[first : first + piece.shape[0], :] = total.astype(target.dtype)
-        at += piece.shape[0]
+    half = len(plan) // 2
+
+    def add(which, index, domain):
+        share = sums[which].shape[1]
+        first = index * share
+        start = first // 16 * 16
+        got = gots[which][start : start + max(share, 16), :].astype(F32)
+        return sums[which][own ^ domain] + got[first - start : first - start + share]
+
+    for this in range(parts):
+
+        @pl.when(part == this)
+        def _():
+            for target, pieces in ((give_out, plan[half:]), (keep_out, plan[:half])):
+                store_rows(
+                    target,
+                    0,
+                    [
+                        add((this ^ flip) * count + which, index, domain)
+                        for flip, index, domain in pieces
+                        for which in range(count)
+                    ],
+                )
 
 
 def sums_body(edge_src, receiver, grad_preact, own_out, recv_out, *back_out):
@@ -239,10 +261,10 @@
 
 def layout(share, parts, tops):
     colours = 2 if parts == 2 and tops and share >= 16 else 1
-    per_part = 4 // parts
     orders = [(["part"] if parts == 2 else []) + list(range(1, tops + 1))]
     if colours == 2:
         orders.append([1, "part"] + list(range(2, tops + 1)))
+    domains = [index << 1 for index in range(2**tops)]
     plans = []
     for order in orders:
         pieces = []
@@ -254,10 +276,9 @@
                     flip = on
                 else:
                     domain |= on << bit
-            count = per_part // colours
-            pieces.append((tuple(which ^ (flip * count) for which in range(count)), count, domain))
-        plans.append(tuple(pieces))
-    return plans, orders
+            pieces.append((flip, domain >> 1, domain))
+        plans.append(pieces)
+    return plans, orders, domains
 
 
 def per_device(
@@ -273,7 +294,7 @@
     bits = dom_axes[::-1]
     share = features // 2 ** len(bits)
     split = traj_axes[:1] if 2 * share >= 16 else ()
-    plans, orders = layout(share, 1 + len(split), len(bits) - 1)
+    plans, orders, domains = layout(share, 1 + len(split), len(bits) - 1)
     colours = len(orders)
     half = 2 * features
     wide = ((edges, features), BF16)
@@ -286,42 +307,39 @@
         far(send_blocks), far(node_lat)
     )
     borrowed = [swap(lent[section], bits[section]) for section in range(rounds)]
-    receiver, recv_rows, send_own, hot, preact_own, grad_msg = call(
+    blocks, sender, receiver, edge_rows, recv_rows, send_own, hot, preact_own, grad_msg = call(
         functools.partial(early_body, rounds),
-        [((1, edges), jnp.int32), wide, wide, ((edges, rounds * LANES), BF16), wide_sum, wide_sum],
-        [SMEM] + [VMEM] * 8,
+        [((1, rounds), jnp.int32)] + [((1, edges), jnp.int32)] * 2 + [wide, wide, wide, ((edges, rounds * LANES), BF16), wide_sum, wide_sum],
+        [SMEM] + [VMEM] * 9,
     )(
-        *map(far, (edge_recv_block, edge_src, recv_node, node_lat, edge_lat)),
+        *map(far, (edge_recv_block, send_blocks.reshape(1, rounds), edge_src, recv_node)),
+        *map(far, (node_lat, edge_lat)),
         *map(far, (grad_edge, grad_agg, weight_edge, weight_recv)),
     )
-    send_rows, hidden, grad_proj, grad_preact, message = call(
-        functools.partial(main_body, rounds),
-        [wide] * 5,
+    sum_rows = [
+        ((2 ** len(bits), share, features), F32), ((share * len(domains), features), BF16)
+    ]
+    sums, gives = [None] * 4, [None] * 4
+    send_rows, grad_preact, message, sums[3], gives[3] = call(
+        functools.partial(main_body, rounds, domains, where),
+        [wide] * 3 + sum_rows,
         [VMEM] * (6 + rounds),
         scratch=[pltpu.VMEM((rounds * LANES, features), BF16)],
     )(
         send_own, hot, preact_own, grad_msg, near(weight_send), near(weight_out),
         *map(near, borrowed),
     )
-
-    factors = [
-        (near(edge_lat), grad_preact), (send_rows, grad_preact), (recv_rows, grad_preact),
-        (hidden, grad_proj),
-    ]
+    for which, rows in ((1, send_rows), (0, edge_rows), (2, recv_rows)):
+        sums[which], gives[which] = call(
+            functools.partial(grads_body, domains, where), sum_rows, [VMEM] * 2
+        )(rows, grad_preact)
+    gots = [near(swap(give, bits[0])) for give in gives]
+    flows = [sum(zip(sums[colour::colours], gots[colour::colours]), ()) for colour in range(colours)]
     rows = half // colours
-    flows = [None] * colours
-    for colour in reversed(range(colours)):
-        used = factors[colour::colours]
-        sums, give = call(
-            functools.partial(grads_body, plans[colour], where),
-            [((len(used), 2 ** len(bits), share, features), F32), ((rows, features), BF16)],
-            [VMEM] * (2 * len(used)),
-        )(*sum(used, ()))
-        flows[colour] = (sums, near(swap(give, bits[0])))
 
     own_sums, recv_sums, *back = call(
         sums_body, [node_sum, node_sum] + [block] * rounds, [VMEM] * 3
-    )(near(edge_src), receiver, grad_preact)
+    )(sender, receiver, grad_preact)
     returned = [swap(back[section], bits[section]) for section in range(rounds)]
 
     def halves(rows):
@@ -333,8 +351,8 @@
             if level:
                 fold = call(split_body, halves(rows), [VMEM] * 2)
             else:
-                body = functools.partial(chip_body, plans[colour], where)
-                fold = call(body, halves(rows), [VMEM] * 2)
+                body = functools.partial(chip_body, plans[colour], 1 + len(split), where)
+                fold = call(body, halves(rows), [VMEM] * len(flows[colour]))
             keep, give = fold(*flows[colour])
             axis = split[0] if order[level] == "part" else bits[order[level]]
             flows[colour] = (keep, near(swap(give, axis)))
@@ -342,16 +360,11 @@
     for flow in flows:
         (total,) = call(round_body, [((rows, features), BF16)], [VMEM] * 2)(*flow)
         for axis in traj_axes[len(split) :]:
-            (total,) = call(round_body, [((rows, features), BF16)], [VMEM] * 2)(
-                total, near(swap(total, axis))
-            )
+            (total,) = call(round_body, [((rows, features), BF16)], [VMEM] * 2)(total, near(swap(total, axis)))
         totals.append(total)
     totals += [near(swap(total, axis)) for axis in split for total in totals]
     (weight_grads,) = call(
-        functools.partial(finish_body, colours, where),
-        [((4 * share, features), F32)],
-        [VMEM] * len(totals),
-        kept=False,
+        functools.partial(finish_body, colours, where), [((4 * share, features), F32)], [VMEM] * len(totals), kept=False
     )(*totals)
     agg, grad_edges = call(
         edge_body, [((nodes, features), BF16), wide], [VMEM] * 5, kept=False
@@ -363,7 +376,7 @@
         kept=False,
         scratch=[pltpu.VMEM((nodes, features), F32)],
     )(
-        near(send_blocks.reshape(1, rounds)), own_sums, recv_sums, near(weight_send), near(weight_recv),
+        blocks, own_sums, recv_sums, near(weight_send), near(weight_recv),
         *map(near, returned),
     )
     return agg[None], grad_edges[None], grad_nodes[None], weight_grads.reshape(4, share, features)

time: 61.3 us -> 60.7 us (level)
  starting transfers between devices: 20.4 us -> 21.2 us
    ppermute x20 -> x22, starting transfers between devices: 20.4 us -> 21.2 us  [swap(): return lax.ppermute(array, axis, [(0, 1), (1, 0)])]
    ppermute x20 -> x22, waiting for transfers between devices: 26.7 us -> 26.2 us  [swap(): return lax.ppermute(array, axis, [(0, 1), (1, 0)])]
    pallas_call x4 -> x5, Pallas kernels: 7.03 us -> 6.69 us  [the longest x1 3.04 us: per_device(): call(functools.partial(early_body, rounds), [((1, rounds), jnp.int32)] +...]
  transfers between devices with their start and end apart: 20 -> 22, of which waited for: 10 -> 9; matrix products, arithmetic and copies ran while one was open for 0% -> 0% of each run, Pallas kernels for 13% -> 14%
where the time goes in v4:
time: 60.7 us; the launch traced here: 60.6 us
  waiting for transfers between devices  26.2 us (43%)
  starting transfers between devices  21.2 us (35%)
  Pallas kernels  12.4 us (20%)
  between operations  0.8 us (1%)
    ppermute x22, waiting for transfers between devices, swap(): return lax.ppermute(array, axis, [(0, 1), (1, 0)])  26.2 us
    ppermute x22, starting transfers between devices, swap(): return lax.ppermute(array, axis, [(0, 1), (1, 0)])  21.2 us
    pallas_call x1, Pallas kernels, per_device(): call(functools.partial(early_body, rounds), [((1, rounds), jnp.int32)] +...  3.04 us
    pallas_call x1, Pallas kernels, per_device(): call(functools.partial(main_body, rounds, domains, where), [wide] * 3 + s...  2.18 us
    pallas_call x1, Pallas kernels, per_device(): call(node_body, [((nodes, features), BF16)], [VMEM] * (5 + rounds), kept=...  1.59 us
    pallas_call x3, Pallas kernels, per_device(): call(functools.partial(grads_body, domains, where), sum_rows, [VMEM] * 2)  1.47 us
    pallas_call x1, Pallas kernels, per_device(): call(edge_body, [((nodes, features), BF16), wide], [VMEM] * 5, kept=False)  1.37 us
  transfers between devices with their start and end apart: 22, of which 9 were waited for; matrix products, arithmetic and copies ran while one was open for 0% of the time, Pallas kernels for 14%

profile of v4, /device:TPU:0, one launch (start us, length us, event | category | flops | bytes accessed | tf_op | source)
XLA Modules:
  0.0 60.6 jit_solution(2382625529118375760)
XLA Ops:
  0.6 1.0 %shard_map.148 = (bf16[128,512]{1,0:T(8,128)(2,1)S(1)}, bf16[128,512]{1,0:T(8,128)(2,1)S(1)}, bf16[128,512]{1,0:T(8,128)(2,1)S(1)}, bf16[128,512]{1,0:T(8,128)(2,1)S(1)}) custom-call(s32[4]{0:T(128)} %send_blocks.1, bf16[256,512]{1,0:T(8,128)(2,1)} %bitcast.13), custom_call_target="tpu_custom_call" | custom-call | tf_op jit(solution)/shard_map/pallas_call | solution.py:306
  2.2 2.6 %collective-permute-start.1 = (bf16[128,512]{1,0:T(8,128)(2,1)S(1)}, bf16[128,512]{1,0:T(8,128)(2,1)S(1)}, u32[]{:S(2)}, u32[]{:S(2)}) collective-permute-start(bf16[128,512]{1,0:T(8,128)(2,1)S(1)} %get-tuple-element.58), channel_id=1, source_target_pairs={{0,2},{2,0},{1,3},{3,1},{4,6},{6,4},{5,7},{7,5},{8,10},{10,8},{9,1... | collective-permute-start | bytes 393224 | tf_op jit(solution)/shard_map/ppermute | solution.py:52
  4.8 1.6 %collective-permute-start.2 = (bf16[128,512]{1,0:T(8,128)(2,1)S(1)}, bf16[128,512]{1,0:T(8,128)(2,1)S(1)}, u32[]{:S(2)}, u32[]{:S(2)}) collective-permute-start(bf16[128,512]{1,0:T(8,128)(2,1)S(1)} %get-tuple-element.59), channel_id=1, source_target_pairs={{0,4},{4,0},{1,5},{5,1},{2,6},{6,2},{3,7},{7,3},{8,12},{12,8},{9,1... | collective-permute-start | bytes 393224 | tf_op jit(solution)/shard_map/ppermute | solution.py:52
  6.4 2.6 %collective-permute-start.3 = (bf16[128,512]{1,0:T(8,128)(2,1)S(1)}, bf16[128,512]{1,0:T(8,128)(2,1)S(1)}, u32[]{:S(2)}, u32[]{:S(2)}) collective-permute-start(bf16[128,512]{1,0:T(8,128)(2,1)S(1)} %get-tuple-element.60), channel_id=1, source_target_pairs={{0,8},{8,0},{1,9},{9,1},{2,10},{10,2},{3,11},{11,3},{4,12},{12,4},... | collective-permute-start | bytes 393224 | tf_op jit(solution)/shard_map/ppermute | solution.py:52
  9.0 3.0 %shard_map.147 = (s32[1,4]{1,0:T(1,128)S(1)}, s32[1,512]{1,0:T(1,128)S(1)}, s32[1,512]{1,0:T(1,128)S(1)}, bf16[512,512]{1,0:T(8,128)(2,1)S(1)}, bf16[512,512]{1,...) custom-call(s32[4]{0:T(128)} %recv_block.1, ...), custom_call_target="tpu_custom_call" | custom-call | tf_op jit(solution)/shard_map/pallas_call | solution.py:310
  12.0 0.7 %collective-permute-done.2.refs_2_ = bf16[128,512]{1,0:T(8,128)(2,1)S(1)} collective-permute-done((bf16[128,512]{1,0:T(8,128)(2,1)S(1)}, bf16[128,512]{1,0:T(8,128)(2,1)S(1)}, u32[]{:S(2)}, u32[]{:S(2)}) %collective-permute-start.2) | collective-permute-done | bytes 131104 | tf_op jit(solution)/shard_map/ppermute | solution.py:52
  12.7 2.7 %collective-permute-done.3.refs_3_ = bf16[128,512]{1,0:T(8,128)(2,1)S(1)} collective-permute-done((bf16[128,512]{1,0:T(8,128)(2,1)S(1)}, bf16[128,512]{1,0:T(8,128)(2,1)S(1)}, u32[]{:S(2)}, u32[]{:S(2)}) %collective-permute-start.3) | collective-permute-done | bytes 131104 | tf_op jit(solution)/shard_map/ppermute | solution.py:52
  15.4 2.2 %shard_map.149 = (bf16[512,512]{1,0:T(8,128)(2,1)S(1)}, bf16[512,512]{1,0:T(8,128)(2,1)S(1)}, bf16[512,512]{1,0:T(8,128)(2,1)S(1)}, f32[16,32,512]{2,1,0:T(8,128)S(1)}, bf16[256,512]{1,0:T(8,128)(2,1)S(1)}) custom-call(bf16[512,512]{1,0:T(8,128)(2,1)S(1)} %get-tuple-element.53.send_own, bf16[512,512]{1,0:T(8,128)(2,1)S(1)} %get-tuple-element.54.hot, ...), custom_call_target="tpu_custom_call" | custom-call | tf_op jit(solution)/shard_map/pallas_call | solution.py:323
  21.6 1.6 %collective-permute-start.10 = (bf16[256,512]{1,0:T(8,128)(2,1)S(1)}, bf16[256,512]{1,0:T(8,128)(2,1)S(1)}, u32[]{:S(2)}, u32[]{:S(2)}) collective-permute-start(bf16[256,512]{1,0:T(8,128)(2,1)S(1)} %get-tuple-element.80), channel_id=1, source_target_pairs={{0,16},{16,0},{1,17},{17,1},{2,18},{18,2},{3,19},{19,3},{4,20},{20... | collective-permute-start | bytes 786440 | tf_op jit(solution)/shard_map/ppermute | solution.py:52
  23.2 5.6 %collective-permute-done.16.got = bf16[256,512]{1,0:T(8,128)(2,1)S(1)} collective-permute-done((bf16[256,512]{1,0:T(8,128)(2,1)S(1)}, bf16[256,512]{1,0:T(8,128)(2,1)S(1)}, u32[]{:S(2)}, u32[]{:S(2)}) %collective-permute-start.16) | collective-permute-done | bytes 262176 | tf_op jit(solution)/shard_map/ppermute | solution.py:52
  28.8 1.6 %collective-permute-start.17 = (bf16[128,512]{1,0:T(8,128)(2,1)S(1)}, bf16[128,512]{1,0:T(8,128)(2,1)S(1)}, u32[]{:S(2)}, u32[]{:S(2)}) collective-permute-start(bf16[128,512]{1,0:T(8,128)(2,1)S(1)} %get-tuple-element.95), channel_id=1, source_target_pairs={{0,16},{16,0},{1,17},{17,1},{2,18},{18,2},{3,19},{19,3},{4,20},{20... | collective-permute-start | bytes 393224 | tf_op jit(solution)/shard_map/ppermute | solution.py:52
  31.0 2.9 %collective-permute-done.17.got = bf16[128,512]{1,0:T(8,128)(2,1)S(1)} collective-permute-done((bf16[128,512]{1,0:T(8,128)(2,1)S(1)}, bf16[128,512]{1,0:T(8,128)(2,1)S(1)}, u32[]{:S(2)}, u32[]{:S(2)}) %collective-permute-start.17) | collective-permute-done | bytes 131104 | tf_op jit(solution)/shard_map/ppermute | solution.py:52
  34.4 1.1 %collective-permute-done.11.got = bf16[128,512]{1,0:T(8,128)(2,1)S(1)} collective-permute-done((bf16[128,512]{1,0:T(8,128)(2,1)S(1)}, bf16[128,512]{1,0:T(8,128)(2,1)S(1)}, u32[]{:S(2)}, u32[]{:S(2)}) %collective-permute-start.11) | collective-permute-done | bytes 131104 | tf_op jit(solution)/shard_map/ppermute | solution.py:52
  36.1 0.7 %shard_map.151 = (f32[256,512]{1,0:T(8,128)S(1)}, f32[256,512]{1,0:T(8,128)S(1)}, bf16[128,512]{1,0:T(8,128)(2,1)S(1)}, bf16[128,512]{1,0:T(8,128)(2,1)S(1)}, bf...) custom-call(s32[1,512]{1,0:T(1,128)S(1)} %get-tuple-element.66.edge_src, ...), custom_call_target="tpu_custom_call" | custom-call | tf_op jit(solution)/shard_map/pallas_call | solution.py:340
  37.4 1.5 %collective-permute-start.6 = (bf16[128,512]{1,0:T(8,128)(2,1)S(1)}, bf16[128,512]{1,0:T(8,128)(2,1)S(1)}, u32[]{:S(2)}, u32[]{:S(2)}) collective-permute-start(bf16[128,512]{1,0:T(8,128)(2,1)S(1)} %get-tuple-element.71), channel_id=1, source_target_pairs={{0,4},{4,0},{1,5},{5,1},{2,6},{6,2},{3,7},{7,3},{8,12},{12,8},{9,1... | collective-permute-start | bytes 393224 | tf_op jit(solution)/shard_map/ppermute | solution.py:52
  39.0 1.5 %collective-permute-start.7 = (bf16[128,512]{1,0:T(8,128)(2,1)S(1)}, bf16[128,512]{1,0:T(8,128)(2,1)S(1)}, u32[]{:S(2)}, u32[]{:S(2)}) collective-permute-start(bf16[128,512]{1,0:T(8,128)(2,1)S(1)} %get-tuple-element.72), channel_id=1, source_target_pairs={{0,8},{8,0},{1,9},{9,1},{2,10},{10,2},{3,11},{11,3},{4,12},{12,4},... | collective-permute-start | bytes 393224 | tf_op jit(solution)/shard_map/ppermute | solution.py:52
  40.5 1.5 %collective-permute-start.19 = (bf16[32,512]{1,0:T(8,128)(2,1)S(1)}, bf16[32,512]{1,0:T(8,128)(2,1)S(1)}, u32[]{:S(2)}, u32[]{:S(2)}) collective-permute-start(bf16[32,512]{1,0:T(8,128)(2,1)S(1)} %get-tuple-element.99), channel_id=1, source_target_pairs={{0,8},{8,0},{1,9},{9,1},{2,10},{10,2},{3,11},{11,3},{4,12},{12,4},... | collective-permute-start | bytes 98312 | tf_op jit(solution)/shard_map/ppermute | solution.py:52
  42.0 7.7 %collective-permute-done.19.got = bf16[32,512]{1,0:T(8,128)(2,1)S(1)} collective-permute-done((bf16[32,512]{1,0:T(8,128)(2,1)S(1)}, bf16[32,512]{1,0:T(8,128)(2,1)S(1)}, u32[]{:S(2)}, u32[]{:S(2)}) %collective-permute-start.19) | collective-permute-done | bytes 32800 | tf_op jit(solution)/shard_map/ppermute | solution.py:52
  49.7 4.8 %collective-permute-done.13.got = bf16[32,512]{1,0:T(8,128)(2,1)S(1)} collective-permute-done((bf16[32,512]{1,0:T(8,128)(2,1)S(1)}, bf16[32,512]{1,0:T(8,128)(2,1)S(1)}, u32[]{:S(2)}, u32[]{:S(2)}) %collective-permute-start.13) | collective-permute-done | bytes 32800 | tf_op jit(solution)/shard_map/ppermute | solution.py:52
  54.5 1.4 %collective-permute-start.21 = (bf16[32,512]{1,0:T(8,128)(2,1)S(1)}, bf16[32,512]{1,0:T(8,128)(2,1)S(1)}, u32[]{:S(2)}, u32[]{:S(2)}) collective-permute-start(bf16[32,512]{1,0:T(8,128)(2,1)S(1)} %shard_map.165.refs_1_), channel_id=1, source_target_pairs={{0,16},{16,0},{1,17},{17,1},{2,18},{18,2},{3,19},{19,3},{4,20},{20... | collective-permute-start | bytes 98312 | tf_op jit(solution)/shard_map/ppermute | solution.py:52
  55.9 0.7 %collective-permute-start.20 = (bf16[32,512]{1,0:T(8,128)(2,1)S(1)}, bf16[32,512]{1,0:T(8,128)(2,1)S(1)}, u32[]{:S(2)}, u32[]{:S(2)}) collective-permute-start(bf16[32,512]{1,0:T(8,128)(2,1)S(1)} %shard_map.159.refs_0_), channel_id=1, source_target_pairs={{0,16},{16,0},{1,17},{17,1},{2,18},{18,2},{3,19},{19,3},{4,20},{20... | collective-permute-start | bytes 98312 | tf_op jit(solution)/shard_map/ppermute | solution.py:52
  56.6 1.4 %shard_map.150 = (bf16[256,512]{1,0:T(8,128)(2,1)}, bf16[512,512]{1,0:T(8,128)(2,1)}) custom-call(s32[1,512]{1,0:T(1,128)S(1)} %get-tuple-element.52.receiver, bf16[512,512]{1,0:T(8,128)(2,1)S(1)} %get-tuple-element.61.grad_preact.latter, bf16[512,512]{1,0:T(8,128)(2,1)S(1)} %get-tuple-element.62.message, bf16[512,512]{1,0:T(8,128)(2,1)S(1)} %bitcast.12, ...), custom_call_target="tpu_custom_call" | custom-call | tf_op jit(solution)/shard_map/pallas_call | solution.py:369
  58.0 1.6 %shard_map.152 = bf16[256,512]{1,0:T(8,128)(2,1)} custom-call(s32[1,4]{1,0:T(1,128)S(1)} %get-tuple-element.65.send_blocks, f32[256,512]{1,0:T(8,128)S(1)} %get-tuple-element.67.own_sums, f32[256,512]{1,0:T(8,128)S(1)} %get-tuple-element.68.recv_sums, bf16[512,512]{1,0:T(8,128)(2,1)S(1)} %copy-done.3, bf16[512,512]{1,0:T(8,128)(2,1)S(1)} %copy-done.2, ...), custom_call_target="tpu_custom_call" | custom-call | tf_op jit(solution)/shard_map/pallas_call | solution.py:372
  59.8 0.7 %shard_map.166 = f32[128,512]{1,0:T(8,128)} custom-call(bf16[32,512]{1,0:T(8,128)(2,1)S(1)} %shard_map.159.refs_0_, bf16[32,512]{1,0:T(8,128)(2,1)S(1)} %shard_map.165.refs_1_, bf16[32,512]{1,0:T(8,128)(2,1)S(1)} %collective-permute-done.20.refs_2_, bf16[32,512]{1,0:T(8,128)(2,1)S(1)} %collective-permute-done.21.refs_3_), custom_call_target="tpu_custom_call" | custom-call | tf_op jit(solution)/shard_map/pallas_call | solution.py:366
  (50 shorter events, 7.3 us)
Async XLA Ops:
  1.6 10.4 %collective-permute-start = (bf16[128,512]{1,0:T(8,128)(2,1)S(1)}, bf16[128,512]{1,0:T(8,128)(2,1)S(1)}, u32[]{:S(2)}, u32[]{:S(2)}) collective-permute-start(bf16[128,512]{1,0:T(8,128)(2,1)S(1)} %get-tuple-element.57), channel_id=1, source_target_pairs={{0,1},{1,0},{2,3},{3,2},{4,5},{5,4},{6,7},{7,6},{8,9},{9,8},{10,11... | collective-permute-start | bytes 393224 | tf_op jit(solution)/shard_map/ppermute | solution.py:52
  2.2 9.8 %collective-permute-start.1 = (bf16[128,512]{1,0:T(8,128)(2,1)S(1)}, bf16[128,512]{1,0:T(8,128)(2,1)S(1)}, u32[]{:S(2)}, u32[]{:S(2)}) collective-permute-start(bf16[128,512]{1,0:T(8,128)(2,1)S(1)} %get-tuple-element.58), channel_id=1, source_target_pairs={{0,2},{2,0},{1,3},{3,1},{4,6},{6,4},{5,7},{7,5},{8,10},{10,8},{9,1... | collective-permute-start | bytes 393224 | tf_op jit(solution)/shard_map/ppermute | solution.py:52
  4.8 7.9 %collective-permute-start.2 = (bf16[128,512]{1,0:T(8,128)(2,1)S(1)}, bf16[128,512]{1,0:T(8,128)(2,1)S(1)}, u32[]{:S(2)}, u32[]{:S(2)}) collective-permute-start(bf16[128,512]{1,0:T(8,128)(2,1)S(1)} %get-tuple-element.59), channel_id=1, source_target_pairs={{0,4},{4,0},{1,5},{5,1},{2,6},{6,2},{3,7},{7,3},{8,12},{12,8},{9,1... | collective-permute-start | bytes 393224 | tf_op jit(solution)/shard_map/ppermute | solution.py:52
  6.4 9.0 %collective-permute-start.3 = (bf16[128,512]{1,0:T(8,128)(2,1)S(1)}, bf16[128,512]{1,0:T(8,128)(2,1)S(1)}, u32[]{:S(2)}, u32[]{:S(2)}) collective-permute-start(bf16[128,512]{1,0:T(8,128)(2,1)S(1)} %get-tuple-element.60), channel_id=1, source_target_pairs={{0,8},{8,0},{1,9},{9,1},{2,10},{10,2},{3,11},{11,3},{4,12},{12,4},... | collective-permute-start | bytes 393224 | tf_op jit(solution)/shard_map/ppermute | solution.py:52
  17.6 2.8 %collective-permute-start.15 = (bf16[256,512]{1,0:T(8,128)(2,1)S(1)}, bf16[256,512]{1,0:T(8,128)(2,1)S(1)}, u32[]{:S(2)}, u32[]{:S(2)}) collective-permute-start(bf16[256,512]{1,0:T(8,128)(2,1)S(1)} %get-tuple-element.91), channel_id=1, source_target_pairs={{0,1},{1,0},{2,3},{3,2},{4,5},{5,4},{6,7},{7,6},{8,9},{9,8},{10,11... | collective-permute-start | bytes 786440 | tf_op jit(solution)/shard_map/ppermute | solution.py:52
  18.2 2.2 %collective-permute-start.14 = (bf16[256,512]{1,0:T(8,128)(2,1)S(1)}, bf16[256,512]{1,0:T(8,128)(2,1)S(1)}, u32[]{:S(2)}, u32[]{:S(2)}) collective-permute-start(bf16[256,512]{1,0:T(8,128)(2,1)S(1)} %get-tuple-element.89), channel_id=1, source_target_pairs={{0,1},{1,0},{2,3},{3,2},{4,5},{5,4},{6,7},{7,6},{8,9},{9,8},{10,11... | collective-permute-start | bytes 786440 | tf_op jit(solution)/shard_map/ppermute | solution.py:52
  19.2 1.8 %collective-permute-start.9 = (bf16[256,512]{1,0:T(8,128)(2,1)S(1)}, bf16[256,512]{1,0:T(8,128)(2,1)S(1)}, u32[]{:S(2)}, u32[]{:S(2)}) collective-permute-start(bf16[256,512]{1,0:T(8,128)(2,1)S(1)} %get-tuple-element.78), channel_id=1, source_target_pairs={{0,1},{1,0},{2,3},{3,2},{4,5},{5,4},{6,7},{7,6},{8,9},{9,8},{10,11... | collective-permute-start | bytes 786440 | tf_op jit(solution)/shard_map/ppermute | solution.py:52
  19.8 1.7 %collective-permute-start.8 = (bf16[256,512]{1,0:T(8,128)(2,1)S(1)}, bf16[256,512]{1,0:T(8,128)(2,1)S(1)}, u32[]{:S(2)}, u32[]{:S(2)}) collective-permute-start(bf16[256,512]{1,0:T(8,128)(2,1)S(1)} %get-tuple-element.75), channel_id=1, source_target_pairs={{0,1},{1,0},{2,3},{3,2},{4,5},{5,4},{6,7},{7,6},{8,9},{9,8},{10,11... | collective-permute-start | bytes 786440 | tf_op jit(solution)/shard_map/ppermute | solution.py:52
  20.5 8.3 %collective-permute-start.16 = (bf16[256,512]{1,0:T(8,128)(2,1)S(1)}, bf16[256,512]{1,0:T(8,128)(2,1)S(1)}, u32[]{:S(2)}, u32[]{:S(2)}) collective-permute-start(bf16[256,512]{1,0:T(8,128)(2,1)S(1)} %get-tuple-element.93), channel_id=1, source_target_pairs={{0,2},{2,0},{1,3},{3,1},{4,6},{6,4},{5,7},{7,5},{8,10},{10,8},{9,1... | collective-permute-start | bytes 786440 | tf_op jit(solution)/shard_map/ppermute | solution.py:52
  21.6 8.8 %collective-permute-start.10 = (bf16[256,512]{1,0:T(8,128)(2,1)S(1)}, bf16[256,512]{1,0:T(8,128)(2,1)S(1)}, u32[]{:S(2)}, u32[]{:S(2)}) collective-permute-start(bf16[256,512]{1,0:T(8,128)(2,1)S(1)} %get-tuple-element.80), channel_id=1, source_target_pairs={{0,16},{16,0},{1,17},{17,1},{2,18},{18,2},{3,19},{19,3},{4,20},{20... | collective-permute-start | bytes 786440 | tf_op jit(solution)/shard_map/ppermute | solution.py:52
  28.8 5.0 %collective-permute-start.17 = (bf16[128,512]{1,0:T(8,128)(2,1)S(1)}, bf16[128,512]{1,0:T(8,128)(2,1)S(1)}, u32[]{:S(2)}, u32[]{:S(2)}) collective-permute-start(bf16[128,512]{1,0:T(8,128)(2,1)S(1)} %get-tuple-element.95), channel_id=1, source_target_pairs={{0,16},{16,0},{1,17},{17,1},{2,18},{18,2},{3,19},{19,3},{4,20},{20... | collective-permute-start | bytes 393224 | tf_op jit(solution)/shard_map/ppermute | solution.py:52
  30.4 5.0 %collective-permute-start.11 = (bf16[128,512]{1,0:T(8,128)(2,1)S(1)}, bf16[128,512]{1,0:T(8,128)(2,1)S(1)}, u32[]{:S(2)}, u32[]{:S(2)}) collective-permute-start(bf16[128,512]{1,0:T(8,128)(2,1)S(1)} %get-tuple-element.82), channel_id=1, source_target_pairs={{0,2},{2,0},{1,3},{3,1},{4,6},{6,4},{5,7},{7,5},{8,10},{10,8},{9,1... | collective-permute-start | bytes 393224 | tf_op jit(solution)/shard_map/ppermute | solution.py:52
  33.9 5.1 %collective-permute-start.18 = (bf16[64,512]{1,0:T(8,128)(2,1)S(1)}, bf16[64,512]{1,0:T(8,128)(2,1)S(1)}, u32[]{:S(2)}, u32[]{:S(2)}) collective-permute-start(bf16[64,512]{1,0:T(8,128)(2,1)S(1)} %get-tuple-element.97), channel_id=1, source_target_pairs={{0,4},{4,0},{1,5},{5,1},{2,6},{6,2},{3,7},{7,3},{8,12},{12,8},{9,1... | collective-permute-start | bytes 196616 | tf_op jit(solution)/shard_map/ppermute | solution.py:52
  35.5 5.0 %collective-permute-start.12 = (bf16[64,512]{1,0:T(8,128)(2,1)S(1)}, bf16[64,512]{1,0:T(8,128)(2,1)S(1)}, u32[]{:S(2)}, u32[]{:S(2)}) collective-permute-start(bf16[64,512]{1,0:T(8,128)(2,1)S(1)} %get-tuple-element.84), channel_id=1, source_target_pairs={{0,4},{4,0},{1,5},{5,1},{2,6},{6,2},{3,7},{7,3},{8,12},{12,8},{9,1... | collective-permute-start | bytes 196616 | tf_op jit(solution)/shard_map/ppermute | solution.py:52
  36.1 20.5 %copy-start = (bf16[1,512,512]{2,1,0:T(8,128)(2,1)S(1)}, bf16[1,512,512]{2,1,0:T(8,128)(2,1)}, u32[]{:S(2)}) copy-start(bf16[1,512,512]{2,1,0:T(8,128)(2,1)} %param.14) | copy-start | bytes 1572868
  36.1 20.5 %copy-start.1 = (bf16[512,512]{1,0:T(8,128)(2,1)S(1)}, bf16[512,512]{1,0:T(8,128)(2,1)}, u32[]{:S(2)}) copy-start(bf16[512,512]{1,0:T(8,128)(2,1)} %weight_edge.3) | copy-start | bytes 1572868
  36.8 19.1 %collective-permute-start.4 = (bf16[128,512]{1,0:T(8,128)(2,1)S(1)}, bf16[128,512]{1,0:T(8,128)(2,1)S(1)}, u32[]{:S(2)}, u32[]{:S(2)}) collective-permute-start(bf16[128,512]{1,0:T(8,128)(2,1)S(1)} %get-tuple-element.69), channel_id=1, source_target_pairs={{0,1},{1,0},{2,3},{3,2},{4,5},{5,4},{6,7},{7,6},{8,9},{9,8},{10,11... | collective-permute-start | bytes 393224 | tf_op jit(solution)/shard_map/ppermute | solution.py:52
  36.9 21.1 %collective-permute-start.5 = (bf16[128,512]{1,0:T(8,128)(2,1)S(1)}, bf16[128,512]{1,0:T(8,128)(2,1)S(1)}, u32[]{:S(2)}, u32[]{:S(2)}) collective-permute-start(bf16[128,512]{1,0:T(8,128)(2,1)S(1)} %get-tuple-element.70), channel_id=1, source_target_pairs={{0,2},{2,0},{1,3},{3,1},{4,6},{6,4},{5,7},{7,5},{8,10},{10,8},{9,1... | collective-permute-start | bytes 393224 | tf_op jit(solution)/shard_map/ppermute | solution.py:52
  37.4 20.5 %collective-permute-start.6 = (bf16[128,512]{1,0:T(8,128)(2,1)S(1)}, bf16[128,512]{1,0:T(8,128)(2,1)S(1)}, u32[]{:S(2)}, u32[]{:S(2)}) collective-permute-start(bf16[128,512]{1,0:T(8,128)(2,1)S(1)} %get-tuple-element.71), channel_id=1, source_target_pairs={{0,4},{4,0},{1,5},{5,1},{2,6},{6,2},{3,7},{7,3},{8,12},{12,8},{9,1... | collective-permute-start | bytes 393224 | tf_op jit(solution)/shard_map/ppermute | solution.py:52
  39.0 19.0 %collective-permute-start.7 = (bf16[128,512]{1,0:T(8,128)(2,1)S(1)}, bf16[128,512]{1,0:T(8,128)(2,1)S(1)}, u32[]{:S(2)}, u32[]{:S(2)}) collective-permute-start(bf16[128,512]{1,0:T(8,128)(2,1)S(1)} %get-tuple-element.72), channel_id=1, source_target_pairs={{0,8},{8,0},{1,9},{9,1},{2,10},{10,2},{3,11},{11,3},{4,12},{12,4},... | collective-permute-start | bytes 393224 | tf_op jit(solution)/shard_map/ppermute | solution.py:52
  40.5 9.1 %collective-permute-start.19 = (bf16[32,512]{1,0:T(8,128)(2,1)S(1)}, bf16[32,512]{1,0:T(8,128)(2,1)S(1)}, u32[]{:S(2)}, u32[]{:S(2)}) collective-permute-start(bf16[32,512]{1,0:T(8,128)(2,1)S(1)} %get-tuple-element.99), channel_id=1, source_target_pairs={{0,8},{8,0},{1,9},{9,1},{2,10},{10,2},{3,11},{11,3},{4,12},{12,4},... | collective-permute-start | bytes 98312 | tf_op jit(solution)/shard_map/ppermute | solution.py:52
  49.7 4.8 %collective-permute-start.13 = (bf16[32,512]{1,0:T(8,128)(2,1)S(1)}, bf16[32,512]{1,0:T(8,128)(2,1)S(1)}, u32[]{:S(2)}, u32[]{:S(2)}) collective-permute-start(bf16[32,512]{1,0:T(8,128)(2,1)S(1)} %get-tuple-element.86), channel_id=1, source_target_pairs={{0,8},{8,0},{1,9},{9,1},{2,10},{10,2},{3,11},{11,3},{4,12},{12,4},... | collective-permute-start | bytes 98312 | tf_op jit(solution)/shard_map/ppermute | solution.py:52
  54.5 5.1 %collective-permute-start.21 = (bf16[32,512]{1,0:T(8,128)(2,1)S(1)}, bf16[32,512]{1,0:T(8,128)(2,1)S(1)}, u32[]{:S(2)}, u32[]{:S(2)}) collective-permute-start(bf16[32,512]{1,0:T(8,128)(2,1)S(1)} %shard_map.165.refs_1_), channel_id=1, source_target_pairs={{0,16},{16,0},{1,17},{17,1},{2,18},{18,2},{3,19},{19,3},{4,20},{20... | collective-permute-start | bytes 98312 | tf_op jit(solution)/shard_map/ppermute | solution.py:52
  55.9 4.0 %collective-permute-start.20 = (bf16[32,512]{1,0:T(8,128)(2,1)S(1)}, bf16[32,512]{1,0:T(8,128)(2,1)S(1)}, u32[]{:S(2)}, u32[]{:S(2)}) collective-permute-start(bf16[32,512]{1,0:T(8,128)(2,1)S(1)} %shard_map.159.refs_0_), channel_id=1, source_target_pairs={{0,16},{16,0},{1,17},{17,1},{2,18},{18,2},{3,19},{19,3},{4,20},{20... | collective-permute-start | bytes 98312 | tf_op jit(solution)/shard_map/ppermute | solution.py:52
  (3 other events, 14.3 us)
